TPU v7x, 32 devices: a whole 2x2x4 slice. The times are simulated.
32 devices in a mesh: page: 8 (over z, x), head: 4 (over y, core).
Axes of the slice: x: 2, y: 2, z: 4, core: 2. Of those that a mesh axis runs over, the one named last changes fastest.
Arguments:
- tokens: bfloat16 [2, 2, 4096, 768], P(None, None, ('page', 'head')), may hold values from -6 to 6
- spatial: bfloat16 [2, 2, 4096, 768], P(None, None, ('page', 'head')), may hold values from -6 to 6
- box_coords: int32 [2, 2, 2, 4096], P(None, None, None, 'page'), may hold values from 0 to 1023
- reading_order: int32 [2, 2, 4096], P(None, None, 'page'), may hold values from 0 to 127
- page_len: int32 [2, 8], P(None, 'page'), may hold values from 256 to 512, as said below
- w_attn: bfloat16 [2, 5, 768, 768], P(None, None, 'page', 'head'), may hold values from -0.21875 to 0.21875
- tables: bfloat16 [2, 3, 12, 128, 128], P(None, None, 'head', 'page'), may hold values from -3 to 3
- w_out: bfloat16 [2, 768, 768], P(None, 'head', 'page'), may hold values from -0.875 to 0.875
- ln_gain: bfloat16 [2, 768], P(None, ('page', 'head')), may hold values from 0.5 to 1.5
- ln_shift: bfloat16 [2, 768], P(None, ('page', 'head')), may hold values from -1.796875 to 1.796875
- w_up: bfloat16 [768, 3072], P(None, ('page', 'head')), may hold values from -0.21875 to 0.21875
- w_down: bfloat16 [3072, 768], P(('page', 'head')), may hold values from -0.109375 to 0.109375
- grad_out: bfloat16 [2, 4096, 768], P(None, ('page', 'head')), may hold values from -6 to 6
Outputs:
- out: bfloat16 [2, 4096, 768], P(None, ('page', 'head'))
- grad_tokens: bfloat16 [2, 2, 4096, 768], P(None, None, ('page', 'head'))
- grad_w_attn: float32 [2, 5, 768, 768], P(None, None, 'page', 'head')
- grad_tables: float32 [2, 3, 12, 128, 128], P(None, None, 'head', 'page')
- grad_w_out: float32 [2, 768, 768], P(None, 'head', 'page')
- grad_ln_gain: float32 [2, 768], P(None, ('page', 'head'))
- grad_ln_shift: float32 [2, 768], P(None, ('page', 'head'))
- grad_w_up: float32 [768, 3072], P(None, ('page', 'head'))
- grad_w_down: float32 [3072, 768], P(('page', 'head'))
Inputs may be any that keep to these rules, and one draw needn't show every extreme that they name: `page_len`: each entry is 512 (a slot with one page) or 512 / 2 (a slot with two pages); both values occur in every draw.
All inputs are finite; a program needn't handle non-finite values.
Results may differ from a plain program's by a relative error of at most 0.02.
Values may be sent and summed in bfloat16 or wider, within the bound.
No kernel may reach another device: no remote copies, remote signals or barrier semaphores. Data moves between devices by JAX's collectives and lax.ppermute only.
A program may use at most 192 MiB of HBM per device.

v0:
```python
import functools

import jax
import jax.numpy as jnp
from jax import lax
from jax.experimental import pallas as pl
from jax.experimental.pallas import tpu as pltpu
from jax.sharding import PartitionSpec as P

COORD = 1024
EPS = 1e-05
GROUPS = 8
SCALE = 7e8
EXTRA = 16
f32 = jnp.float32
bf16 = jnp.bfloat16
AB = ((1,), (0,))
ABT = ((1,), (1,))
ATB = ((0,), (0,))
SMEM = pl.BlockSpec(memory_space=pltpu.SMEM)
VM = pl.BlockSpec(memory_space=pltpu.VMEM)
HBM = pl.BlockSpec(memory_space=pltpu.HBM)
PARAMS = pltpu.CompilerParams(vmem_limit_bytes=14 * 1024 * 1024)
FAR_X = (4, 2, 1)
FAR_Z = (4, 1, 2)
X_FIRST = (1, 4, 2)


def cost(microseconds):
    return pl.CostEstimate(
        flops=int(microseconds * SCALE), bytes_accessed=int(microseconds * 3e5), transcendentals=0
    )


def struct(shape, kind):
    return pltpu.VMEM(tuple(shape), kind)


def pin(*values):
    return [pltpu.with_memory_space_constraint(value, pltpu.VMEM) for value in values]


def dot(left, right, dims):
    return lax.dot_general(left, right, (dims, ((), ())), preferred_element_type=f32)


def swap(value, axis, mask):
    count = lax.axis_size(axis)
    return lax.ppermute(value, axis, [(place, place ^ mask) for place in range(count)])


def after(value, *earlier):
    return lax.optimization_barrier((value, earlier))[0]


def gather_rows(own):
    side = swap(own, "head", 2)
    return own, side, swap(own, "head", 1), swap(side, "head", 1)


def scatter_rows(keep, send):
    own = keep.shape[0] // 2
    near = swap(send, "head", 1)
    far = swap((keep[own:] + near[own:].astype(f32)).astype(bf16), "head", 2)
    return keep, near, far


def page_bits():
    count = lax.axis_size("page")
    return [1 << bit for bit in reversed(range(count.bit_length() - 1))]


def gather_pages(own):
    full = own
    for depth, mask in enumerate(page_bits()):
        full = jnp.stack([full, swap(full, "page", mask)], axis=depth)
    return full.reshape((lax.axis_size("page"),) + own.shape)


def scatter_pages(blocks):
    masks = page_bits()
    part = blocks.reshape((2,) * len(masks) + blocks.shape[1:])
    for depth in reversed(range(len(masks))):
        keep = lax.index_in_dim(part, 0, depth, keepdims=False)
        send = lax.index_in_dim(part, 1, depth, keepdims=False)
        part = keep.astype(f32) + swap(send.astype(bf16), "page", masks[depth]).astype(f32)
    return part


def by_page(blocks):
    count = blocks.shape[0]
    order = jnp.arange(count, dtype=jnp.int32) ^ lax.axis_index("page")
    return jnp.take(blocks, order, axis=0)


def regroup(full, heads):
    pages, share, columns = full.shape
    if heads == 1:
        return full.reshape(GROUPS, -1, columns)
    parts = full.reshape(GROUPS, pages // GROUPS, heads, share // heads, columns)
    return parts.transpose(0, 2, 1, 3, 4).reshape(GROUPS, -1, columns)


def ungroup(full, pages, heads):
    columns = full.shape[2]
    if heads == 1:
        return full.reshape(pages, -1, columns)
    parts = full.reshape(GROUPS, heads, pages // GROUPS, -1, columns)
    return parts.transpose(0, 2, 1, 3, 4).reshape(pages, -1, columns)


def direct():
    return lax.axis_size("page") == GROUPS


def join_kernel(first_ref, second_ref, out_ref):
    half = first_ref.shape[0]
    out_ref[:half] = first_ref[...]
    out_ref[half:] = second_ref[...]


def join(first, second):
    return pl.pallas_call(
        join_kernel,
        in_specs=[VM] * 2,
        out_shape=struct((2 * first.shape[0],) + first.shape[1:], first.dtype),
        compiler_params=PARAMS,
        cost_estimate=cost(0.4),
        name="join",
    )(*pin(first, second))


def fold_kernel(first_ref, second_ref, keep_ref, send_ref):
    half = keep_ref.shape[0]
    keep_ref[...] = first_ref[:half].astype(f32) + second_ref[:half].astype(f32)
    send_ref[...] = (first_ref[half:].astype(f32) + second_ref[half:].astype(f32)).astype(bf16)


def fold(first, second):
    half = (first.shape[0] // 2,) + first.shape[1:]
    return pl.pallas_call(
        fold_kernel,
        in_specs=[VM] * 2,
        out_shape=(struct(half, f32), struct(half, bf16)),
        compiler_params=PARAMS,
        cost_estimate=cost(0.6),
        name="fold",
    )(*pin(first, second))


class Gather:
    def __init__(self, share, masks):
        self.part, self.masks = share[None], list(masks)

    def start(self, *earlier):
        self.part = after(self.part, *earlier)
        self.got = swap(self.part, "page", self.masks.pop(0))

    def step(self, *earlier):
        self.part = join(self.part, after(self.got, *earlier))
        self.start(*earlier)

    def result(self):
        return self.part, self.got


def generic_gather(share, columns=None, heads=1):
    full = by_page(gather_pages(share))
    if heads == 1:
        full = regroup(full, 1)
    else:
        full = jnp.concatenate([regroup(full[..., :columns], 1), regroup(full[..., columns:], heads)], axis=2)
    return full[: GROUPS // 2], full[GROUPS // 2 :]


class Scatter:
    def __init__(self, keep, send, masks):
        self.keep, self.send, self.masks = keep, send, list(masks)

    def start(self, *earlier):
        self.send = after(self.send, *earlier)
        self.got = swap(self.send, "page", self.masks.pop())

    def step(self, *earlier):
        self.keep, self.send = fold(self.keep, after(self.got, *earlier))
        self.start(*earlier)

    def result(self, *earlier):
        return self.keep[0] + after(self.got, *earlier)[0].astype(f32)


def generic_scatter(keep, send, columns=None, heads=1):
    pages = lax.axis_size("page")
    full = jnp.concatenate([keep.astype(bf16), send])
    if heads == 1:
        full = ungroup(full, pages, 1)
    else:
        full = jnp.concatenate(
            [ungroup(full[..., :columns], pages, 1), ungroup(full[..., columns:], pages, heads)], axis=2
        )
    return scatter_pages(by_page(full))


def places(masks):
    if not direct():
        masks = (1, 2, 4)
    return [
        sum(mask for bit, mask in enumerate(masks) if (place >> bit) & 1) for place in range(GROUPS)
    ]


def load_chunk(page, refs, masks, target, start=0):
    share = target.shape[0] // GROUPS
    stop = start + refs[0].shape[2]
    for place, number in enumerate(places(masks)):
        row = pl.multiple_of(jnp.bitwise_xor(page, number) * share, share)
        target[pl.ds(row, share), start:stop] = refs[place // (GROUPS // 2)][place % (GROUPS // 2), :share]


def load_rows(refs, target, *pick):
    count = refs[0].shape[-2]
    for place, ref in enumerate(refs):
        target[place * count : (place + 1) * count] = ref[pick] if pick else ref[...]


def load_extra(page, refs, masks, target):
    share = refs[0].shape[1] - EXTRA
    for place, number in enumerate(places(masks)):
        target[jnp.bitwise_xor(page, number)] = refs[place // (GROUPS // 2)][place % (GROUPS // 2), share:]


def load_split(page, refs, target):
    if len(refs) == 2:
        load_chunk(page, refs, FAR_X, target)
    else:
        load_chunk(page, refs[:2], FAR_Z, target)
        load_chunk(page, refs[2:], FAR_X, target, refs[0].shape[2])


def turned(ids_ref):
    ids = ids_ref[...].astype(f32)
    return jnp.concatenate([ids, ids]).T


def hot_columns(ids, which, buckets):
    lane = lax.broadcasted_iota(jnp.int32, (ids.shape[0], buckets), 1).astype(f32)
    return jnp.where(ids[:, which : which + 1] == lane, 1.0, 0.0).astype(bf16)


def table_rows(head, heads, small):
    return [pl.multiple_of((side * heads + head) * small, small) for side in range(2)]


def attend_kernel(batch, heads, last, page_ref, *refs):
    parts = 2 if last else 4
    rows_refs, w_refs, refs = refs[:4], refs[4 : 4 + parts], refs[4 + parts :]
    if last:
        o_refs, other_ref, refs = refs[:2], refs[2], refs[3:]
    idr_ref, saved, head_ref, refs = refs[0], refs[1:6], refs[6], refs[7:]
    if last:
        saved += refs[:1]
        keep_ref, send_ref, norms_ref, refs = refs[1], refs[2], refs[3], refs[4:]
        wo_ref, extra_ref, refs = refs[0], refs[1], refs[2:]
    left_ref, right_ref, value_ref, prob_ref, w_ref, x_ref, s_ref, hot_ref, head_part_ref, sems = refs
    page = page_ref[0]
    load_rows(rows_refs, x_ref, 0, batch)
    load_rows(rows_refs, s_ref, 1, batch)
    load_split(page, w_refs, w_ref)
    copies = [pltpu.make_async_copy(w_ref, saved[4], sems.at[0])]
    if last:
        load_chunk(page, o_refs, X_FIRST, wo_ref)
        load_extra(page, o_refs, X_FIRST, extra_ref)
        copies.append(pltpu.make_async_copy(wo_ref, saved[5], sems.at[1]))
    rows = x_ref.shape[0]
    width = w_ref.shape[1] // 6
    share = w_ref.shape[0] // GROUPS
    size = width // heads
    buckets = 2 * width // 3
    small, wide = buckets // GROUPS, buckets // 2
    columns = turned(idr_ref)
    for which in range(3):
        hot_ref[:, which * buckets : (which + 1) * buckets] = hot_columns(columns, which, buckets)
    same = columns[:, 3:4] == idr_ref[3:4, :].astype(f32)
    first = dot(x_ref[...], w_ref[:, : 2 * width], AB).astype(bf16)
    second = dot(s_ref[...], w_ref[:, 2 * width : 4 * width], AB).astype(bf16)
    third = dot(x_ref[...], w_ref[:, 4 * width : 5 * width], AB).astype(bf16)
    for head in range(heads):
        low, high = slice(head * size, (head + 1) * size), slice(width + head * size, width + (head + 1) * size)
        left_ref[head] = jnp.concatenate([first[:, low], second[:, low]], axis=1) * bf16(0.125)
        right_ref[head] = jnp.concatenate([first[:, high], second[:, high]], axis=1)
        value_ref[head] = third[:, low]
    for at, ref in enumerate((left_ref, right_ref, value_ref)):
        copies.append(pltpu.make_async_copy(ref, saved[at], sems.at[2 + at]))
    for copy in copies:
        copy.start()

    def save_prob(head):
        return pltpu.make_async_copy(prob_ref.at[head], saved[3].at[head], sems.at[5 + head])

    def body(head, carry):
        sides = []
        for start in table_rows(head, heads, small):
            pieces = [w_ref[pl.ds(group * share + start, small), 5 * width :] for group in range(GROUPS)]
            sides.append(jnp.concatenate(pieces))
        parts = [left_ref[head]]
        for which in range(3):
            table = jnp.concatenate([side[:, which * wide : (which + 1) * wide] for side in sides], axis=1)
            parts.append(dot(hot_ref[:, which * buckets : (which + 1) * buckets], table, AB).astype(bf16))
        left = jnp.concatenate(parts, axis=1)
        right = jnp.concatenate([right_ref[head], hot_ref[...]], axis=1)
        score = jnp.where(same, dot(left, right, ABT), -1e30)
        weight = jnp.exp(score - jnp.max(score, axis=1, keepdims=True))
        prob = (weight * (1.0 / jnp.sum(weight, axis=1, keepdims=True))).astype(bf16)
        prob_ref[head] = prob
        save_prob(head).start()
        head_part_ref[head] = dot(prob, value_ref[head], AB).astype(bf16)
        return carry

    lax.fori_loop(0, heads, body, 0)
    head_ref[...] = jnp.concatenate([head_part_ref[head] for head in range(heads)], axis=1)
    if last:
        part = dot(other_ref[...], wo_ref[:, :width], ABT) + dot(head_ref[...], wo_ref[:, width:], ABT)
        keep_ref[...] = part[: rows // 2]
        send_ref[...] = part[rows // 2 :].astype(bf16)
        inner = norms_ref.shape[1] // GROUPS
        for group in range(GROUPS):
            for which in range(norms_ref.shape[0]):
                norms_ref[which : which + 1, group * inner : (group + 1) * inner] = extra_ref[
                    group, 0:1, which * inner : (which + 1) * inner
                ].astype(f32)
    for copy in copies:
        copy.wait()
    for head in range(heads):
        save_prob(head).wait()


def attend(batch, heads, page, row_parts, chunk, ids_row, final=None):
    rows = ids_row.shape[1]
    features = row_parts[0].shape[-1]
    columns = sum(ref.shape[2] for ref in chunk[::2])
    width = columns // 6
    size = width // heads
    saved = [
        ((heads, rows, 2 * size), bf16),
        ((heads, rows, 2 * size), bf16),
        ((heads, rows, size), bf16),
        ((heads, rows, rows), bf16),
        ((features, columns), bf16),
    ]
    scratch = [pltpu.VMEM(shape, kind) for shape, kind in saved]
    more = ()
    extra_outs, first_scratch = (), []
    if final is not None:
        pair_o, other = final
        more = (*pair_o, other)
        extra_outs = (
            pltpu.HBM((features, 2 * width), bf16),
            struct((rows // 2, features), f32), struct((rows // 2, features), bf16), struct((4, features), f32),
        )
        first_scratch = [pltpu.VMEM((features, 2 * width), bf16), pltpu.VMEM((GROUPS, EXTRA, 2 * width), bf16)]
    outs = tuple(pltpu.HBM(shape, kind) for shape, kind in saved) + (struct((rows, width), bf16),)
    return pl.pallas_call(
        functools.partial(attend_kernel, batch, heads, final is not None),
        in_specs=[SMEM] + [VM] * (4 + len(chunk) + len(more) + 1),
        out_specs=[HBM] * 5 + [VM] + ([] if final is None else [HBM, VM, VM, VM]),
        out_shape=outs + extra_outs,
        scratch_shapes=first_scratch + scratch + [
            pltpu.VMEM((rows, features), bf16),
            pltpu.VMEM((rows, features), bf16),
            pltpu.VMEM((rows, 2 * width), bf16),
            pltpu.VMEM((heads, rows, size), bf16),
            pltpu.SemaphoreType.DMA((5 + heads,)),
        ],
        compiler_params=PARAMS,
        cost_estimate=cost(6.3),
        name="attend",
    )(page, *pin(*row_parts, *chunk, *more, ids_row))


def attend_back_kernel(heads, half, page_ref, *refs):
    da_refs, saved, idr_ref, refs = refs[:4], refs[4:10], refs[10], refs[11:]
    if half == 0:
        other_ref, dproj_ref, dtable_ref, keep_ref, send_ref, refs = refs[0], refs[1], refs[2], refs[3], refs[4], refs[5:]
    else:
        dproj_ref, dtable_ref, part_ref, refs = refs[0], refs[1], refs[2], refs[3:]
    left_ref, right_ref, value_ref, prob_ref, w_ref, wo_ref, refs = refs[0], refs[1], refs[2], refs[3], refs[4], refs[5], refs[6:]
    da_ref, hot_ref, grad_ref, dleft_ref, dright_ref, dvalue_ref, sems = refs
    early = [
        pltpu.make_async_copy(source, target, sems.at[at])
        for at, (source, target) in enumerate(
            ((saved[5], wo_ref), (saved[2], value_ref), (saved[1], right_ref), (saved[0], left_ref))
        )
    ]
    late = pltpu.make_async_copy(saved[4], w_ref, sems.at[4])

    def fetch_prob(head):
        return pltpu.make_async_copy(saved[3].at[head], prob_ref.at[head], sems.at[5 + head])

    early[0].start()
    early[1].start()
    fetch_prob(0).start()
    early[2].start()
    early[3].start()
    for head in range(1, heads):
        fetch_prob(head).start()
    late.start()
    load_rows(da_refs, da_ref)
    rows = da_ref.shape[0]
    width = w_ref.shape[1] // 6
    size = width // heads
    buckets = 2 * width // 3
    small, wide = buckets // GROUPS, buckets // 2
    columns = turned(idr_ref)
    for which in range(3):
        hot_ref[:, which * buckets : (which + 1) * buckets] = hot_columns(columns, which, buckets)
    bucket = lax.broadcasted_iota(jnp.int32, (buckets, rows), 0)
    early[0].wait()
    grad_heads = dot(da_ref[...], wo_ref[:, half * width : (half + 1) * width], AB).astype(bf16)
    for head in range(heads):
        grad_ref[head] = grad_heads[:, head * size : (head + 1) * size]
    for copy in early[1:]:
        copy.wait()

    def body(head, carry):
        fetch_prob(head).wait()
        prob = prob_ref[head]
        grad_out = grad_ref[head]
        grad_prob = dot(grad_out, value_ref[head], ABT)
        weighted = prob.astype(f32) * grad_prob
        row_dot = jnp.sum(weighted, axis=1, keepdims=True)
        grad_score = (weighted - prob.astype(f32) * row_dot).astype(bf16)
        dvalue_ref[head] = dot(prob, grad_out, ATB).astype(bf16)
        right = jnp.concatenate([right_ref[head], hot_ref[...]], axis=1)
        spread = dot(grad_score, right, AB)
        dleft_ref[head] = (spread[:, : 2 * size] * 0.125).astype(bf16)
        dright_ref[head] = dot(grad_score, left_ref[head], ATB).astype(bf16)
        pieces = []
        for which in range(3):
            start = 2 * size + which * buckets
            hot_t = jnp.where(idr_ref[which : which + 1, :] == bucket, 1.0, 0.0).astype(bf16)
            pieces.append(dot(hot_t, spread[:, start : start + buckets].astype(bf16), AB))
        for side, start in enumerate(table_rows(head, heads, small)):
            block = jnp.concatenate([piece[:, side * wide : (side + 1) * wide] for piece in pieces], axis=1)
            for group in range(GROUPS):
                dtable_ref[group, pl.ds(start, small), :] = block[group * small : (group + 1) * small]
        return carry

    lax.fori_loop(0, heads, body, 0)
    every = range(heads)
    dproj_ref[:, :width] = jnp.concatenate([dleft_ref[head][:, :size] for head in every], axis=1)
    dproj_ref[:, width : 2 * width] = jnp.concatenate([dright_ref[head][:, :size] for head in every], axis=1)
    dproj_ref[:, 2 * width : 3 * width] = jnp.concatenate([dleft_ref[head][:, size:] for head in every], axis=1)
    dproj_ref[:, 3 * width : 4 * width] = jnp.concatenate([dright_ref[head][:, size:] for head in every], axis=1)
    dproj_ref[:, 4 * width :] = jnp.concatenate([dvalue_ref[head] for head in every], axis=1)
    late.wait()
    part = dot(dproj_ref[:, : 2 * width], w_ref[:, : 2 * width], ABT)
    part = part + dot(dproj_ref[:, 4 * width :], w_ref[:, 4 * width : 5 * width], ABT)
    if half == 0:
        part = part + other_ref[...]
        keep_ref[...] = part[: rows // 2]
        send_ref[...] = part[rows // 2 :].astype(bf16)
    else:
        part_ref[...] = part


def attend_back(heads, half, page, da_parts, saved, ids_row, other=None):
    rows = ids_row.shape[1]
    features = da_parts[0].shape[-1]
    width = saved[4].shape[1] // 6
    size = width // heads
    outs = (struct((rows, 5 * width), bf16), struct((GROUPS, features // GROUPS, width), f32))
    if half == 0:
        outs += (struct((rows // 2, features), f32), struct((rows // 2, features), bf16))
    else:
        outs += (struct((rows, features), f32),)
    return pl.pallas_call(
        functools.partial(attend_back_kernel, heads, half),
        in_specs=[SMEM] + [VM] * 4 + [HBM] * 6 + [VM] * (2 if half == 0 else 1),
        out_shape=outs,
        scratch_shapes=[pltpu.VMEM(ref.shape, ref.dtype) for ref in saved]
        + [
            pltpu.VMEM((rows, features), bf16),
            pltpu.VMEM((rows, 2 * width), bf16),
            pltpu.VMEM((heads, rows, size), bf16),
            pltpu.VMEM((heads, rows, 2 * size), bf16),
            pltpu.VMEM((heads, rows, 2 * size), bf16),
            pltpu.VMEM((heads, rows, size), bf16),
            pltpu.SemaphoreType.DMA((5 + heads,)),
        ],
        compiler_params=PARAMS,
        cost_estimate=cost(6),
        name="attend_back",
    )(page, *pin(*da_parts), *[pltpu.with_memory_space_constraint(ref, pltpu.HBM) for ref in saved], *pin(ids_row, *([other] if half == 0 else [])))


def put_blocks(page, masks, full_ref, columns, keep_ref, send_ref):
    for place, number in enumerate(places(masks)):
        block = full_ref[jnp.bitwise_xor(page, number), :, columns]
        if place < GROUPS // 2:
            keep_ref[place] = block
        else:
            send_ref[place - GROUPS // 2] = block.astype(bf16)


def attn_weights_kernel(batches, split, page_ref, *refs):
    rows_refs, dproj_refs, dtable_refs = refs[:4], refs[4 : 4 + batches], refs[4 + batches : 4 + 2 * batches]
    out_refs, (x_ref, d_ref, full_ref) = refs[4 + 2 * batches : -3], refs[-3:]
    page = page_ref[0]
    rows = x_ref.shape[1] // batches
    for batch in range(batches):
        at = pl.ds(batch * rows, rows)
        for which in range(2):
            load_rows(rows_refs, x_ref.at[which, at], which, batch)
        d_ref[at] = dproj_refs[batch][...]
    width = d_ref.shape[1] // 5

    def blocks(value):
        return value.reshape(GROUPS, value.shape[0] // GROUPS, value.shape[1])

    x_t = x_ref[0].T
    full_ref[:, :, : 2 * width] = blocks(dot(x_t, d_ref[:, : 2 * width], AB))
    full_ref[:, :, 2 * width : 4 * width] = blocks(dot(x_ref[1].T, d_ref[:, 2 * width : 4 * width], AB))
    full_ref[:, :, 4 * width : 5 * width] = blocks(dot(x_t, d_ref[:, 4 * width :], AB))
    total = dtable_refs[0][...]
    for ref in dtable_refs[1:]:
        total = total + ref[...]
    full_ref[:, :, 5 * width :] = total
    if split:
        put_blocks(page, FAR_Z, full_ref, slice(0, split), *out_refs[:2])
    put_blocks(page, FAR_X, full_ref, slice(split, 6 * width), *out_refs[-2:])


def attn_weights(page, row_parts, dprojs, dtables, split):
    batches = len(dprojs)
    rows, columns = dprojs[0].shape
    columns = 6 * (columns // 5)
    features = row_parts[0].shape[-1]
    inner = features // GROUPS
    outs = ()
    for count in (split, columns - split) if split else (columns,):
        outs += (struct((GROUPS // 2, inner, count), f32), struct((GROUPS // 2, inner, count), bf16))
    return pl.pallas_call(
        functools.partial(attn_weights_kernel, batches, split),
        in_specs=[SMEM] + [VM] * (4 + batches) + [VM] * batches,
        out_shape=outs,
        scratch_shapes=[
            pltpu.VMEM((2, batches * rows, features), bf16),
            pltpu.VMEM((batches * rows, dprojs[0].shape[1]), bf16),
            pltpu.VMEM((GROUPS, inner, columns), f32),
        ],
        compiler_params=PARAMS,
        cost_estimate=cost(4.8),
        name="attn_weights",
    )(page, *pin(*row_parts, *dprojs, *dtables))


def out_weights_kernel(batches, page_ref, *refs):
    da_refs, head_refs, refs = refs[: 4 * batches], refs[4 * batches : 6 * batches], refs[6 * batches :]
    sums_refs, refs = refs[: 2 * batches], refs[2 * batches :]
    keep_ref, send_ref, da_ref, head_ref, full_ref = refs
    page = page_ref[0]
    rows = da_ref.shape[0] // batches
    width = head_ref.shape[2]
    for batch in range(batches):
        at = pl.ds(batch * rows, rows)
        load_rows(da_refs[4 * batch : 4 * batch + 4], da_ref.at[at])
        for half in range(2):
            head_ref[half, at] = head_refs[2 * batch + half][...]
    share = da_ref.shape[1] // GROUPS
    full_ref[:, share:, :] = jnp.zeros((GROUPS, EXTRA, 2 * width), f32)
    for layer in range(2):
        total = sums_refs[layer][...]
        for batch in range(1, batches):
            total = total + sums_refs[2 * batch + layer][...]
        for which in range(2):
            for group in range(GROUPS):
                start = (2 * which + layer) * share
                full_ref[group, share : share + 1, start : start + share] = total[
                    which : which + 1, group * share : (group + 1) * share
                ]
    da_t = da_ref[...].T
    for half in range(2):
        full_ref[:, :share, half * width : (half + 1) * width] = dot(da_t, head_ref[half], AB).reshape(
            GROUPS, share, width
        )
    put_blocks(page, FAR_X, full_ref, slice(0, 2 * width), keep_ref, send_ref)


def out_weights(page, da_parts, head_rows, sums):
    batches = len(da_parts)
    rows, width = head_rows[0].shape
    features = da_parts[0][0].shape[-1]
    chunk = (GROUPS // 2, features // GROUPS + EXTRA, 2 * width)
    return pl.pallas_call(
        functools.partial(out_weights_kernel, batches),
        in_specs=[SMEM] + [VM] * (6 * batches) + [VM] * (2 * batches),
        out_shape=(struct(chunk, f32), struct(chunk, bf16)),
        scratch_shapes=[
            pltpu.VMEM((batches * rows, features), bf16),
            pltpu.VMEM((2, batches * rows, width), bf16),
            pltpu.VMEM((GROUPS,) + chunk[1:], f32),
        ],
        compiler_params=PARAMS,
        cost_estimate=cost(2.7),
        name="out_weights",
    )(page, *pin(*[ref for parts in da_parts for ref in parts], *head_rows, *sums))


def hidden_weights(refs):
    return jnp.concatenate([ref[...].reshape(-1, ref.shape[2]) for ref in refs])


def forward_kernel(own_ref, side_ref, *refs):
    f_refs, (act_ref, slope_ref, keep_ref, send_ref) = refs[:4], refs[4:]
    own, features = own_ref.shape
    rows = jnp.concatenate([own_ref[...], side_ref[...]])
    weight = hidden_weights(f_refs)
    pre = dot(rows, weight[:, :features], ABT)
    normal = 0.5 + 0.5 * lax.erf(pre * 0.7071067811865476)
    act = (pre * normal).astype(bf16)
    act_ref[...] = act
    slope_ref[...] = (normal + pre * jnp.exp(-0.5 * pre * pre) * 0.3989422804014327).astype(bf16)
    part = dot(act, weight[:, features:], AB)
    keep_ref[...] = part[:own]
    send_ref[...] = part[own:].astype(bf16)


def backward_kernel(own_ref, side_ref, *refs):
    f_refs, (act_ref, slope_ref, pre_ref, keep_ref, send_ref) = refs[:4], refs[4:]
    own, features = own_ref.shape
    rows = jnp.concatenate([own_ref[...], side_ref[...]])
    weight = hidden_weights(f_refs)
    grad_act = dot(rows, weight[:, features:], ABT)
    grad_pre = (grad_act * slope_ref[...].astype(f32)).astype(bf16)
    pre_ref[...] = grad_pre
    part = dot(grad_pre, weight[:, :features], AB)
    keep_ref[...] = part[:own]
    send_ref[...] = part[own:].astype(bf16)


def ff_call(kernel, name, parts, weights, saved):
    own, features = parts[0].shape
    hidden = sum(ref.shape[0] * ref.shape[1] for ref in weights)
    outs = (struct((2 * own, hidden), bf16),) * (1 if saved else 2)
    return pl.pallas_call(
        kernel,
        in_specs=[VM] * (6 + len(saved)),
        out_shape=outs + (struct((own, features), f32), struct((own, features), bf16)),
        compiler_params=PARAMS,
        cost_estimate=cost(1.8),
        name=name,
    )(*pin(*parts, *weights, *saved))


def ff_weights_kernel(batches, *refs):
    h_refs, g_refs = refs[: 2 * batches], refs[2 * batches : 4 * batches]
    pre_refs, act_refs = refs[4 * batches : 5 * batches], refs[5 * batches : 6 * batches]
    ours_ref, theirs_ref = refs[6 * batches :]
    features = ours_ref.shape[2]
    features = features // 2
    half = GROUPS * ours_ref.shape[1]
    shape = ours_ref.shape[:2] + (features,)
    for left_refs, right_refs, at in ((pre_refs, h_refs, 0), (act_refs, g_refs, features)):
        left = jnp.concatenate([ref[...] for ref in left_refs])
        right = jnp.concatenate([ref[...] for ref in right_refs])
        total = dot(left, right, ATB).astype(bf16)
        ours_ref[:, :, at : at + features] = total[:half].reshape(shape)
        theirs_ref[:, :, at : at + features] = total[half:].reshape(shape)


def ff_weights(h_parts, g_parts, grad_pres, acts):
    batches = len(acts)
    hidden = acts[0].shape[1]
    features = h_parts[0][0].shape[1]
    chunk = (GROUPS, hidden // (2 * GROUPS), 2 * features)
    return pl.pallas_call(
        functools.partial(ff_weights_kernel, batches),
        in_specs=[VM] * (6 * batches),
        out_shape=(struct(chunk, bf16), struct(chunk, bf16)),
        compiler_params=PARAMS,
        cost_estimate=cost(4.2),
        name="ff_weights",
    )(*pin(*[ref for parts in h_parts + g_parts for ref in parts], *grad_pres, *acts))


def normalize(value):
    centred = value - jnp.mean(value, axis=1, keepdims=True)
    scale = lax.rsqrt(jnp.mean(centred * centred, axis=1, keepdims=True) + EPS)
    return centred * scale, scale


def normalize_back(grad, normal, scale, gain):
    inner = grad * gain
    inner = inner - jnp.mean(inner, axis=1, keepdims=True) - normal * jnp.mean(inner * normal, axis=1, keepdims=True)
    return inner * scale


def norm_sums(grad, normal):
    gain = jnp.sum(grad * normal, axis=0, keepdims=True)
    shift = jnp.sum(grad, axis=0, keepdims=True)
    return jnp.concatenate([gain, shift], axis=0)


def norm_one_kernel(keep_ref, near_ref, far_ref, first_ref, second_ref, norms_ref, normal_ref, scale_ref, low_ref):
    value = first_ref[...].astype(f32) + second_ref[...].astype(f32)
    value = value + (keep_ref[...] + near_ref[...].astype(f32) + far_ref[...].astype(f32))
    normal, scale = normalize(value)
    normal_ref[...] = normal
    scale_ref[...] = scale
    low_ref[...] = (normal * norms_ref[0:1] + norms_ref[2:3]).astype(bf16)


def norm_two_kernel(keep_ref, far_ref, normal_ref, grad_ref, norms_ref, out_ref, dc_ref, dz_ref, sums_ref):
    value = normal_ref[...] * norms_ref[0:1] + norms_ref[2:3]
    value = value + (keep_ref[...] + far_ref[...].astype(f32))
    normal, scale = normalize(value)
    out_ref[...] = (normal * norms_ref[1:2] + norms_ref[3:4]).astype(bf16)
    grad = grad_ref[...].astype(f32)
    dc = normalize_back(grad, normal, scale, norms_ref[1:2])
    dc_ref[...] = dc
    dz_ref[...] = dc.astype(bf16)
    sums_ref[...] = norm_sums(grad, normal)


def norm_back_kernel(keep_ref, far_ref, dc_ref, normal_ref, scale_ref, norms_ref, da_ref, low_ref, sums_ref):
    grad = dc_ref[...] + (keep_ref[...] + far_ref[...].astype(f32))
    normal = normal_ref[...]
    da = normalize_back(grad, normal, scale_ref[...], norms_ref[0:1])
    da_ref[...] = da
    low_ref[...] = da.astype(bf16)
    sums_ref[...] = norm_sums(grad, normal)


def norm_call(kernel, name, outs, *args):
    return pl.pallas_call(kernel, in_specs=[VM] * len(args), out_shape=outs, compiler_params=PARAMS, cost_estimate=cost(0.6), name=name)(*pin(*args))


def local(
    tokens,
    spatial,
    box_coords,
    reading_order,
    page_len,
    w_attn,
    tables,
    w_out,
    ln_gain,
    ln_shift,
    w_up,
    w_down,
    grad_out,
):
    batches, own, features = tokens.shape[1:]
    rows = box_coords.shape[3]
    buckets = tables.shape[4]
    own_heads = tables.shape[2]
    heads = 2 * own_heads
    half = w_attn.shape[3]
    width = 2 * half
    share = w_attn.shape[2]
    step = tables.shape[3]
    coarse = COORD // buckets
    head_index = lax.axis_index("head")
    modality = head_index // 2
    pages = lax.axis_size("page")
    page_index = lax.axis_index("page")
    page = (page_index if direct() else page_index * 0).astype(jnp.int32).reshape(1)

    def mine(value):
        return lax.dynamic_index_in_dim(value, modality, 0, keepdims=False)

    def other(value):
        return lax.dynamic_index_in_dim(value, 1 - modality, 0, keepdims=False)

    def split_table(value):
        pieces = value.reshape(3, own_heads, step, 2, buckets // 2).transpose(3, 1, 2, 0, 4)
        return pieces.reshape(share, half)

    split = 5 * features // 6
    turns = jnp.array([0, 2, 1, 3], jnp.int32)
    blocks = turns ^ head_index
    slots = jnp.take(turns, jnp.arange(4, dtype=jnp.int32) ^ head_index)
    sequence = (0, 1, 3, 4, 2)
    attn_own = mine(w_attn)
    chunk_a = jnp.concatenate([attn_own[which] for which in sequence], axis=1)
    one_a = Gather(chunk_a[:, :split], FAR_Z)
    if direct():
        one_a.start()
    first = one_a.part
    attn_send = other(after(w_attn, first))
    attn_got = swap(attn_send, "head", 2)
    table_own = split_table(mine(after(tables, attn_send)))
    two_a = Gather(jnp.concatenate([chunk_a[:, split:], table_own], axis=1), FAR_X)
    if direct():
        two_a.start()
    table_got = swap(other(after(tables, two_a.part)), "head", 2)
    out_got = swap(other(after(w_out, two_a.part)), "head", 2)
    norms_own = after(jnp.stack([ln_gain, ln_shift]), two_a.part)
    norms_four = gather_rows(norms_own)
    if direct():
        one_a.step(two_a.part)
        out_got, norms_four = after((out_got, norms_four), one_a.part)
    else:
        chunk_a = jnp.concatenate([chunk_a, table_own], axis=1)
    norms_head = jnp.take(jnp.stack(norms_four), slots, axis=0)
    chunk_o = jnp.concatenate([mine(w_out), out_got]).T
    gate, rows_gate = (norms_head,), norms_head
    if direct():
        norms_row = norms_head.transpose(1, 2, 0, 3).reshape(1, -1)
        chunk_o = jnp.concatenate([chunk_o, jnp.pad(norms_row, ((0, EXTRA - 1), (0, 0)))])
        part_o = Gather(chunk_o, X_FIRST)
        two_a.step(one_a.part)
        part_o.start(two_a.part)
        gate = (part_o.part,)
    tokens_late, spatial_late = after((tokens, spatial), first)
    rows_own = jnp.stack([mine(tokens_late), mine(spatial_late)])
    rows_side = swap(after(jnp.stack([other(tokens_late), other(spatial_late)]), *gate), "head", 2)
    rows_near = swap(after(rows_own, *gate), "head", 1)
    attn_got, table_got = after((attn_got, table_got), *gate)
    chunk_b = jnp.concatenate([attn_got[which] for which in sequence] + [split_table(table_got)], axis=1)
    chunk_f = jnp.concatenate([w_up.T, w_down], axis=1)
    part_b = Gather(chunk_b, FAR_X)
    if direct():
        part_f = Gather(chunk_f, FAR_X)
        part_b.start()
        one_a.step(part_b.part)
        two_a.step(one_a.part)
        part_b.step(two_a.part)
        part_o.step(part_b.part)
        rows_gate = part_b.part
        part_f.start(part_b.part, one_a.got, two_a.got)
        half_a = one_a.result() + two_a.result()
    else:
        half_a = generic_gather(chunk_a, 5 * half, 2 * own_heads)
        half_a = tuple(ref[..., :split] for ref in half_a) + tuple(ref[..., split:] for ref in half_a)
        half_b = generic_gather(chunk_b, 5 * half, 2 * own_heads)
        norms_full = by_page(gather_pages(norms_head)).transpose(2, 3, 0, 1, 4).reshape(4, GROUPS, 1, -1)
        norms_full = norms_full.transpose(1, 2, 0, 3).reshape(GROUPS, 1, -1)
        norms_full = jnp.pad(norms_full, ((0, 0), (0, EXTRA - 1), (0, 0)))
        pair_o = generic_gather(chunk_o)
        pair_o = tuple(
            jnp.concatenate([ref, extra], axis=1)
            for ref, extra in zip(pair_o, (norms_full[: GROUPS // 2], norms_full[GROUPS // 2 :]))
        )
        pair_f = generic_gather(chunk_f)
    row_parts = rows_own, rows_side, rows_near, swap(after(rows_side, rows_gate), "head", 1)

    ids = jnp.concatenate(
        [
            mine(reading_order)[None],
            mine(box_coords) // coarse,
            jnp.arange(rows, dtype=jnp.int32)[None, None] // page_len.reshape(1, batches, 1),
        ]
    )
    ids = jnp.take(ids.reshape(4, batches, 4, own), blocks, axis=2).reshape(4, batches, rows)

    state = [dict() for _ in range(batches)]
    gate_b = gate_f = gate_last = page
    if direct():
        gate_b = part_f.part
    for batch, here in enumerate(state):
        here["ids"] = (ids[:, batch],)
        *here["saved_a"], here["head_a"] = attend(
            batch, own_heads, after(page, gate_b), row_parts, half_a, *here["ids"]
        )
        gate_b = here["head_a"]
        if direct() and batch == 0:
            part_b.step(gate_b)
            part_o.step(part_b.part)
            part_f.step(part_o.part)
            gate_b = part_b.part
        elif direct():
            part_f.step(gate_b)
            gate_last = part_f.part
    if direct():
        half_b, pair_o, pair_f = part_b.result(), part_o.result(), part_f.result()
    for batch, here in enumerate(state):
        *here["saved_b"], here["head_b"], here["out_t"], here["keep"], here["send"], norms = attend(
            batch, own_heads, after(page, gate_b, gate_last), row_parts, half_b, *here["ids"],
            final=(pair_o, here["head_a"]),
        )
        gate_b = here["head_b"]
    ff_parts = pair_f + tuple(swap(ref, "head", 1) for ref in pair_f)

    wide = struct((own, features), f32)
    low = struct((own, features), bf16)
    sums = struct((2, features), f32)
    for batch, here in enumerate(state):
        keep, near, far = scatter_rows(here["keep"], here["send"])
        here["normal"], here["scale"], hidden_low = norm_call(
            norm_one_kernel, "norm_one", (wide, struct((own, 1), f32), low),
            keep[:own], near[:own], far, tokens[0, batch], tokens[1, batch], norms,
        )
        here["h"] = hidden_low, swap(hidden_low, "head", 2)
        here["act"], here["slope"], keep, send = ff_call(forward_kernel, "forward", here["h"], ff_parts, ())
        here["out"], here["dc"], dz, here["sums_two"] = norm_call(
            norm_two_kernel, "norm_two", (low, wide, low, sums),
            keep, swap(send, "head", 2), here["normal"], grad_out[batch], norms,
        )
        here["g"] = dz, swap(dz, "head", 2)
        here["grad_pre"], keep, send = ff_call(
            backward_kernel, "backward", here["g"], ff_parts, (here["act"], here["slope"])
        )
        here["da"], da_low, here["sums_one"] = norm_call(
            norm_back_kernel, "norm_back", (wide, low, sums),
            keep, swap(send, "head", 2), here["dc"], here["normal"], here["scale"], norms,
        )
        here["a"] = gather_rows(da_low)

    def every(name):
        return [here[name] for here in state]

    ours, theirs = ff_weights(every("h"), every("g"), every("grad_pre"), every("act"))
    keep_f, send_f = fold(ours, swap(theirs, "head", 1))
    part_f = Scatter(keep_f, send_f, FAR_X)
    if direct():
        part_f.start()

    def saved_of(here, name):
        return [*here[name][:4], state[0][name][4], state[0]["out_t"]]

    def back_b(here, *gate):
        here["dproj_b"], here["dtable_b"], here["part"] = attend_back(
            own_heads, 1, after(page, *gate), here["a"], saved_of(here, "saved_b"), *here["ids"]
        )
        return here["dproj_b"]

    def back_a(here, *gate):
        here["dproj_a"], here["dtable_a"], here["keep"], here["send"] = attend_back(
            own_heads, 0, after(page, *gate), here["a"], saved_of(here, "saved_a"), *here["ids"],
            here["part"],
        )
        here["near"] = swap(here["send"], "head", 1)
        return here["dproj_a"]

    gate = back_b(state[0], part_f.send, *[here["a"][0] for here in state])
    keep_o, send_o = out_weights(
        after(page, gate),
        every("a"),
        [here[name] for here in state for name in ("head_a", "head_b")],
        [here[name] for here in state for name in ("sums_one", "sums_two")],
    )
    part_o = Scatter(keep_o, send_o, FAR_X)
    gate = (send_o,)
    if direct():
        part_o.start(part_f.send)
        part_f.step(part_o.send)
        gate += (part_f.send,)
    for here in state[1:]:
        gate = (back_b(here, *gate),)
    weights_b = attn_weights(after(page, *gate), row_parts, every("dproj_b"), every("dtable_b"), split)
    one_b, two_b = Scatter(*weights_b[:2], FAR_Z), Scatter(*weights_b[2:], FAR_X)
    gate = (weights_b[1],)
    if direct():
        two_b.start(part_f.send)
        one_b.start(two_b.send)
        part_o.step(one_b.send)
        gate = (part_o.send,)
    gate = (back_a(state[0], *gate),)
    if direct():
        part_f.step(part_o.send)
        gate += (part_f.send,)
    for here in state[1:]:
        gate = (back_a(here, *gate),)
    if direct():
        two_b.step(part_f.send)
        gate += (two_b.send,)
    weights_a = attn_weights(after(page, *gate), row_parts, every("dproj_a"), every("dtable_a"), split)
    one_a, two_a = Scatter(*weights_a[:2], FAR_Z), Scatter(*weights_a[2:], FAR_X)
    if direct():
        two_a.start(two_b.send)
        one_a.start(two_a.send)
        one_b.step(one_a.send)
        part_o.step(one_b.send)
        two_b.step(part_o.send)
        two_a.step(two_b.send)
        one_b.step(two_a.send)
        one_a.step(one_b.send)
        two_a.step(one_a.send)
        grad_b = jnp.concatenate([one_b.result(one_a.send), two_b.result(one_a.send)], axis=1)
        one_a.step(two_a.send)
        dff, dout = part_f.result(one_a.send), part_o.result(one_a.send)
        grad_a = jnp.concatenate([one_a.result(), two_a.result()], axis=1)
        dnorms = dout[share].reshape(4, 4, -1).transpose(1, 0, 2)
        dout = dout[:share]
    else:
        inner = features // GROUPS
        dff = generic_scatter(keep_f, send_f)
        dout = generic_scatter(keep_o[:, :inner], send_o[:, :inner])
        flat = jnp.concatenate([keep_o[:, inner], send_o[:, inner].astype(f32)]).reshape(GROUPS, 4, -1)
        flat = flat.transpose(1, 0, 2).reshape(4, pages, 4, -1).transpose(1, 2, 0, 3)
        dnorms = scatter_pages(by_page(flat))
        grads = []
        for weights in (weights_a, weights_b):
            keep = jnp.concatenate(weights[::2], axis=2)
            send = jnp.concatenate(weights[1::2], axis=2)
            grads.append(generic_scatter(keep, send, 5 * half, 2 * own_heads))
        grad_a, grad_b = grads

    dnorms = jnp.take(dnorms, blocks, axis=0)
    pair = dnorms[:2] + swap(dnorms[2:], "head", 1)
    dnorms = (pair[0] + swap(pair[1], "head", 2)).reshape(2, 2, -1)

    def both_modalities(ours, theirs):
        got = swap(theirs.astype(bf16), "head", 2).astype(f32)
        return jnp.where(modality == 0, jnp.stack([ours, got]), jnp.stack([got, ours]))

    token_grads = []
    for here in state:
        total = here["keep"] + after(here["near"], weights_a[1]).astype(f32)
        token_grads.append(both_modalities(total[:own], total[own:]) + here["da"][None])

    got_b = swap(grad_b.astype(bf16), "head", 2).astype(f32)
    chunks = jnp.where(modality == 0, jnp.stack([grad_a, got_b]), jnp.stack([got_b, grad_a]))
    dattn = jnp.stack([chunks[:, :, which * half : (which + 1) * half] for which in (0, 1, 4, 2, 3)], axis=1)
    dtable = chunks[:, :, 5 * half :].reshape(2, 2, own_heads, step, 3, buckets // 2)
    dtable = dtable.transpose(0, 4, 2, 3, 1, 5).reshape(2, 3, own_heads, step, buckets)
    dout = dout.reshape(share, 2, half).transpose(1, 2, 0)
    return (
        jnp.stack([here["out"] for here in state]),
        jnp.stack(token_grads, axis=1).astype(bf16),
        dattn,
        dtable,
        both_modalities(dout[0], dout[1]),
        dnorms[0],
        dnorms[1],
        dff[:, :features].T,
        dff[:, features:],
    )


def solution(mesh):
    return jax.shard_map(
        local,
        mesh=mesh,
        in_specs=(
            P(None, None, ("page", "head"), None),
            P(None, None, ("page", "head"), None),
            P(None, None, None, "page"),
            P(None, None, "page"),
            P(None, "page"),
            P(None, None, "page", "head"),
            P(None, None, "head", "page", None),
            P(None, "head", "page"),
            P(None, ("page", "head")),
            P(None, ("page", "head")),
            P(None, ("page", "head")),
            P(("page", "head"), None),
            P(None, ("page", "head"), None),
        ),
        out_specs=(
            P(None, ("page", "head"), None),
            P(None, None, ("page", "head"), None),
            P(None, None, "page", "head"),
            P(None, None, "head", "page", None),
            P(None, "head", "page"),
            P(None, ("page", "head")),
            P(None, ("page", "head")),
            P(None, ("page", "head")),
            P(("page", "head"), None),
        ),
        check_vma=False,
    )
```

profile of v0, /device:TPU:0, one launch (start us, length us, event | category | flops | bytes accessed | tf_op | source)
XLA Modules:
  0.0 285.2 jit_solution(8095252582408950139)
XLA Ops:
  1.9 4.1 %collective-permute-start.6 = (bf16[1,96,640]{2,1,0:T(8,128)(2,1)S(1)}, bf16[1,96,640]{2,1,0:T(8,128)(2,1)S(1)}, u32[]{:S(2)}, u32[]{:S(2)}) collective-permute-start(bf16[1,96,640]{2,1,0:T(8,128)(2,1)S(1)} %fusion.11.first_ref), channel_id=1, source_target_pairs={{0,16},{4,20},{8,24},{12,28},{16,0},{20,4},{24,8},{28,12},{1,17},{... | collective-permute-start | bytes 368648 | tf_op jit(solution)/shard_map/ppermute | solution.py:49
  8.3 1.9 collective-permute-start.3
  14.7 1.9 collective-permute-start.2
  26.8 2.7 collective-permute-start.8
  34.9 3.2 %collective-permute-done.8.second_ref = bf16[1,96,1152]{2,1,0:T(8,128)(2,1)S(1)} collective-permute-done((bf16[1,96,1152]{2,1,0:T(8,128)(2,1)S(1)}, bf16[1,96,1152]{2,1,0:T(8,128)(2,1)S(1)}, u32[]{:S(2)}, u32[]{:S(2)}) %collective-permute-start.8) | collective-permute-done | bytes 221216 | tf_op jit(solution)/shard_map/ppermute | solution.py:49
  38.2 1.7 collective-permute-done.14.refs_1_
  44.3 3.1 %collective-permute-done.18.second_ref = bf16[1,112,384]{2,1,0:T(8,128)(2,1)S(1)} collective-permute-done((bf16[1,112,384]{2,1,0:T(8,128)(2,1)S(1)}, bf16[1,112,384]{2,1,0:T(8,128)(2,1)S(1)}, u32[]{:S(2)}, u32[]{:S(2)}) %collective-permute-start.18) | collective-permute-done | bytes 86048 | tf_op jit(solution)/shard_map/ppermute | solution.py:49
  47.9 7.6 %collective-permute-done.13.refs_7_ = bf16[4,96,512]{2,1,0:T(8,128)(2,1)} collective-permute-done((bf16[4,96,512]{2,1,0:T(8,128)(2,1)}, bf16[4,96,512]{2,1,0:T(8,128)(2,1)}, u32[]{:S(2)}, u32[]{:S(2)}) %collective-permute-start.13) | collective-permute-done | bytes 393248 | tf_op jit(solution)/shard_map/ppermute | solution.py:49
  55.4 2.6 collective-permute-start.19
  59.4 8.1 %attend.4 = (bf16[3,512,128]{2,1,0:T(8,128)(2,1)}, bf16[3,512,128]{2,1,0:T(8,128)(2,1)}, bf16[3,512,64]{2,1,0:T(8,128)(2,1)}, bf16[3,512,512]{2,1,0:T(8,128)(2,1...) custom-call(s32[1]{0:T(128)} %bitcast.page_ref, bf16[2,2,128,768]{3,2,1,0:T(8,128)(2,1)S(1)} %pad_maximum_fusion.refs_0_, ...), custom_call_target="tpu_custom_call" | custom-call | flops 4409999872 | bytes 1890000 | tf_op jit(solution)/shard_map/attend/pallas_call | solution.py:362
  67.4 2.4 collective-permute-done.11.second_ref
  71.7 6.8 %collective-permute-done.17.second_ref = bf16[1,96,1536]{2,1,0:T(8,128)(2,1)S(1)} collective-permute-done((bf16[1,96,1536]{2,1,0:T(8,128)(2,1)S(1)}, bf16[1,96,1536]{2,1,0:T(8,128)(2,1)S(1)}, u32[]{:S(2)}, u32[]{:S(2)}) %collective-permute-start.17) | collective-permute-done | bytes 294944 | tf_op jit(solution)/shard_map/ppermute | solution.py:49
  78.6 2.0 collective-permute-start.22
  80.6 7.6 %attend.5 = (bf16[3,512,128]{2,1,0:T(8,128)(2,1)}, bf16[3,512,128]{2,1,0:T(8,128)(2,1)}, bf16[3,512,64]{2,1,0:T(8,128)(2,1)}, bf16[3,512,512]{2,1,0:T(8,128)(2,1...) custom-call(s32[1]{0:T(128)} %bitcast.page_ref, bf16[2,2,128,768]{3,2,1,0:T(8,128)(2,1)S(1)} %pad_maximum_fusion.refs_0_, ...), custom_call_target="tpu_custom_call" | custom-call | flops 4409999872 | bytes 1890000 | tf_op jit(solution)/shard_map/attend/pallas_call | solution.py:362
  88.3 6.6 %collective-permute-done.20.second_ref = bf16[2,96,1536]{2,1,0:T(8,128)(2,1)S(1)} collective-permute-done((bf16[2,96,1536]{2,1,0:T(8,128)(2,1)S(1)}, bf16[2,96,1536]{2,1,0:T(8,128)(2,1)S(1)}, u32[]{:S(2)}, u32[]{:S(2)}) %collective-permute-start.20) | collective-permute-done | bytes 589856 | tf_op jit(solution)/shard_map/ppermute | solution.py:49
  96.4 3.5 %collective-permute-done.22.refs_7_ = bf16[4,112,384]{2,1,0:T(8,128)(2,1)S(1)} collective-permute-done((bf16[4,112,384]{2,1,0:T(8,128)(2,1)S(1)}, bf16[4,112,384]{2,1,0:T(8,128)(2,1)S(1)}, u32[]{:S(2)}, u32[]{:S(2)}) %collective-permute-start.22) | collective-permute-done | bytes 344096 | tf_op jit(solution)/shard_map/ppermute | solution.py:49
  99.9 8.1 %attend.6 = (bf16[3,512,128]{2,1,0:T(8,128)(2,1)}, bf16[3,512,128]{2,1,0:T(8,128)(2,1)}, bf16[3,512,64]{2,1,0:T(8,128)(2,1)}, bf16[3,512,512]{2,1,0:T(8,128)(2,1...) custom-call(s32[1]{0:T(128)} %bitcast.page_ref, ...), custom_call_target="tpu_custom_call" | custom-call | flops 4409999872 | bytes 1890000 | tf_op jit(solution)/shard_map/attend/pallas_call | solution.py:362
  108.0 7.7 %attend.7 = (bf16[3,512,128]{2,1,0:T(8,128)(2,1)}, bf16[3,512,128]{2,1,0:T(8,128)(2,1)}, bf16[3,512,64]{2,1,0:T(8,128)(2,1)}, bf16[3,512,512]{2,1,0:T(8,128)(2,1...) custom-call(s32[1]{0:T(128)} %bitcast.page_ref, ...), custom_call_target="tpu_custom_call" | custom-call | flops 4409999872 | bytes 1890000 | tf_op jit(solution)/shard_map/attend/pallas_call | solution.py:362
  116.4 1.9 collective-permute-done.26.refs_1_
  119.7 2.0 collective-permute-done.23
  122.6 4.1 %collective-permute-done.31.far_ref = bf16[128,768]{1,0:T(8,128)(2,1)S(1)} collective-permute-done((bf16[128,768]{1,0:T(8,128)(2,1)S(1)}, bf16[128,768]{1,0:T(8,128)(2,1)S(1)}, u32[]{:S(2)}, u32[]{:S(2)}) %collective-permute-start.31) | collective-permute-done | bytes 196640 | tf_op jit(solution)/shard_map/ppermute | solution.py:49
  127.8 3.1 %collective-permute-done.24.far_ref = bf16[128,768]{1,0:T(8,128)(2,1)S(1)} collective-permute-done((bf16[128,768]{1,0:T(8,128)(2,1)S(1)}, bf16[128,768]{1,0:T(8,128)(2,1)S(1)}, u32[]{:S(2)}, u32[]{:S(2)}) %collective-permute-start.24) | collective-permute-done | bytes 196640 | tf_op jit(solution)/shard_map/ppermute | solution.py:49
  132.0 3.1 %collective-permute-done.32.side_ref.refs_3_ = bf16[128,768]{1,0:T(8,128)(2,1)S(1)} collective-permute-done((bf16[128,768]{1,0:T(8,128)(2,1)S(1)}, bf16[128,768]{1,0:T(8,128)(2,1)S(1)}, u32[]{:S(2)}, u32[]{:S(2)}) %collective-permute-start.32) | collective-permute-done | bytes 196640 | tf_op jit(solution)/shard_map/ppermute | solution.py:49
  135.1 1.7 forward.3
  139.0 1.7 forward.2
  141.5 1.7 collective-permute-done.33.far_ref
  144.9 3.7 %collective-permute-done.29.far_ref = bf16[128,768]{1,0:T(8,128)(2,1)S(1)} collective-permute-done((bf16[128,768]{1,0:T(8,128)(2,1)S(1)}, bf16[128,768]{1,0:T(8,128)(2,1)S(1)}, u32[]{:S(2)}, u32[]{:S(2)}) %collective-permute-start.29) | collective-permute-done | bytes 196640 | tf_op jit(solution)/shard_map/ppermute | solution.py:49
  149.8 3.0 %collective-permute-done.35.side_ref.refs_7_ = bf16[128,768]{1,0:T(8,128)(2,1)S(1)} collective-permute-done((bf16[128,768]{1,0:T(8,128)(2,1)S(1)}, bf16[128,768]{1,0:T(8,128)(2,1)S(1)}, u32[]{:S(2)}, u32[]{:S(2)}) %collective-permute-start.35) | collective-permute-done | bytes 196640 | tf_op jit(solution)/shard_map/ppermute | solution.py:49
  156.8 2.7 ff_weights.1
  160.3 3.7 %collective-permute-done.36.second_ref = bf16[8,96,1536]{2,1,0:T(8,128)(2,1)S(1)} collective-permute-done((bf16[8,96,1536]{2,1,0:T(8,128)(2,1)S(1)}, bf16[8,96,1536]{2,1,0:T(8,128)(2,1)S(1)}, u32[]{:S(2)}, u32[]{:S(2)}) %collective-permute-start.36) | collective-permute-done | bytes 2359328 | tf_op jit(solution)/shard_map/ppermute | solution.py:49
  170.6 4.1 %collective-permute-done.38.far_ref = bf16[128,768]{1,0:T(8,128)(2,1)S(1)} collective-permute-done((bf16[128,768]{1,0:T(8,128)(2,1)S(1)}, bf16[128,768]{1,0:T(8,128)(2,1)S(1)}, u32[]{:S(2)}, u32[]{:S(2)}) %collective-permute-start.38) | collective-permute-done | bytes 196640 | tf_op jit(solution)/shard_map/ppermute | solution.py:49
  178.4 1.8 pad_maximum_fusion.3
  180.2 2.9 %collective-permute-done.42.refs_5_.refs_1_ = bf16[128,768]{1,0:T(8,128)(2,1)} collective-permute-done((bf16[128,768]{1,0:T(8,128)(2,1)}, bf16[128,768]{1,0:T(8,128)(2,1)}, u32[]{:S(2)}, u32[]{:S(2)}) %collective-permute-start.42) | collective-permute-done | bytes 196640 | tf_op jit(solution)/shard_map/ppermute | solution.py:49
  183.3 7.9 %attend_back.4 = (bf16[512,960]{1,0:T(8,128)(2,1)S(1)}, f32[8,96,192]{2,1,0:T(8,128)S(1)}, f32[512,768]{1,0:T(8,128)S(1)}) custom-call(s32[1]{0:T(128)} %bitcast.page_ref, bf16[128,768]{1,0:T(8,128)(2,1)} %get-tuple-element.284.refs_0_, bf16[128,768]{1,0:T(8,128)(2,1)} %collective-permute-done.39.refs_1_, bf16[128,768]{1,0:T(8,128)(2,1)} %collective-permute-done.40.refs_2_, ...), custom_call_target="tpu_custom_call" | custom-call | flops 4200000000 | bytes 1800000 | tf_op jit(solution)/shard_map/attend_back/pallas_call | solution.py:476
  191.3 2.6 out_weights.1
  195.4 7.7 %attend_back.5 = (bf16[512,960]{1,0:T(8,128)(2,1)S(1)}, f32[8,96,192]{2,1,0:T(8,128)S(1)}, f32[512,768]{1,0:T(8,128)S(1)}) custom-call(s32[1]{0:T(128)} %bitcast.page_ref, bf16[128,768]{1,0:T(8,128)(2,1)} %get-tuple-element.289.refs_4_.refs_0_, bf16[128,768]{1,0:T(8,128)(2,1)} %collective-permute-done.42.refs_5_.refs_1_, ...), custom_call_target="tpu_custom_call" | custom-call | flops 4200000000 | bytes 1800000 | tf_op jit(solution)/shard_map/attend_back/pallas_call | solution.py:476
  203.2 4.0 %attn_weights.2 = (f32[4,96,640]{2,1,0:T(8,128)S(1)}, bf16[4,96,640]{2,1,0:T(8,128)(2,1)S(1)}, f32[4,96,512]{2,1,0:T(8,128)S(1)}, bf16[4,96,512]{2,1,0:T(8,128)(2,1)S(1)}) custom-call(s32[1]{0:T(128)} %bitcast.page_ref, bf16[2,2,128,768]{3,2,1,0:T(8,128)(2,1)S(1)} %copy-done.3, bf16[2,2,128,768]{3,2,1,0:T(8,128)(2,1)S(1)} %copy-done.11, ...), custom_call_target="tpu_custom_call" | custom-call | flops 3360000000 | bytes 1440000 | tf_op jit(solution)/shard_map/attn_weights/pallas_call | solution.py:542
  210.8 8.0 %attend_back.6 = (bf16[512,960]{1,0:T(8,128)(2,1)S(1)}, f32[8,96,192]{2,1,0:T(8,128)S(1)}, f32[256,768]{1,0:T(8,128)S(1)}, bf16[256,768]{1,0:T(8,128)(2,1)S(1)}) custom-call(s32[1]{0:T(128)} %bitcast.page_ref, bf16[128,768]{1,0:T(8,128)(2,1)} %get-tuple-element.284.refs_0_, bf16[128,768]{1,0:T(8,128)(2,1)} %collective-permute-done.39.refs_1_, ...), custom_call_target="tpu_custom_call" | custom-call | flops 4200000000 | bytes 1800000 | tf_op jit(solution)/shard_map/attend_back/pallas_call | solution.py:476
  220.6 7.6 %attend_back.7 = (bf16[512,960]{1,0:T(8,128)(2,1)S(1)}, f32[8,96,192]{2,1,0:T(8,128)S(1)}, f32[256,768]{1,0:T(8,128)S(1)}, bf16[256,768]{1,0:T(8,128)(2,1)S(1)}) custom-call(s32[1]{0:T(128)} %bitcast.page_ref, bf16[128,768]{1,0:T(8,128)(2,1)} %get-tuple-element.289.refs_4_.refs_0_, bf16[128,768]{1,0:T(8,128)(2,1)} %collective-permute-done.42.refs_5_.refs_1_, ...), custom_call_target="tpu_custom_call" | custom-call | flops 4200000000 | bytes 1800000 | tf_op jit(solution)/shard_map/attend_back/pallas_call | solution.py:476
  228.3 4.0 %attn_weights.3 = (f32[4,96,640]{2,1,0:T(8,128)S(1)}, bf16[4,96,640]{2,1,0:T(8,128)(2,1)S(1)}, f32[4,96,512]{2,1,0:T(8,128)S(1)}, bf16[4,96,512]{2,1,0:T(8,128)(2,1)S(1)}) custom-call(s32[1]{0:T(128)} %bitcast.page_ref, bf16[2,2,128,768]{3,2,1,0:T(8,128)(2,1)S(1)} %copy-done.3, bf16[2,2,128,768]{3,2,1,0:T(8,128)(2,1)S(1)} %copy-done.11, ...), custom_call_target="tpu_custom_call" | custom-call | flops 3360000000 | bytes 1440000 | tf_op jit(solution)/shard_map/attn_weights/pallas_call | solution.py:542
  236.1 2.3 collective-permute-start.70
  238.4 3.1 %collective-permute-done.50 = bf16[128,768]{1,0:T(8,128)(2,1)S(1)} collective-permute-done((bf16[128,768]{1,0:T(8,128)(2,1)S(1)}, bf16[128,768]{1,0:T(8,128)(2,1)S(1)}, u32[]{:S(2)}, u32[]{:S(2)}) %collective-permute-start.50) | collective-permute-done | bytes 196640 | tf_op jit(solution)/shard_map/ppermute | solution.py:49
  241.7 2.6 collective-permute-done.56.second_ref
  249.5 4.8 %collective-permute-done.53.second_ref = bf16[4,96,640]{2,1,0:T(8,128)(2,1)S(1)} collective-permute-done((bf16[4,96,640]{2,1,0:T(8,128)(2,1)S(1)}, bf16[4,96,640]{2,1,0:T(8,128)(2,1)S(1)}, u32[]{:S(2)}, u32[]{:S(2)}) %collective-permute-start.53) | collective-permute-done | bytes 491552 | tf_op jit(solution)/shard_map/ppermute | solution.py:49
  254.5 7.9 %collective-permute-done.64 = bf16[1,96,512]{2,1,0:T(8,128)(2,1)S(1)} collective-permute-done((bf16[1,96,512]{2,1,0:T(8,128)(2,1)S(1)}, bf16[1,96,512]{2,1,0:T(8,128)(2,1)S(1)}, u32[]{:S(2)}, u32[]{:S(2)}) %collective-permute-start.64) | collective-permute-done | bytes 98336 | tf_op jit(solution)/shard_map/ppermute | solution.py:49
  263.1 2.6 collective-permute-done.63
  269.1 4.4 %collective-permute-done.62 = bf16[1,96,512]{2,1,0:T(8,128)(2,1)S(1)} collective-permute-done((bf16[1,96,512]{2,1,0:T(8,128)(2,1)S(1)}, bf16[1,96,512]{2,1,0:T(8,128)(2,1)S(1)}, u32[]{:S(2)}, u32[]{:S(2)}) %collective-permute-start.62) | collective-permute-done | bytes 98336 | tf_op jit(solution)/shard_map/ppermute | solution.py:49
  278.0 2.7 collective-permute-done.69
  (348 shorter events, 87.7 us)
Async XLA Ops:
  1.9 12.7 %collective-permute-start.6 = (bf16[1,96,640]{2,1,0:T(8,128)(2,1)S(1)}, bf16[1,96,640]{2,1,0:T(8,128)(2,1)S(1)}, u32[]{:S(2)}, u32[]{:S(2)}) collective-permute-start(bf16[1,96,640]{2,1,0:T(8,128)(2,1)S(1)} %fusion.11.first_ref), channel_id=1, source_target_pairs={{0,16},{4,20},{8,24},{12,28},{16,0},{20,4},{24,8},{28,12},{1,17},{... | collective-permute-start | bytes 368648 | tf_op jit(solution)/shard_map/ppermute | solution.py:49
  8.2 8.7 %collective-permute-start.7 = (bf16[1,96,512]{2,1,0:T(8,128)(2,1)S(1)}, bf16[1,96,512]{2,1,0:T(8,128)(2,1)S(1)}, u32[]{:S(2)}, u32[]{:S(2)}) collective-permute-start(bf16[1,96,512]{2,1,0:T(8,128)(2,1)S(1)} %fusion.14.first_ref), channel_id=1, source_target_pairs={{0,16},{4,20},{8,24},{12,28},{16,0},{20,4},{24,8},{28,12},{1,17},{... | collective-permute-start | bytes 294920 | tf_op jit(solution)/shard_map/ppermute | solution.py:49
  8.3 8.3 %collective-permute-start.3 = (bf16[2,2,24]{2,1,0:T(2,128)(2,1)S(1)}, bf16[2,2,24]{2,1,0:T(2,128)(2,1)S(1)}, u32[]{:S(2)}, u32[]{:S(2)}) collective-permute-start(bf16[2,2,24]{2,1,0:T(2,128)(2,1)S(1)} %pad_maximum_fusion.10), channel_id=1, source_target_pairs={{0,2},{1,3},{2,0},{3,1},{4,6},{5,7},{6,4},{7,5},{8,10},{9,11},{10,... | collective-permute-start | bytes 584 | tf_op jit(solution)/shard_map/ppermute | solution.py:49
  10.2 15.3 %collective-permute-start = (bf16[5,96,192]{2,1,0:T(8,128)(2,1)S(1)}, bf16[5,96,192]{2,1,0:T(8,128)(2,1)}, u32[]{:S(2)}, u32[]{:S(2)}) collective-permute-start(bf16[5,96,192]{2,1,0:T(8,128)(2,1)S(1)} %dynamic-slice_bitcast_fusion), channel_id=1, source_target_pairs={{0,2},{1,3},{2,0},{3,1},{4,6},{5,7},{6,4},{7,5},{8,10},{9,11},{10,... | collective-permute-start | bytes 552968 | tf_op jit(solution)/shard_map/ppermute | solution.py:49
  16.6 8.8 %collective-permute-start.1 = (bf16[3,3,16,128]{3,2,1,0:T(8,128)(2,1)}, bf16[3,3,16,128]{3,2,1,0:T(8,128)(2,1)S(1)}, u32[]{:S(2)}, u32[]{:S(2)}) collective-permute-start(bf16[3,3,16,128]{3,2,1,0:T(8,128)(2,1)} %dynamic-slice_bitcast_fusion.6), channel_id=1, source_target_pairs={{0,2},{1,3},{2,0},{3,1},{4,6},{5,7},{6,4},{7,5},{8,10},{9,11},{10,... | collective-permute-start | bytes 110600 | tf_op jit(solution)/shard_map/ppermute | solution.py:49
  20.6 19.4 %collective-permute-start.14 = (bf16[2,2,128,768]{3,2,1,0:T(8,128)(2,1)}, bf16[2,2,128,768]{3,2,1,0:T(8,128)(2,1)S(1)}, u32[]{:S(2)}, u32[]{:S(2)}) collective-permute-start(bf16[2,2,128,768]{3,2,1,0:T(8,128)(2,1)} %pad_maximum_fusion.1), channel_id=1, source_target_pairs={{0,2},{1,3},{2,0},{3,1},{4,6},{5,7},{6,4},{7,5},{8,10},{9,11},{10,... | collective-permute-start | bytes 2359304 | tf_op jit(solution)/shard_map/ppermute | solution.py:49
  22.3 8.5 %collective-permute-start.10 = (bf16[2,96,640]{2,1,0:T(8,128)(2,1)S(1)}, bf16[2,96,640]{2,1,0:T(8,128)(2,1)S(1)}, u32[]{:S(2)}, u32[]{:S(2)}) collective-permute-start(bf16[2,96,640]{2,1,0:T(8,128)(2,1)S(1)} %join.10.first_ref), channel_id=1, source_target_pairs={{0,4},{4,0},{8,12},{12,8},{16,20},{20,16},{24,28},{28,24},{1,5},{5... | collective-permute-start | bytes 737288 | tf_op jit(solution)/shard_map/ppermute | solution.py:49
  23.8 8.7 %collective-permute-start.9 = (bf16[2,96,512]{2,1,0:T(8,128)(2,1)S(1)}, bf16[2,96,512]{2,1,0:T(8,128)(2,1)S(1)}, u32[]{:S(2)}, u32[]{:S(2)}) collective-permute-start(bf16[2,96,512]{2,1,0:T(8,128)(2,1)S(1)} %join.11.first_ref), channel_id=1, source_target_pairs={{0,8},{4,12},{8,0},{12,4},{16,24},{20,28},{24,16},{28,20},{1,9},{5... | collective-permute-start | bytes 589832 | tf_op jit(solution)/shard_map/ppermute | solution.py:49
  26.8 11.4 %collective-permute-start.8 = (bf16[1,96,1152]{2,1,0:T(8,128)(2,1)S(1)}, bf16[1,96,1152]{2,1,0:T(8,128)(2,1)S(1)}, u32[]{:S(2)}, u32[]{:S(2)}) collective-permute-start(bf16[1,96,1152]{2,1,0:T(8,128)(2,1)S(1)} %bitcast.154), channel_id=1, source_target_pairs={{0,16},{4,20},{8,24},{12,28},{16,0},{20,4},{24,8},{28,12},{1,17},{... | collective-permute-start | bytes 663560 | tf_op jit(solution)/shard_map/ppermute | solution.py:49
  30.7 27.7 %collective-permute-start.15 = (bf16[2,2,128,768]{3,2,1,0:T(8,128)(2,1)S(1)}, bf16[2,2,128,768]{3,2,1,0:T(8,128)(2,1)}, u32[]{:S(2)}, u32[]{:S(2)}) collective-permute-start(bf16[2,2,128,768]{3,2,1,0:T(8,128)(2,1)S(1)} %pad_maximum_fusion.refs_0_), channel_id=1, source_target_pairs={{0,1},{1,0},{2,3},{3,2},{4,5},{5,4},{6,7},{7,6},{8,9},{9,8},{10,11... | collective-permute-start | bytes 2359304 | tf_op jit(solution)/shard_map/ppermute | solution.py:49
  39.9 18.4 %collective-permute-start.16 = (bf16[2,2,128,768]{3,2,1,0:T(8,128)(2,1)S(1)}, bf16[2,2,128,768]{3,2,1,0:T(8,128)(2,1)}, u32[]{:S(2)}, u32[]{:S(2)}) collective-permute-start(bf16[2,2,128,768]{3,2,1,0:T(8,128)(2,1)S(1)} %collective-permute-done.14.refs_1_), channel_id=1, source_target_pairs={{0,1},{1,0},{2,3},{3,2},{4,5},{5,4},{6,7},{7,6},{8,9},{9,8},{10,11... | collective-permute-start | bytes 2359304 | tf_op jit(solution)/shard_map/ppermute | solution.py:49
  40.0 18.0 %collective-permute-start.12 = (bf16[4,96,640]{2,1,0:T(8,128)(2,1)S(1)}, bf16[4,96,640]{2,1,0:T(8,128)(2,1)}, u32[]{:S(2)}, u32[]{:S(2)}) collective-permute-start(bf16[4,96,640]{2,1,0:T(8,128)(2,1)S(1)} %join.12.refs_4_), channel_id=1, source_target_pairs={{0,8},{4,12},{8,0},{12,4},{16,24},{20,28},{24,16},{28,20},{1,9},{5... | collective-permute-start | bytes 1474568 | tf_op jit(solution)/shard_map/ppermute | solution.py:49
  43.7 11.7 %collective-permute-start.13 = (bf16[4,96,512]{2,1,0:T(8,128)(2,1)}, bf16[4,96,512]{2,1,0:T(8,128)(2,1)}, u32[]{:S(2)}, u32[]{:S(2)}) collective-permute-start(bf16[4,96,512]{2,1,0:T(8,128)(2,1)} %copy-done.12), channel_id=1, source_target_pairs={{0,4},{4,0},{8,12},{12,8},{16,20},{20,16},{24,28},{28,24},{1,5},{5... | collective-permute-start | bytes 1179656 | tf_op jit(solution)/shard_map/ppermute | solution.py:49
  47.4 22.5 %collective-permute-start.11 = (bf16[2,96,1152]{2,1,0:T(8,128)(2,1)S(1)}, bf16[2,96,1152]{2,1,0:T(8,128)(2,1)S(1)}, u32[]{:S(2)}, u32[]{:S(2)}) collective-permute-start(bf16[2,96,1152]{2,1,0:T(8,128)(2,1)S(1)} %join.14.first_ref), channel_id=1, source_target_pairs={{0,8},{4,12},{8,0},{12,4},{16,24},{20,28},{24,16},{28,20},{1,9},{5... | collective-permute-start | bytes 1327112 | tf_op jit(solution)/shard_map/ppermute | solution.py:49
  55.4 16.2 %collective-permute-start.19 = (bf16[2,112,384]{2,1,0:T(8,128)(2,1)S(1)}, bf16[2,112,384]{2,1,0:T(8,128)(2,1)S(1)}, u32[]{:S(2)}, u32[]{:S(2)}) collective-permute-start(bf16[2,112,384]{2,1,0:T(8,128)(2,1)S(1)} %join.16.first_ref), channel_id=1, source_target_pairs={{0,16},{4,20},{8,24},{12,28},{16,0},{20,4},{24,8},{28,12},{1,17},{... | collective-permute-start | bytes 516104 | tf_op jit(solution)/shard_map/ppermute | solution.py:49
  58.0 20.5 %collective-permute-start.17 = (bf16[1,96,1536]{2,1,0:T(8,128)(2,1)S(1)}, bf16[1,96,1536]{2,1,0:T(8,128)(2,1)S(1)}, u32[]{:S(2)}, u32[]{:S(2)}) collective-permute-start(bf16[1,96,1536]{2,1,0:T(8,128)(2,1)S(1)} %maximum_bitcast_fusion.1.first_ref), channel_id=1, source_target_pairs={{0,16},{4,20},{8,24},{12,28},{16,0},{20,4},{24,8},{28,12},{1,17},{... | collective-permute-start | bytes 884744 | tf_op jit(solution)/shard_map/ppermute | solution.py:49
  70.0 29.9 %collective-permute-start.21 = (bf16[4,96,1152]{2,1,0:T(8,128)(2,1)S(1)}, bf16[4,96,1152]{2,1,0:T(8,128)(2,1)S(1)}, u32[]{:S(2)}, u32[]{:S(2)}) collective-permute-start(bf16[4,96,1152]{2,1,0:T(8,128)(2,1)S(1)} %join.15.refs_4_), channel_id=1, source_target_pairs={{0,4},{4,0},{8,12},{12,8},{16,20},{20,16},{24,28},{28,24},{1,5},{5... | collective-permute-start | bytes 2654216 | tf_op jit(solution)/shard_map/ppermute | solution.py:49
  78.5 16.3 %collective-permute-start.20 = (bf16[2,96,1536]{2,1,0:T(8,128)(2,1)S(1)}, bf16[2,96,1536]{2,1,0:T(8,128)(2,1)S(1)}, u32[]{:S(2)}, u32[]{:S(2)}) collective-permute-start(bf16[2,96,1536]{2,1,0:T(8,128)(2,1)S(1)} %join.18.first_ref), channel_id=1, source_target_pairs={{0,8},{4,12},{8,0},{12,4},{16,24},{20,28},{24,16},{28,20},{1,9},{5... | collective-permute-start | bytes 1769480 | tf_op jit(solution)/shard_map/ppermute | solution.py:49
  78.6 21.3 %collective-permute-start.22 = (bf16[4,112,384]{2,1,0:T(8,128)(2,1)S(1)}, bf16[4,112,384]{2,1,0:T(8,128)(2,1)S(1)}, u32[]{:S(2)}, u32[]{:S(2)}) collective-permute-start(bf16[4,112,384]{2,1,0:T(8,128)(2,1)S(1)} %join.17.refs_6_), channel_id=1, source_target_pairs={{0,8},{4,12},{8,0},{12,4},{16,24},{20,28},{24,16},{28,20},{1,9},{5... | collective-permute-start | bytes 1032200 | tf_op jit(solution)/shard_map/ppermute | solution.py:49
  94.9 23.3 %collective-permute-start.26 = (bf16[4,96,1536]{2,1,0:T(8,128)(2,1)S(1)}, bf16[4,96,1536]{2,1,0:T(8,128)(2,1)S(1)}, u32[]{:S(2)}, u32[]{:S(2)}) collective-permute-start(bf16[4,96,1536]{2,1,0:T(8,128)(2,1)S(1)} %join.19.refs_0_), channel_id=1, source_target_pairs={{0,4},{4,0},{8,12},{12,8},{16,20},{20,16},{24,28},{28,24},{1,5},{5... | collective-permute-start | bytes 3538952 | tf_op jit(solution)/shard_map/ppermute | solution.py:49
  115.9 19.2 %collective-permute-start.27 = (bf16[4,96,1536]{2,1,0:T(8,128)(2,1)S(1)}, bf16[4,96,1536]{2,1,0:T(8,128)(2,1)S(1)}, u32[]{:S(2)}, u32[]{:S(2)}) collective-permute-start(bf16[4,96,1536]{2,1,0:T(8,128)(2,1)S(1)} %join.19.refs_0_), channel_id=1, source_target_pairs={{0,1},{1,0},{2,3},{3,2},{4,5},{5,4},{6,7},{7,6},{8,9},{9,8},{10,11... | collective-permute-start | bytes 3538952 | tf_op jit(solution)/shard_map/ppermute | solution.py:49
  118.3 16.9 %collective-permute-start.28 = (bf16[4,96,1536]{2,1,0:T(8,128)(2,1)S(1)}, bf16[4,96,1536]{2,1,0:T(8,128)(2,1)S(1)}, u32[]{:S(2)}, u32[]{:S(2)}) collective-permute-start(bf16[4,96,1536]{2,1,0:T(8,128)(2,1)S(1)} %collective-permute-done.26.refs_1_), channel_id=1, source_target_pairs={{0,1},{1,0},{2,3},{3,2},{4,5},{5,4},{6,7},{7,6},{8,9},{9,8},{10,11... | collective-permute-start | bytes 3538952 | tf_op jit(solution)/shard_map/ppermute | solution.py:49
  121.8 9.1 %collective-permute-start.24 = (bf16[128,768]{1,0:T(8,128)(2,1)S(1)}, bf16[128,768]{1,0:T(8,128)(2,1)S(1)}, u32[]{:S(2)}, u32[]{:S(2)}) collective-permute-start(bf16[128,768]{1,0:T(8,128)(2,1)S(1)} %get-tuple-element.440), channel_id=1, source_target_pairs={{0,2},{1,3},{2,0},{3,1},{4,6},{5,7},{6,4},{7,5},{8,10},{9,11},{10,... | collective-permute-start | bytes 589832 | tf_op jit(solution)/shard_map/ppermute | solution.py:49
  127.0 8.1 %collective-permute-start.32 = (bf16[128,768]{1,0:T(8,128)(2,1)S(1)}, bf16[128,768]{1,0:T(8,128)(2,1)S(1)}, u32[]{:S(2)}, u32[]{:S(2)}) collective-permute-start(bf16[128,768]{1,0:T(8,128)(2,1)S(1)} %get-tuple-element.264.own_ref.refs_2_), channel_id=1, source_target_pairs={{0,2},{1,3},{2,0},{3,1},{4,6},{5,7},{6,4},{7,5},{8,10},{9,11},{10,... | collective-permute-start | bytes 589832 | tf_op jit(solution)/shard_map/ppermute | solution.py:49
  140.7 7.9 %collective-permute-start.29 = (bf16[128,768]{1,0:T(8,128)(2,1)S(1)}, bf16[128,768]{1,0:T(8,128)(2,1)S(1)}, u32[]{:S(2)}, u32[]{:S(2)}) collective-permute-start(bf16[128,768]{1,0:T(8,128)(2,1)S(1)} %get-tuple-element.259), channel_id=1, source_target_pairs={{0,2},{1,3},{2,0},{3,1},{4,6},{5,7},{6,4},{7,5},{8,10},{9,11},{10,... | collective-permute-start | bytes 589832 | tf_op jit(solution)/shard_map/ppermute | solution.py:49
  144.2 8.6 %collective-permute-start.35 = (bf16[128,768]{1,0:T(8,128)(2,1)S(1)}, bf16[128,768]{1,0:T(8,128)(2,1)S(1)}, u32[]{:S(2)}, u32[]{:S(2)}) collective-permute-start(bf16[128,768]{1,0:T(8,128)(2,1)S(1)} %get-tuple-element.270.own_ref.refs_6_), channel_id=1, source_target_pairs={{0,2},{1,3},{2,0},{3,1},{4,6},{5,7},{6,4},{7,5},{8,10},{9,11},{10,... | collective-permute-start | bytes 589832 | tf_op jit(solution)/shard_map/ppermute | solution.py:49
  159.6 8.1 %collective-permute-start.37 = (bf16[128,768]{1,0:T(8,128)(2,1)S(1)}, bf16[128,768]{1,0:T(8,128)(2,1)S(1)}, u32[]{:S(2)}, u32[]{:S(2)}) collective-permute-start(bf16[128,768]{1,0:T(8,128)(2,1)S(1)} %get-tuple-element.281), channel_id=1, source_target_pairs={{0,2},{1,3},{2,0},{3,1},{4,6},{5,7},{6,4},{7,5},{8,10},{9,11},{10,... | collective-permute-start | bytes 589832 | tf_op jit(solution)/shard_map/ppermute | solution.py:49
  165.5 29.1 %collective-permute-start.46 = (bf16[4,96,1536]{2,1,0:T(8,128)(2,1)}, bf16[4,96,1536]{2,1,0:T(8,128)(2,1)S(1)}, u32[]{:S(2)}, u32[]{:S(2)}) collective-permute-start(bf16[4,96,1536]{2,1,0:T(8,128)(2,1)} %get-tuple-element.279), channel_id=1, source_target_pairs={{0,4},{4,0},{8,12},{12,8},{16,20},{20,16},{24,28},{28,24},{1,5},{5... | collective-permute-start | bytes 3538952 | tf_op jit(solution)/shard_map/ppermute | solution.py:49
  169.3 8.6 %collective-permute-start.39 = (bf16[128,768]{1,0:T(8,128)(2,1)}, bf16[128,768]{1,0:T(8,128)(2,1)}, u32[]{:S(2)}, u32[]{:S(2)}) collective-permute-start(bf16[128,768]{1,0:T(8,128)(2,1)} %get-tuple-element.284.refs_0_), channel_id=1, source_target_pairs={{0,2},{1,3},{2,0},{3,1},{4,6},{5,7},{6,4},{7,5},{8,10},{9,11},{10,... | collective-permute-start | bytes 589832 | tf_op jit(solution)/shard_map/ppermute | solution.py:49
  180.2 10.9 %collective-permute-start.43 = (bf16[128,768]{1,0:T(8,128)(2,1)}, bf16[128,768]{1,0:T(8,128)(2,1)S(1)}, u32[]{:S(2)}, u32[]{:S(2)}) collective-permute-start(bf16[128,768]{1,0:T(8,128)(2,1)} %get-tuple-element.289.refs_4_.refs_0_), channel_id=1, source_target_pairs={{0,1},{1,0},{2,3},{3,2},{4,5},{5,4},{6,7},{7,6},{8,9},{9,8},{10,11... | collective-permute-start | bytes 589832 | tf_op jit(solution)/shard_map/ppermute | solution.py:49
  183.2 8.0 %collective-permute-start.44 = (bf16[128,768]{1,0:T(8,128)(2,1)}, bf16[128,768]{1,0:T(8,128)(2,1)S(1)}, u32[]{:S(2)}, u32[]{:S(2)}) collective-permute-start(bf16[128,768]{1,0:T(8,128)(2,1)} %collective-permute-done.42.refs_5_.refs_1_), channel_id=1, source_target_pairs={{0,1},{1,0},{2,3},{3,2},{4,5},{5,4},{6,7},{7,6},{8,9},{9,8},{10,11... | collective-permute-start | bytes 589832 | tf_op jit(solution)/shard_map/ppermute | solution.py:49
  193.9 16.3 %collective-permute-start.45 = (bf16[4,112,384]{2,1,0:T(8,128)(2,1)S(1)}, bf16[4,112,384]{2,1,0:T(8,128)(2,1)S(1)}, u32[]{:S(2)}, u32[]{:S(2)}) collective-permute-start(bf16[4,112,384]{2,1,0:T(8,128)(2,1)S(1)} %get-tuple-element.306), channel_id=1, source_target_pairs={{0,4},{4,0},{8,12},{12,8},{16,20},{20,16},{24,28},{28,24},{1,5},{5... | collective-permute-start | bytes 1032200 | tf_op jit(solution)/shard_map/ppermute | solution.py:49
  194.8 24.1 %collective-permute-start.48 = (bf16[2,96,1536]{2,1,0:T(8,128)(2,1)S(1)}, bf16[2,96,1536]{2,1,0:T(8,128)(2,1)S(1)}, u32[]{:S(2)}, u32[]{:S(2)}) collective-permute-start(bf16[2,96,1536]{2,1,0:T(8,128)(2,1)S(1)} %get-tuple-element.310), channel_id=1, source_target_pairs={{0,8},{4,12},{8,0},{12,4},{16,24},{20,28},{24,16},{28,20},{1,9},{5... | collective-permute-start | bytes 1769480 | tf_op jit(solution)/shard_map/ppermute | solution.py:49
  207.2 11.8 %collective-permute-start.49 = (bf16[4,96,512]{2,1,0:T(8,128)(2,1)S(1)}, bf16[4,96,512]{2,1,0:T(8,128)(2,1)S(1)}, u32[]{:S(2)}, u32[]{:S(2)}) collective-permute-start(bf16[4,96,512]{2,1,0:T(8,128)(2,1)S(1)} %get-tuple-element.322), channel_id=1, source_target_pairs={{0,4},{4,0},{8,12},{12,8},{16,20},{20,16},{24,28},{28,24},{1,5},{5... | collective-permute-start | bytes 1179656 | tf_op jit(solution)/shard_map/ppermute | solution.py:49
  208.7 24.3 %collective-permute-start.54 = (bf16[4,96,640]{2,1,0:T(8,128)(2,1)S(1)}, bf16[4,96,640]{2,1,0:T(8,128)(2,1)S(1)}, u32[]{:S(2)}, u32[]{:S(2)}) collective-permute-start(bf16[4,96,640]{2,1,0:T(8,128)(2,1)S(1)} %get-tuple-element.323), channel_id=1, source_target_pairs={{0,8},{4,12},{8,0},{12,4},{16,24},{20,28},{24,16},{28,20},{1,9},{5... | collective-permute-start | bytes 1474568 | tf_op jit(solution)/shard_map/ppermute | solution.py:49
  210.2 23.5 %collective-permute-start.58 = (bf16[2,112,384]{2,1,0:T(8,128)(2,1)S(1)}, bf16[2,112,384]{2,1,0:T(8,128)(2,1)S(1)}, u32[]{:S(2)}, u32[]{:S(2)}) collective-permute-start(bf16[2,112,384]{2,1,0:T(8,128)(2,1)S(1)} %get-tuple-element.326), channel_id=1, source_target_pairs={{0,8},{4,12},{8,0},{12,4},{16,24},{20,28},{24,16},{28,20},{1,9},{5... | collective-permute-start | bytes 516104 | tf_op jit(solution)/shard_map/ppermute | solution.py:49
  218.8 16.3 %collective-permute-start.47 = (bf16[256,768]{1,0:T(8,128)(2,1)S(1)}, bf16[256,768]{1,0:T(8,128)(2,1)S(1)}, u32[]{:S(2)}, u32[]{:S(2)}) collective-permute-start(bf16[256,768]{1,0:T(8,128)(2,1)S(1)} %get-tuple-element.335), channel_id=1, source_target_pairs={{0,1},{1,0},{2,3},{3,2},{4,5},{5,4},{6,7},{7,6},{8,9},{9,8},{10,11... | collective-permute-start | bytes 1179656 | tf_op jit(solution)/shard_map/ppermute | solution.py:49
  219.1 17.0 %collective-permute-start.57 = (bf16[2,96,512]{2,1,0:T(8,128)(2,1)S(1)}, bf16[2,96,512]{2,1,0:T(8,128)(2,1)S(1)}, u32[]{:S(2)}, u32[]{:S(2)}) collective-permute-start(bf16[2,96,512]{2,1,0:T(8,128)(2,1)S(1)} %get-tuple-element.351), channel_id=1, source_target_pairs={{0,8},{4,12},{8,0},{12,4},{16,24},{20,28},{24,16},{28,20},{1,9},{5... | collective-permute-start | bytes 589832 | tf_op jit(solution)/shard_map/ppermute | solution.py:49
  232.3 12.0 %collective-permute-start.56 = (bf16[4,96,512]{2,1,0:T(8,128)(2,1)S(1)}, bf16[4,96,512]{2,1,0:T(8,128)(2,1)S(1)}, u32[]{:S(2)}, u32[]{:S(2)}) collective-permute-start(bf16[4,96,512]{2,1,0:T(8,128)(2,1)S(1)} %get-tuple-element.364), channel_id=1, source_target_pairs={{0,4},{4,0},{8,12},{12,8},{16,20},{20,16},{24,28},{28,24},{1,5},{5... | collective-permute-start | bytes 1179656 | tf_op jit(solution)/shard_map/ppermute | solution.py:49
  233.0 21.3 %collective-permute-start.53 = (bf16[4,96,640]{2,1,0:T(8,128)(2,1)S(1)}, bf16[4,96,640]{2,1,0:T(8,128)(2,1)S(1)}, u32[]{:S(2)}, u32[]{:S(2)}) collective-permute-start(bf16[4,96,640]{2,1,0:T(8,128)(2,1)S(1)} %get-tuple-element.365), channel_id=1, source_target_pairs={{0,8},{4,12},{8,0},{12,4},{16,24},{20,28},{24,16},{28,20},{1,9},{5... | collective-permute-start | bytes 1474568 | tf_op jit(solution)/shard_map/ppermute | solution.py:49
  233.7 15.2 %collective-permute-start.55 = (bf16[2,96,640]{2,1,0:T(8,128)(2,1)S(1)}, bf16[2,96,640]{2,1,0:T(8,128)(2,1)S(1)}, u32[]{:S(2)}, u32[]{:S(2)}) collective-permute-start(bf16[2,96,640]{2,1,0:T(8,128)(2,1)S(1)} %get-tuple-element.370), channel_id=1, source_target_pairs={{0,4},{4,0},{8,12},{12,8},{16,20},{20,16},{24,28},{28,24},{1,5},{5... | collective-permute-start | bytes 737288 | tf_op jit(solution)/shard_map/ppermute | solution.py:49
  236.1 37.7 %collective-permute-start.70 = (bf16[1,96,1536]{2,1,0:T(8,128)(2,1)S(1)}, bf16[1,96,1536]{2,1,0:T(8,128)(2,1)S(1)}, u32[]{:S(2)}, u32[]{:S(2)}) collective-permute-start(bf16[1,96,1536]{2,1,0:T(8,128)(2,1)S(1)} %get-tuple-element.340), channel_id=1, source_target_pairs={{0,16},{4,20},{8,24},{12,28},{16,0},{20,4},{24,8},{28,12},{1,17},{... | collective-permute-start | bytes 884744 | tf_op jit(solution)/shard_map/ppermute | solution.py:49
  244.3 29.4 %collective-permute-start.66 = (bf16[1,112,384]{2,1,0:T(8,128)(2,1)S(1)}, bf16[1,112,384]{2,1,0:T(8,128)(2,1)S(1)}, u32[]{:S(2)}, u32[]{:S(2)}) collective-permute-start(bf16[1,112,384]{2,1,0:T(8,128)(2,1)S(1)} %get-tuple-element.376), channel_id=1, source_target_pairs={{0,16},{4,20},{8,24},{12,28},{16,0},{20,4},{24,8},{28,12},{1,17},{... | collective-permute-start | bytes 258056 | tf_op jit(solution)/shard_map/ppermute | solution.py:49
  245.6 16.8 %collective-permute-start.64 = (bf16[1,96,512]{2,1,0:T(8,128)(2,1)S(1)}, bf16[1,96,512]{2,1,0:T(8,128)(2,1)S(1)}, u32[]{:S(2)}, u32[]{:S(2)}) collective-permute-start(bf16[1,96,512]{2,1,0:T(8,128)(2,1)S(1)} %get-tuple-element.379), channel_id=1, source_target_pairs={{0,16},{4,20},{8,24},{12,28},{16,0},{20,4},{24,8},{28,12},{1,17},{... | collective-permute-start | bytes 294920 | tf_op jit(solution)/shard_map/ppermute | solution.py:49
  248.8 17.9 %collective-permute-start.60 = (bf16[2,96,512]{2,1,0:T(8,128)(2,1)S(1)}, bf16[2,96,512]{2,1,0:T(8,128)(2,1)S(1)}, u32[]{:S(2)}, u32[]{:S(2)}) collective-permute-start(bf16[2,96,512]{2,1,0:T(8,128)(2,1)S(1)} %get-tuple-element.382), channel_id=1, source_target_pairs={{0,8},{4,12},{8,0},{12,4},{16,24},{20,28},{24,16},{28,20},{1,9},{5... | collective-permute-start | bytes 589832 | tf_op jit(solution)/shard_map/ppermute | solution.py:49
  254.3 11.4 %collective-permute-start.63 = (bf16[1,96,640]{2,1,0:T(8,128)(2,1)S(1)}, bf16[1,96,640]{2,1,0:T(8,128)(2,1)S(1)}, u32[]{:S(2)}, u32[]{:S(2)}) collective-permute-start(bf16[1,96,640]{2,1,0:T(8,128)(2,1)S(1)} %get-tuple-element.385), channel_id=1, source_target_pairs={{0,16},{4,20},{8,24},{12,28},{16,0},{20,4},{24,8},{28,12},{1,17},{... | collective-permute-start | bytes 368648 | tf_op jit(solution)/shard_map/ppermute | solution.py:49
  266.7 11.2 %collective-permute-start.65 = (bf16[96,1152]{1,0:T(8,128)(2,1)S(1)}, bf16[96,1152]{1,0:T(8,128)(2,1)S(1)}, u32[]{:S(2)}, u32[]{:S(2)}) collective-permute-start(bf16[96,1152]{1,0:T(8,128)(2,1)S(1)} %pad_maximum_fusion.4), channel_id=1, source_target_pairs={{0,2},{1,3},{2,0},{3,1},{4,6},{5,7},{6,4},{7,5},{8,10},{9,11},{10,... | collective-permute-start | bytes 663560 | tf_op jit(solution)/shard_map/ppermute | solution.py:49
  273.6 8.3 %collective-permute-start.61 = (bf16[1,96,640]{2,1,0:T(8,128)(2,1)S(1)}, bf16[1,96,640]{2,1,0:T(8,128)(2,1)S(1)}, u32[]{:S(2)}, u32[]{:S(2)}) collective-permute-start(bf16[1,96,640]{2,1,0:T(8,128)(2,1)S(1)} %get-tuple-element.397), channel_id=1, source_target_pairs={{0,16},{4,20},{8,24},{12,28},{16,0},{20,4},{24,8},{28,12},{1,17},{... | collective-permute-start | bytes 368648 | tf_op jit(solution)/shard_map/ppermute | solution.py:49
  (75 other events, 627.0 us)
where the time goes:
time: 290 us; the launch traced here: 285 us
  waiting for transfers between devices  103 us (36%)
  Pallas kernels  88.6 us (31%)
  starting transfers between devices  61.4 us (21%)
  local copies, waits for them, and re-layouts  21.5 us (7%)
  other arithmetic  8.02 us (3%)
    ppermute x71, waiting for transfers between devices, swap(): lax.ppermute(value, axis, [(place, place ^ mask) for place in range(count)])  103 us
    ppermute x71, starting transfers between devices, swap(): lax.ppermute(value, axis, [(place, place ^ mask) for place in range(count)])  61.4 us
    pallas_call x4, Pallas kernels, attend(): pl.pallas_call(functools.partial(attend_kernel, batch, heads, final is no...  31.5 us
    pallas_call x4, Pallas kernels, attend_back(): pl.pallas_call(functools.partial(attend_back_kernel, heads, half), in_spe...  31.2 us
    unnamed x109, local copies, waits for them, and re-layouts  9.26 us
    pallas_call x2, Pallas kernels, attn_weights(): pl.pallas_call(functools.partial(attn_weights_kernel, batches, split), in...  8.01 us
    pallas_call x4, Pallas kernels, ff_call(): pl.pallas_call(kernel, in_specs=[VM] * (6 + len(saved)), out_shape=outs +...  6.53 us
  transfers between devices with their start and end apart: 71, of which 32 were waited for; matrix products, arithmetic and copies ran while one was open for 6% of the time, Pallas kernels for 30%

commit v1 on v0

--- a/solution.py
+++ b/solution.py
@@ -10,7 +10,7 @@
 COORD = 1024
 EPS = 1e-05
 GROUPS = 8
-SCALE = 7e8
+SCALE = 7e+08
 EXTRA = 16
 f32 = jnp.float32
 bf16 = jnp.bfloat16
@@ -143,7 +143,7 @@
         in_specs=[VM] * 2,
         out_shape=(struct(half, f32), struct(half, bf16)),
         compiler_params=PARAMS,
-        cost_estimate=cost(0.6),
+        cost_estimate=cost(0.48),
         name="fold",
     )(*pin(first, second))
 
@@ -209,12 +209,25 @@
     ]
 
 
+def page_of(place, page, masks):
+    if not direct():
+        masks = (1, 2, 4)
+    for bit, mask in enumerate(masks):
+        page = jnp.bitwise_xor(page, jnp.bitwise_and(lax.shift_right_logical(place, bit), 1) * mask)
+    return page
+
+
 def load_chunk(page, refs, masks, target, start=0):
     share = target.shape[0] // GROUPS
     stop = start + refs[0].shape[2]
-    for place, number in enumerate(places(masks)):
-        row = pl.multiple_of(jnp.bitwise_xor(page, number) * share, share)
-        target[pl.ds(row, share), start:stop] = refs[place // (GROUPS // 2)][place % (GROUPS // 2), :share]
+    for half, ref in enumerate(refs):
+
+        def body(place, carry):
+            row = page_of(place + half * (GROUPS // 2), page, masks) * share
+            target[pl.ds(pl.multiple_of(row, share), share), start:stop] = ref[place, :share]
+            return carry
+
+        lax.fori_loop(0, GROUPS // 2, body, 0)
 
 
 def load_rows(refs, target, *pick):
@@ -494,12 +507,14 @@
 
 
 def put_blocks(page, masks, full_ref, columns, keep_ref, send_ref):
-    for place, number in enumerate(places(masks)):
-        block = full_ref[jnp.bitwise_xor(page, number), :, columns]
-        if place < GROUPS // 2:
-            keep_ref[place] = block
-        else:
-            send_ref[place - GROUPS // 2] = block.astype(bf16)
+    half = GROUPS // 2
+
+    def body(place, carry):
+        keep_ref[place] = full_ref[page_of(place, page, masks), :, columns]
+        send_ref[place] = full_ref[page_of(place + half, page, masks), :, columns].astype(bf16)
+        return carry
+
+    lax.fori_loop(0, half, body, 0)
 
 
 def attn_weights_kernel(batches, split, page_ref, *refs):
@@ -549,7 +564,7 @@
             pltpu.VMEM((GROUPS, inner, columns), f32),
         ],
         compiler_params=PARAMS,
-        cost_estimate=cost(4.8),
+        cost_estimate=cost(3.12),
         name="attn_weights",
     )(page, *pin(*row_parts, *dprojs, *dtables))
 
@@ -678,7 +693,7 @@
         in_specs=[VM] * (6 * batches),
         out_shape=(struct(chunk, bf16), struct(chunk, bf16)),
         compiler_params=PARAMS,
-        cost_estimate=cost(4.2),
+        cost_estimate=cost(3.36),
         name="ff_weights",
     )(*pin(*[ref for parts in h_parts + g_parts for ref in parts], *grad_pres, *acts))
 
@@ -964,22 +979,22 @@
         gate = (back_a(here, *gate),)
     if direct():
         two_b.step(part_f.send)
-        gate += (two_b.send,)
+        part_o.step(two_b.send)
+        gate += (two_b.send, part_o.send)
     weights_a = attn_weights(after(page, *gate), row_parts, every("dproj_a"), every("dtable_a"), split)
     one_a, two_a = Scatter(*weights_a[:2], FAR_Z), Scatter(*weights_a[2:], FAR_X)
     if direct():
         two_a.start(two_b.send)
         one_a.start(two_a.send)
         one_b.step(one_a.send)
-        part_o.step(one_b.send)
-        two_b.step(part_o.send)
+        two_b.step(one_b.send)
         two_a.step(two_b.send)
         one_b.step(two_a.send)
         one_a.step(one_b.send)
         two_a.step(one_a.send)
         grad_b = jnp.concatenate([one_b.result(one_a.send), two_b.result(one_a.send)], axis=1)
+        dff, dout = part_f.result(one_a.send), part_o.result(one_a.send)
         one_a.step(two_a.send)
-        dff, dout = part_f.result(one_a.send), part_o.result(one_a.send)
         grad_a = jnp.concatenate([one_a.result(), two_a.result()], axis=1)
         dnorms = dout[share].reshape(4, 4, -1).transpose(1, 0, 2)
         dout = dout[:share]

time: 290 us -> 287 us (0.990)
  waiting for transfers between devices: 103 us -> 93.3 us
    ppermute x71, waiting for transfers between devices: 103 us -> 93.3 us  [swap(): lax.ppermute(value, axis, [(place, place ^ mask) for place in range(count)])]
  transfers between devices with their start and end apart: 71 -> 71, of which waited for: 32 -> 31; matrix products, arithmetic and copies ran while one was open for 6% -> 7% of each run, Pallas kernels for 30% -> 30%
where the time goes in v1:
time: 287 us; the launch traced here: 282 us
  waiting for transfers between devices  93.3 us (33%)
  Pallas kernels  89.6 us (31%)
  starting transfers between devices  63.9 us (22%)
  local copies, waits for them, and re-layouts  22.2 us (8%)
  other arithmetic  10.8 us (4%)
    ppermute x71, waiting for transfers between devices, swap(): lax.ppermute(value, axis, [(place, place ^ mask) for place in range(count)])  93.3 us
    ppermute x71, starting transfers between devices, swap(): lax.ppermute(value, axis, [(place, place ^ mask) for place in range(count)])  63.9 us
    pallas_call x4, Pallas kernels, attend(): pl.pallas_call(functools.partial(attend_kernel, batch, heads, final is no...  32.4 us
    pallas_call x4, Pallas kernels, attend_back(): pl.pallas_call(functools.partial(attend_back_kernel, heads, half), in_spe...  31.2 us
    unnamed x109, local copies, waits for them, and re-layouts  9.26 us
    pallas_call x2, Pallas kernels, attn_weights(): pl.pallas_call(functools.partial(attn_weights_kernel, batches, split), in...  8.11 us
    pallas_call x4, Pallas kernels, ff_call(): pl.pallas_call(kernel, in_specs=[VM] * (6 + len(saved)), out_shape=outs +...  6.53 us
  transfers between devices with their start and end apart: 71, of which 31 were waited for; matrix products, arithmetic and copies ran while one was open for 7% of the time, Pallas kernels for 30%

profile of v1, /device:TPU:0, one launch (start us, length us, event | category | flops | bytes accessed | tf_op | source)
XLA Modules:
  0.0 282.3 jit_solution(10451058948047645451)
XLA Ops:
  1.9 4.1 %collective-permute-start.6 = (bf16[1,96,640]{2,1,0:T(8,128)(2,1)S(1)}, bf16[1,96,640]{2,1,0:T(8,128)(2,1)S(1)}, u32[]{:S(2)}, u32[]{:S(2)}) collective-permute-start(bf16[1,96,640]{2,1,0:T(8,128)(2,1)S(1)} %fusion.11.first_ref), channel_id=1, source_target_pairs={{0,16},{4,20},{8,24},{12,28},{16,0},{20,4},{24,8},{28,12},{1,17},{... | collective-permute-start | bytes 368648 | tf_op jit(solution)/shard_map/ppermute | solution.py:49
  8.3 1.9 collective-permute-start.3
  14.7 1.9 collective-permute-start.2
  18.0 1.7 collective-permute-done.2
  26.8 2.7 collective-permute-start.8
  34.9 3.2 %collective-permute-done.8.second_ref = bf16[1,96,1152]{2,1,0:T(8,128)(2,1)S(1)} collective-permute-done((bf16[1,96,1152]{2,1,0:T(8,128)(2,1)S(1)}, bf16[1,96,1152]{2,1,0:T(8,128)(2,1)S(1)}, u32[]{:S(2)}, u32[]{:S(2)}) %collective-permute-start.8) | collective-permute-done | bytes 221216 | tf_op jit(solution)/shard_map/ppermute | solution.py:49
  38.2 1.7 collective-permute-done.14.refs_1_
  44.3 3.1 %collective-permute-done.18.second_ref = bf16[1,112,384]{2,1,0:T(8,128)(2,1)S(1)} collective-permute-done((bf16[1,112,384]{2,1,0:T(8,128)(2,1)S(1)}, bf16[1,112,384]{2,1,0:T(8,128)(2,1)S(1)}, u32[]{:S(2)}, u32[]{:S(2)}) %collective-permute-start.18) | collective-permute-done | bytes 86048 | tf_op jit(solution)/shard_map/ppermute | solution.py:49
  47.9 7.6 %collective-permute-done.13.refs_7_ = bf16[4,96,512]{2,1,0:T(8,128)(2,1)} collective-permute-done((bf16[4,96,512]{2,1,0:T(8,128)(2,1)}, bf16[4,96,512]{2,1,0:T(8,128)(2,1)}, u32[]{:S(2)}, u32[]{:S(2)}) %collective-permute-start.13) | collective-permute-done | bytes 393248 | tf_op jit(solution)/shard_map/ppermute | solution.py:49
  55.4 2.6 collective-permute-start.19
  59.4 8.2 %attend.4 = (bf16[3,512,128]{2,1,0:T(8,128)(2,1)}, bf16[3,512,128]{2,1,0:T(8,128)(2,1)}, bf16[3,512,64]{2,1,0:T(8,128)(2,1)}, bf16[3,512,512]{2,1,0:T(8,128)(2,1...) custom-call(s32[1]{0:T(128)} %bitcast.page_ref, bf16[2,2,128,768]{3,2,1,0:T(8,128)(2,1)S(1)} %pad_maximum_fusion.refs_0_, ...), custom_call_target="tpu_custom_call" | custom-call | flops 4409999872 | bytes 1890000 | tf_op jit(solution)/shard_map/attend/pallas_call | solution.py:375
  67.6 2.2 collective-permute-done.11.second_ref
  70.0 1.7 collective-permute-start.21
  71.7 6.8 %collective-permute-done.17.second_ref = bf16[1,96,1536]{2,1,0:T(8,128)(2,1)S(1)} collective-permute-done((bf16[1,96,1536]{2,1,0:T(8,128)(2,1)S(1)}, bf16[1,96,1536]{2,1,0:T(8,128)(2,1)S(1)}, u32[]{:S(2)}, u32[]{:S(2)}) %collective-permute-start.17) | collective-permute-done | bytes 294944 | tf_op jit(solution)/shard_map/ppermute | solution.py:49
  78.6 2.0 collective-permute-start.22
  80.6 7.8 %attend.5 = (bf16[3,512,128]{2,1,0:T(8,128)(2,1)}, bf16[3,512,128]{2,1,0:T(8,128)(2,1)}, bf16[3,512,64]{2,1,0:T(8,128)(2,1)}, bf16[3,512,512]{2,1,0:T(8,128)(2,1...) custom-call(s32[1]{0:T(128)} %bitcast.page_ref, bf16[2,2,128,768]{3,2,1,0:T(8,128)(2,1)S(1)} %pad_maximum_fusion.refs_0_, ...), custom_call_target="tpu_custom_call" | custom-call | flops 4409999872 | bytes 1890000 | tf_op jit(solution)/shard_map/attend/pallas_call | solution.py:375
  88.5 6.4 %collective-permute-done.20.second_ref = bf16[2,96,1536]{2,1,0:T(8,128)(2,1)S(1)} collective-permute-done((bf16[2,96,1536]{2,1,0:T(8,128)(2,1)S(1)}, bf16[2,96,1536]{2,1,0:T(8,128)(2,1)S(1)}, u32[]{:S(2)}, u32[]{:S(2)}) %collective-permute-start.20) | collective-permute-done | bytes 589856 | tf_op jit(solution)/shard_map/ppermute | solution.py:49
  96.4 3.5 %collective-permute-done.22.refs_7_ = bf16[4,112,384]{2,1,0:T(8,128)(2,1)S(1)} collective-permute-done((bf16[4,112,384]{2,1,0:T(8,128)(2,1)S(1)}, bf16[4,112,384]{2,1,0:T(8,128)(2,1)S(1)}, u32[]{:S(2)}, u32[]{:S(2)}) %collective-permute-start.22) | collective-permute-done | bytes 344096 | tf_op jit(solution)/shard_map/ppermute | solution.py:49
  99.9 8.4 %attend.6 = (bf16[3,512,128]{2,1,0:T(8,128)(2,1)}, bf16[3,512,128]{2,1,0:T(8,128)(2,1)}, bf16[3,512,64]{2,1,0:T(8,128)(2,1)}, bf16[3,512,512]{2,1,0:T(8,128)(2,1...) custom-call(s32[1]{0:T(128)} %bitcast.page_ref, ...), custom_call_target="tpu_custom_call" | custom-call | flops 4409999872 | bytes 1890000 | tf_op jit(solution)/shard_map/attend/pallas_call | solution.py:375
  108.3 8.0 %attend.7 = (bf16[3,512,128]{2,1,0:T(8,128)(2,1)}, bf16[3,512,128]{2,1,0:T(8,128)(2,1)}, bf16[3,512,64]{2,1,0:T(8,128)(2,1)}, bf16[3,512,512]{2,1,0:T(8,128)(2,1...) custom-call(s32[1]{0:T(128)} %bitcast.page_ref, ...), custom_call_target="tpu_custom_call" | custom-call | flops 4409999872 | bytes 1890000 | tf_op jit(solution)/shard_map/attend/pallas_call | solution.py:375
  119.7 2.4 collective-permute-done.23
  123.0 3.5 %collective-permute-done.31.far_ref = bf16[128,768]{1,0:T(8,128)(2,1)S(1)} collective-permute-done((bf16[128,768]{1,0:T(8,128)(2,1)S(1)}, bf16[128,768]{1,0:T(8,128)(2,1)S(1)}, u32[]{:S(2)}, u32[]{:S(2)}) %collective-permute-start.31) | collective-permute-done | bytes 196640 | tf_op jit(solution)/shard_map/ppermute | solution.py:49
  127.6 3.1 %collective-permute-done.24.far_ref = bf16[128,768]{1,0:T(8,128)(2,1)S(1)} collective-permute-done((bf16[128,768]{1,0:T(8,128)(2,1)S(1)}, bf16[128,768]{1,0:T(8,128)(2,1)S(1)}, u32[]{:S(2)}, u32[]{:S(2)}) %collective-permute-start.24) | collective-permute-done | bytes 196640 | tf_op jit(solution)/shard_map/ppermute | solution.py:49
  131.8 3.1 %collective-permute-done.32.side_ref.refs_3_ = bf16[128,768]{1,0:T(8,128)(2,1)S(1)} collective-permute-done((bf16[128,768]{1,0:T(8,128)(2,1)S(1)}, bf16[128,768]{1,0:T(8,128)(2,1)S(1)}, u32[]{:S(2)}, u32[]{:S(2)}) %collective-permute-start.32) | collective-permute-done | bytes 196640 | tf_op jit(solution)/shard_map/ppermute | solution.py:49
  134.9 1.7 forward.3
  138.8 1.7 forward.2
  141.3 1.7 collective-permute-done.33.far_ref
  144.7 3.7 %collective-permute-done.29.far_ref = bf16[128,768]{1,0:T(8,128)(2,1)S(1)} collective-permute-done((bf16[128,768]{1,0:T(8,128)(2,1)S(1)}, bf16[128,768]{1,0:T(8,128)(2,1)S(1)}, u32[]{:S(2)}, u32[]{:S(2)}) %collective-permute-start.29) | collective-permute-done | bytes 196640 | tf_op jit(solution)/shard_map/ppermute | solution.py:49
  149.6 3.0 %collective-permute-done.35.side_ref.refs_7_ = bf16[128,768]{1,0:T(8,128)(2,1)S(1)} collective-permute-done((bf16[128,768]{1,0:T(8,128)(2,1)S(1)}, bf16[128,768]{1,0:T(8,128)(2,1)S(1)}, u32[]{:S(2)}, u32[]{:S(2)}) %collective-permute-start.35) | collective-permute-done | bytes 196640 | tf_op jit(solution)/shard_map/ppermute | solution.py:49
  156.8 2.6 ff_weights.1
  160.3 3.7 %collective-permute-done.36.second_ref = bf16[8,96,1536]{2,1,0:T(8,128)(2,1)S(1)} collective-permute-done((bf16[8,96,1536]{2,1,0:T(8,128)(2,1)S(1)}, bf16[8,96,1536]{2,1,0:T(8,128)(2,1)S(1)}, u32[]{:S(2)}, u32[]{:S(2)}) %collective-permute-start.36) | collective-permute-done | bytes 2359328 | tf_op jit(solution)/shard_map/ppermute | solution.py:49
  170.6 4.0 %collective-permute-done.38.far_ref = bf16[128,768]{1,0:T(8,128)(2,1)S(1)} collective-permute-done((bf16[128,768]{1,0:T(8,128)(2,1)S(1)}, bf16[128,768]{1,0:T(8,128)(2,1)S(1)}, u32[]{:S(2)}, u32[]{:S(2)}) %collective-permute-start.38) | collective-permute-done | bytes 196640 | tf_op jit(solution)/shard_map/ppermute | solution.py:49
  178.4 1.8 pad_maximum_fusion.3
  180.2 2.9 %collective-permute-done.42.refs_5_.refs_1_ = bf16[128,768]{1,0:T(8,128)(2,1)} collective-permute-done((bf16[128,768]{1,0:T(8,128)(2,1)}, bf16[128,768]{1,0:T(8,128)(2,1)}, u32[]{:S(2)}, u32[]{:S(2)}) %collective-permute-start.42) | collective-permute-done | bytes 196640 | tf_op jit(solution)/shard_map/ppermute | solution.py:49
  183.3 7.9 %attend_back.4 = (bf16[512,960]{1,0:T(8,128)(2,1)S(1)}, f32[8,96,192]{2,1,0:T(8,128)S(1)}, f32[512,768]{1,0:T(8,128)S(1)}) custom-call(s32[1]{0:T(128)} %bitcast.page_ref, bf16[128,768]{1,0:T(8,128)(2,1)} %get-tuple-element.284.refs_0_, bf16[128,768]{1,0:T(8,128)(2,1)} %collective-permute-done.39.refs_1_, bf16[128,768]{1,0:T(8,128)(2,1)} %collective-permute-done.40.refs_2_, ...), custom_call_target="tpu_custom_call" | custom-call | flops 4200000000 | bytes 1800000 | tf_op jit(solution)/shard_map/attend_back/pallas_call | solution.py:489
  191.2 2.6 out_weights.1
  195.5 7.8 %attend_back.5 = (bf16[512,960]{1,0:T(8,128)(2,1)S(1)}, f32[8,96,192]{2,1,0:T(8,128)S(1)}, f32[512,768]{1,0:T(8,128)S(1)}) custom-call(s32[1]{0:T(128)} %bitcast.page_ref, bf16[128,768]{1,0:T(8,128)(2,1)} %get-tuple-element.289.refs_4_.refs_0_, bf16[128,768]{1,0:T(8,128)(2,1)} %collective-permute-done.42.refs_5_.refs_1_, ...), custom_call_target="tpu_custom_call" | custom-call | flops 4200000000 | bytes 1800000 | tf_op jit(solution)/shard_map/attend_back/pallas_call | solution.py:489
  203.2 4.1 %attn_weights.2 = (f32[4,96,640]{2,1,0:T(8,128)S(1)}, bf16[4,96,640]{2,1,0:T(8,128)(2,1)S(1)}, f32[4,96,512]{2,1,0:T(8,128)S(1)}, bf16[4,96,512]{2,1,0:T(8,128)(2,1)S(1)}) custom-call(s32[1]{0:T(128)} %bitcast.page_ref, bf16[2,2,128,768]{3,2,1,0:T(8,128)(2,1)S(1)} %copy-done.3, bf16[2,2,128,768]{3,2,1,0:T(8,128)(2,1)S(1)} %copy-done.11, ...), custom_call_target="tpu_custom_call" | custom-call | flops 2184000000 | bytes 936000 | tf_op jit(solution)/shard_map/attn_weights/pallas_call | solution.py:557
  210.9 8.0 %attend_back.6 = (bf16[512,960]{1,0:T(8,128)(2,1)S(1)}, f32[8,96,192]{2,1,0:T(8,128)S(1)}, f32[256,768]{1,0:T(8,128)S(1)}, bf16[256,768]{1,0:T(8,128)(2,1)S(1)}) custom-call(s32[1]{0:T(128)} %bitcast.page_ref, bf16[128,768]{1,0:T(8,128)(2,1)} %get-tuple-element.284.refs_0_, bf16[128,768]{1,0:T(8,128)(2,1)} %collective-permute-done.39.refs_1_, ...), custom_call_target="tpu_custom_call" | custom-call | flops 4200000000 | bytes 1800000 | tf_op jit(solution)/shard_map/attend_back/pallas_call | solution.py:489
  219.1 2.3 collective-permute-start.70
  222.1 7.6 %attend_back.7 = (bf16[512,960]{1,0:T(8,128)(2,1)S(1)}, f32[8,96,192]{2,1,0:T(8,128)S(1)}, f32[256,768]{1,0:T(8,128)S(1)}, bf16[256,768]{1,0:T(8,128)(2,1)S(1)}) custom-call(s32[1]{0:T(128)} %bitcast.page_ref, bf16[128,768]{1,0:T(8,128)(2,1)} %get-tuple-element.289.refs_4_.refs_0_, bf16[128,768]{1,0:T(8,128)(2,1)} %collective-permute-done.42.refs_5_.refs_1_, ...), custom_call_target="tpu_custom_call" | custom-call | flops 4200000000 | bytes 1800000 | tf_op jit(solution)/shard_map/attend_back/pallas_call | solution.py:489
  229.7 4.0 %attn_weights.3 = (f32[4,96,640]{2,1,0:T(8,128)S(1)}, bf16[4,96,640]{2,1,0:T(8,128)(2,1)S(1)}, f32[4,96,512]{2,1,0:T(8,128)S(1)}, bf16[4,96,512]{2,1,0:T(8,128)(2,1)S(1)}) custom-call(s32[1]{0:T(128)} %bitcast.page_ref, bf16[2,2,128,768]{3,2,1,0:T(8,128)(2,1)S(1)} %copy-done.3, bf16[2,2,128,768]{3,2,1,0:T(8,128)(2,1)S(1)} %copy-done.11, ...), custom_call_target="tpu_custom_call" | custom-call | flops 2184000000 | bytes 936000 | tf_op jit(solution)/shard_map/attn_weights/pallas_call | solution.py:557
  238.5 4.1 %collective-permute-done.51 = bf16[128,768]{1,0:T(8,128)(2,1)S(1)} collective-permute-done((bf16[128,768]{1,0:T(8,128)(2,1)S(1)}, bf16[128,768]{1,0:T(8,128)(2,1)S(1)}, u32[]{:S(2)}, u32[]{:S(2)}) %collective-permute-start.51) | collective-permute-done | bytes 196640 | tf_op jit(solution)/shard_map/ppermute | solution.py:49
  242.8 3.1 %collective-permute-done.57.second_ref = bf16[4,96,512]{2,1,0:T(8,128)(2,1)S(1)} collective-permute-done((bf16[4,96,512]{2,1,0:T(8,128)(2,1)S(1)}, bf16[4,96,512]{2,1,0:T(8,128)(2,1)S(1)}, u32[]{:S(2)}, u32[]{:S(2)}) %collective-permute-start.57) | collective-permute-done | bytes 393248 | tf_op jit(solution)/shard_map/ppermute | solution.py:49
  245.9 1.6 collective-permute-start.66
  252.5 1.9 collective-permute-done.66
  269.2 3.6 %collective-permute-done.62 = bf16[1,96,512]{2,1,0:T(8,128)(2,1)S(1)} collective-permute-done((bf16[1,96,512]{2,1,0:T(8,128)(2,1)S(1)}, bf16[1,96,512]{2,1,0:T(8,128)(2,1)S(1)}, u32[]{:S(2)}, u32[]{:S(2)}) %collective-permute-start.62) | collective-permute-done | bytes 98336 | tf_op jit(solution)/shard_map/ppermute | solution.py:49
  273.0 6.0 %collective-permute-done.61 = bf16[1,96,640]{2,1,0:T(8,128)(2,1)S(1)} collective-permute-done((bf16[1,96,640]{2,1,0:T(8,128)(2,1)S(1)}, bf16[1,96,640]{2,1,0:T(8,128)(2,1)S(1)}, u32[]{:S(2)}, u32[]{:S(2)}) %collective-permute-start.61) | collective-permute-done | bytes 122912 | tf_op jit(solution)/shard_map/ppermute | solution.py:49
  (348 shorter events, 90.7 us)
Async XLA Ops:
  1.9 12.7 %collective-permute-start.6 = (bf16[1,96,640]{2,1,0:T(8,128)(2,1)S(1)}, bf16[1,96,640]{2,1,0:T(8,128)(2,1)S(1)}, u32[]{:S(2)}, u32[]{:S(2)}) collective-permute-start(bf16[1,96,640]{2,1,0:T(8,128)(2,1)S(1)} %fusion.11.first_ref), channel_id=1, source_target_pairs={{0,16},{4,20},{8,24},{12,28},{16,0},{20,4},{24,8},{28,12},{1,17},{... | collective-permute-start | bytes 368648 | tf_op jit(solution)/shard_map/ppermute | solution.py:49
  8.2 8.7 %collective-permute-start.7 = (bf16[1,96,512]{2,1,0:T(8,128)(2,1)S(1)}, bf16[1,96,512]{2,1,0:T(8,128)(2,1)S(1)}, u32[]{:S(2)}, u32[]{:S(2)}) collective-permute-start(bf16[1,96,512]{2,1,0:T(8,128)(2,1)S(1)} %fusion.14.first_ref), channel_id=1, source_target_pairs={{0,16},{4,20},{8,24},{12,28},{16,0},{20,4},{24,8},{28,12},{1,17},{... | collective-permute-start | bytes 294920 | tf_op jit(solution)/shard_map/ppermute | solution.py:49
  8.3 8.3 %collective-permute-start.3 = (bf16[2,2,24]{2,1,0:T(2,128)(2,1)S(1)}, bf16[2,2,24]{2,1,0:T(2,128)(2,1)S(1)}, u32[]{:S(2)}, u32[]{:S(2)}) collective-permute-start(bf16[2,2,24]{2,1,0:T(2,128)(2,1)S(1)} %pad_maximum_fusion.10), channel_id=1, source_target_pairs={{0,2},{1,3},{2,0},{3,1},{4,6},{5,7},{6,4},{7,5},{8,10},{9,11},{10,... | collective-permute-start | bytes 584 | tf_op jit(solution)/shard_map/ppermute | solution.py:49
  10.2 15.3 %collective-permute-start = (bf16[5,96,192]{2,1,0:T(8,128)(2,1)S(1)}, bf16[5,96,192]{2,1,0:T(8,128)(2,1)}, u32[]{:S(2)}, u32[]{:S(2)}) collective-permute-start(bf16[5,96,192]{2,1,0:T(8,128)(2,1)S(1)} %dynamic-slice_bitcast_fusion), channel_id=1, source_target_pairs={{0,2},{1,3},{2,0},{3,1},{4,6},{5,7},{6,4},{7,5},{8,10},{9,11},{10,... | collective-permute-start | bytes 552968 | tf_op jit(solution)/shard_map/ppermute | solution.py:49
  16.6 8.8 %collective-permute-start.1 = (bf16[3,3,16,128]{3,2,1,0:T(8,128)(2,1)}, bf16[3,3,16,128]{3,2,1,0:T(8,128)(2,1)S(1)}, u32[]{:S(2)}, u32[]{:S(2)}) collective-permute-start(bf16[3,3,16,128]{3,2,1,0:T(8,128)(2,1)} %dynamic-slice_bitcast_fusion.6), channel_id=1, source_target_pairs={{0,2},{1,3},{2,0},{3,1},{4,6},{5,7},{6,4},{7,5},{8,10},{9,11},{10,... | collective-permute-start | bytes 110600 | tf_op jit(solution)/shard_map/ppermute | solution.py:49
  20.6 19.4 %collective-permute-start.14 = (bf16[2,2,128,768]{3,2,1,0:T(8,128)(2,1)}, bf16[2,2,128,768]{3,2,1,0:T(8,128)(2,1)S(1)}, u32[]{:S(2)}, u32[]{:S(2)}) collective-permute-start(bf16[2,2,128,768]{3,2,1,0:T(8,128)(2,1)} %pad_maximum_fusion.1), channel_id=1, source_target_pairs={{0,2},{1,3},{2,0},{3,1},{4,6},{5,7},{6,4},{7,5},{8,10},{9,11},{10,... | collective-permute-start | bytes 2359304 | tf_op jit(solution)/shard_map/ppermute | solution.py:49
  22.3 8.5 %collective-permute-start.10 = (bf16[2,96,640]{2,1,0:T(8,128)(2,1)S(1)}, bf16[2,96,640]{2,1,0:T(8,128)(2,1)S(1)}, u32[]{:S(2)}, u32[]{:S(2)}) collective-permute-start(bf16[2,96,640]{2,1,0:T(8,128)(2,1)S(1)} %join.10.first_ref), channel_id=1, source_target_pairs={{0,4},{4,0},{8,12},{12,8},{16,20},{20,16},{24,28},{28,24},{1,5},{5... | collective-permute-start | bytes 737288 | tf_op jit(solution)/shard_map/ppermute | solution.py:49
  23.8 8.7 %collective-permute-start.9 = (bf16[2,96,512]{2,1,0:T(8,128)(2,1)S(1)}, bf16[2,96,512]{2,1,0:T(8,128)(2,1)S(1)}, u32[]{:S(2)}, u32[]{:S(2)}) collective-permute-start(bf16[2,96,512]{2,1,0:T(8,128)(2,1)S(1)} %join.11.first_ref), channel_id=1, source_target_pairs={{0,8},{4,12},{8,0},{12,4},{16,24},{20,28},{24,16},{28,20},{1,9},{5... | collective-permute-start | bytes 589832 | tf_op jit(solution)/shard_map/ppermute | solution.py:49
  26.8 11.4 %collective-permute-start.8 = (bf16[1,96,1152]{2,1,0:T(8,128)(2,1)S(1)}, bf16[1,96,1152]{2,1,0:T(8,128)(2,1)S(1)}, u32[]{:S(2)}, u32[]{:S(2)}) collective-permute-start(bf16[1,96,1152]{2,1,0:T(8,128)(2,1)S(1)} %bitcast.154), channel_id=1, source_target_pairs={{0,16},{4,20},{8,24},{12,28},{16,0},{20,4},{24,8},{28,12},{1,17},{... | collective-permute-start | bytes 663560 | tf_op jit(solution)/shard_map/ppermute | solution.py:49
  30.7 27.7 %collective-permute-start.15 = (bf16[2,2,128,768]{3,2,1,0:T(8,128)(2,1)S(1)}, bf16[2,2,128,768]{3,2,1,0:T(8,128)(2,1)}, u32[]{:S(2)}, u32[]{:S(2)}) collective-permute-start(bf16[2,2,128,768]{3,2,1,0:T(8,128)(2,1)S(1)} %pad_maximum_fusion.refs_0_), channel_id=1, source_target_pairs={{0,1},{1,0},{2,3},{3,2},{4,5},{5,4},{6,7},{7,6},{8,9},{9,8},{10,11... | collective-permute-start | bytes 2359304 | tf_op jit(solution)/shard_map/ppermute | solution.py:49
  39.9 18.4 %collective-permute-start.16 = (bf16[2,2,128,768]{3,2,1,0:T(8,128)(2,1)S(1)}, bf16[2,2,128,768]{3,2,1,0:T(8,128)(2,1)}, u32[]{:S(2)}, u32[]{:S(2)}) collective-permute-start(bf16[2,2,128,768]{3,2,1,0:T(8,128)(2,1)S(1)} %collective-permute-done.14.refs_1_), channel_id=1, source_target_pairs={{0,1},{1,0},{2,3},{3,2},{4,5},{5,4},{6,7},{7,6},{8,9},{9,8},{10,11... | collective-permute-start | bytes 2359304 | tf_op jit(solution)/shard_map/ppermute | solution.py:49
  40.0 18.0 %collective-permute-start.12 = (bf16[4,96,640]{2,1,0:T(8,128)(2,1)S(1)}, bf16[4,96,640]{2,1,0:T(8,128)(2,1)}, u32[]{:S(2)}, u32[]{:S(2)}) collective-permute-start(bf16[4,96,640]{2,1,0:T(8,128)(2,1)S(1)} %join.12.refs_4_), channel_id=1, source_target_pairs={{0,8},{4,12},{8,0},{12,4},{16,24},{20,28},{24,16},{28,20},{1,9},{5... | collective-permute-start | bytes 1474568 | tf_op jit(solution)/shard_map/ppermute | solution.py:49
  43.7 11.7 %collective-permute-start.13 = (bf16[4,96,512]{2,1,0:T(8,128)(2,1)}, bf16[4,96,512]{2,1,0:T(8,128)(2,1)}, u32[]{:S(2)}, u32[]{:S(2)}) collective-permute-start(bf16[4,96,512]{2,1,0:T(8,128)(2,1)} %copy-done.12), channel_id=1, source_target_pairs={{0,4},{4,0},{8,12},{12,8},{16,20},{20,16},{24,28},{28,24},{1,5},{5... | collective-permute-start | bytes 1179656 | tf_op jit(solution)/shard_map/ppermute | solution.py:49
  47.4 22.5 %collective-permute-start.11 = (bf16[2,96,1152]{2,1,0:T(8,128)(2,1)S(1)}, bf16[2,96,1152]{2,1,0:T(8,128)(2,1)S(1)}, u32[]{:S(2)}, u32[]{:S(2)}) collective-permute-start(bf16[2,96,1152]{2,1,0:T(8,128)(2,1)S(1)} %join.14.first_ref), channel_id=1, source_target_pairs={{0,8},{4,12},{8,0},{12,4},{16,24},{20,28},{24,16},{28,20},{1,9},{5... | collective-permute-start | bytes 1327112 | tf_op jit(solution)/shard_map/ppermute | solution.py:49
  55.4 16.2 %collective-permute-start.19 = (bf16[2,112,384]{2,1,0:T(8,128)(2,1)S(1)}, bf16[2,112,384]{2,1,0:T(8,128)(2,1)S(1)}, u32[]{:S(2)}, u32[]{:S(2)}) collective-permute-start(bf16[2,112,384]{2,1,0:T(8,128)(2,1)S(1)} %join.16.first_ref), channel_id=1, source_target_pairs={{0,16},{4,20},{8,24},{12,28},{16,0},{20,4},{24,8},{28,12},{1,17},{... | collective-permute-start | bytes 516104 | tf_op jit(solution)/shard_map/ppermute | solution.py:49
  58.0 20.5 %collective-permute-start.17 = (bf16[1,96,1536]{2,1,0:T(8,128)(2,1)S(1)}, bf16[1,96,1536]{2,1,0:T(8,128)(2,1)S(1)}, u32[]{:S(2)}, u32[]{:S(2)}) collective-permute-start(bf16[1,96,1536]{2,1,0:T(8,128)(2,1)S(1)} %maximum_bitcast_fusion.1.first_ref), channel_id=1, source_target_pairs={{0,16},{4,20},{8,24},{12,28},{16,0},{20,4},{24,8},{28,12},{1,17},{... | collective-permute-start | bytes 884744 | tf_op jit(solution)/shard_map/ppermute | solution.py:49
  70.0 29.9 %collective-permute-start.21 = (bf16[4,96,1152]{2,1,0:T(8,128)(2,1)S(1)}, bf16[4,96,1152]{2,1,0:T(8,128)(2,1)S(1)}, u32[]{:S(2)}, u32[]{:S(2)}) collective-permute-start(bf16[4,96,1152]{2,1,0:T(8,128)(2,1)S(1)} %join.15.refs_4_), channel_id=1, source_target_pairs={{0,4},{4,0},{8,12},{12,8},{16,20},{20,16},{24,28},{28,24},{1,5},{5... | collective-permute-start | bytes 2654216 | tf_op jit(solution)/shard_map/ppermute | solution.py:49
  78.5 16.3 %collective-permute-start.20 = (bf16[2,96,1536]{2,1,0:T(8,128)(2,1)S(1)}, bf16[2,96,1536]{2,1,0:T(8,128)(2,1)S(1)}, u32[]{:S(2)}, u32[]{:S(2)}) collective-permute-start(bf16[2,96,1536]{2,1,0:T(8,128)(2,1)S(1)} %join.18.first_ref), channel_id=1, source_target_pairs={{0,8},{4,12},{8,0},{12,4},{16,24},{20,28},{24,16},{28,20},{1,9},{5... | collective-permute-start | bytes 1769480 | tf_op jit(solution)/shard_map/ppermute | solution.py:49
  78.6 21.3 %collective-permute-start.22 = (bf16[4,112,384]{2,1,0:T(8,128)(2,1)S(1)}, bf16[4,112,384]{2,1,0:T(8,128)(2,1)S(1)}, u32[]{:S(2)}, u32[]{:S(2)}) collective-permute-start(bf16[4,112,384]{2,1,0:T(8,128)(2,1)S(1)} %join.17.refs_6_), channel_id=1, source_target_pairs={{0,8},{4,12},{8,0},{12,4},{16,24},{20,28},{24,16},{28,20},{1,9},{5... | collective-permute-start | bytes 1032200 | tf_op jit(solution)/shard_map/ppermute | solution.py:49
  94.9 23.3 %collective-permute-start.26 = (bf16[4,96,1536]{2,1,0:T(8,128)(2,1)S(1)}, bf16[4,96,1536]{2,1,0:T(8,128)(2,1)S(1)}, u32[]{:S(2)}, u32[]{:S(2)}) collective-permute-start(bf16[4,96,1536]{2,1,0:T(8,128)(2,1)S(1)} %join.19.refs_0_), channel_id=1, source_target_pairs={{0,4},{4,0},{8,12},{12,8},{16,20},{20,16},{24,28},{28,24},{1,5},{5... | collective-permute-start | bytes 3538952 | tf_op jit(solution)/shard_map/ppermute | solution.py:49
  116.4 18.5 %collective-permute-start.27 = (bf16[4,96,1536]{2,1,0:T(8,128)(2,1)S(1)}, bf16[4,96,1536]{2,1,0:T(8,128)(2,1)S(1)}, u32[]{:S(2)}, u32[]{:S(2)}) collective-permute-start(bf16[4,96,1536]{2,1,0:T(8,128)(2,1)S(1)} %join.19.refs_0_), channel_id=1, source_target_pairs={{0,1},{1,0},{2,3},{3,2},{4,5},{5,4},{6,7},{7,6},{8,9},{9,8},{10,11... | collective-permute-start | bytes 3538952 | tf_op jit(solution)/shard_map/ppermute | solution.py:49
  118.3 16.7 %collective-permute-start.28 = (bf16[4,96,1536]{2,1,0:T(8,128)(2,1)S(1)}, bf16[4,96,1536]{2,1,0:T(8,128)(2,1)S(1)}, u32[]{:S(2)}, u32[]{:S(2)}) collective-permute-start(bf16[4,96,1536]{2,1,0:T(8,128)(2,1)S(1)} %collective-permute-done.26.refs_1_), channel_id=1, source_target_pairs={{0,1},{1,0},{2,3},{3,2},{4,5},{5,4},{6,7},{7,6},{8,9},{9,8},{10,11... | collective-permute-start | bytes 3538952 | tf_op jit(solution)/shard_map/ppermute | solution.py:49
  122.1 8.6 %collective-permute-start.24 = (bf16[128,768]{1,0:T(8,128)(2,1)S(1)}, bf16[128,768]{1,0:T(8,128)(2,1)S(1)}, u32[]{:S(2)}, u32[]{:S(2)}) collective-permute-start(bf16[128,768]{1,0:T(8,128)(2,1)S(1)} %get-tuple-element.440), channel_id=1, source_target_pairs={{0,2},{1,3},{2,0},{3,1},{4,6},{5,7},{6,4},{7,5},{8,10},{9,11},{10,... | collective-permute-start | bytes 589832 | tf_op jit(solution)/shard_map/ppermute | solution.py:49
  126.8 8.1 %collective-permute-start.32 = (bf16[128,768]{1,0:T(8,128)(2,1)S(1)}, bf16[128,768]{1,0:T(8,128)(2,1)S(1)}, u32[]{:S(2)}, u32[]{:S(2)}) collective-permute-start(bf16[128,768]{1,0:T(8,128)(2,1)S(1)} %get-tuple-element.264.own_ref.refs_2_), channel_id=1, source_target_pairs={{0,2},{1,3},{2,0},{3,1},{4,6},{5,7},{6,4},{7,5},{8,10},{9,11},{10,... | collective-permute-start | bytes 589832 | tf_op jit(solution)/shard_map/ppermute | solution.py:49
  140.5 7.9 %collective-permute-start.29 = (bf16[128,768]{1,0:T(8,128)(2,1)S(1)}, bf16[128,768]{1,0:T(8,128)(2,1)S(1)}, u32[]{:S(2)}, u32[]{:S(2)}) collective-permute-start(bf16[128,768]{1,0:T(8,128)(2,1)S(1)} %get-tuple-element.259), channel_id=1, source_target_pairs={{0,2},{1,3},{2,0},{3,1},{4,6},{5,7},{6,4},{7,5},{8,10},{9,11},{10,... | collective-permute-start | bytes 589832 | tf_op jit(solution)/shard_map/ppermute | solution.py:49
  144.0 8.6 %collective-permute-start.35 = (bf16[128,768]{1,0:T(8,128)(2,1)S(1)}, bf16[128,768]{1,0:T(8,128)(2,1)S(1)}, u32[]{:S(2)}, u32[]{:S(2)}) collective-permute-start(bf16[128,768]{1,0:T(8,128)(2,1)S(1)} %get-tuple-element.270.own_ref.refs_6_), channel_id=1, source_target_pairs={{0,2},{1,3},{2,0},{3,1},{4,6},{5,7},{6,4},{7,5},{8,10},{9,11},{10,... | collective-permute-start | bytes 589832 | tf_op jit(solution)/shard_map/ppermute | solution.py:49
  159.5 8.1 %collective-permute-start.37 = (bf16[128,768]{1,0:T(8,128)(2,1)S(1)}, bf16[128,768]{1,0:T(8,128)(2,1)S(1)}, u32[]{:S(2)}, u32[]{:S(2)}) collective-permute-start(bf16[128,768]{1,0:T(8,128)(2,1)S(1)} %get-tuple-element.281), channel_id=1, source_target_pairs={{0,2},{1,3},{2,0},{3,1},{4,6},{5,7},{6,4},{7,5},{8,10},{9,11},{10,... | collective-permute-start | bytes 589832 | tf_op jit(solution)/shard_map/ppermute | solution.py:49
  165.5 29.1 %collective-permute-start.46 = (bf16[4,96,1536]{2,1,0:T(8,128)(2,1)}, bf16[4,96,1536]{2,1,0:T(8,128)(2,1)S(1)}, u32[]{:S(2)}, u32[]{:S(2)}) collective-permute-start(bf16[4,96,1536]{2,1,0:T(8,128)(2,1)} %get-tuple-element.279), channel_id=1, source_target_pairs={{0,4},{4,0},{8,12},{12,8},{16,20},{20,16},{24,28},{28,24},{1,5},{5... | collective-permute-start | bytes 3538952 | tf_op jit(solution)/shard_map/ppermute | solution.py:49
  169.3 8.6 %collective-permute-start.39 = (bf16[128,768]{1,0:T(8,128)(2,1)}, bf16[128,768]{1,0:T(8,128)(2,1)}, u32[]{:S(2)}, u32[]{:S(2)}) collective-permute-start(bf16[128,768]{1,0:T(8,128)(2,1)} %get-tuple-element.284.refs_0_), channel_id=1, source_target_pairs={{0,2},{1,3},{2,0},{3,1},{4,6},{5,7},{6,4},{7,5},{8,10},{9,11},{10,... | collective-permute-start | bytes 589832 | tf_op jit(solution)/shard_map/ppermute | solution.py:49
  180.2 10.9 %collective-permute-start.43 = (bf16[128,768]{1,0:T(8,128)(2,1)}, bf16[128,768]{1,0:T(8,128)(2,1)S(1)}, u32[]{:S(2)}, u32[]{:S(2)}) collective-permute-start(bf16[128,768]{1,0:T(8,128)(2,1)} %get-tuple-element.289.refs_4_.refs_0_), channel_id=1, source_target_pairs={{0,1},{1,0},{2,3},{3,2},{4,5},{5,4},{6,7},{7,6},{8,9},{9,8},{10,11... | collective-permute-start | bytes 589832 | tf_op jit(solution)/shard_map/ppermute | solution.py:49
  183.2 8.0 %collective-permute-start.44 = (bf16[128,768]{1,0:T(8,128)(2,1)}, bf16[128,768]{1,0:T(8,128)(2,1)S(1)}, u32[]{:S(2)}, u32[]{:S(2)}) collective-permute-start(bf16[128,768]{1,0:T(8,128)(2,1)} %collective-permute-done.42.refs_5_.refs_1_), channel_id=1, source_target_pairs={{0,1},{1,0},{2,3},{3,2},{4,5},{5,4},{6,7},{7,6},{8,9},{9,8},{10,11... | collective-permute-start | bytes 589832 | tf_op jit(solution)/shard_map/ppermute | solution.py:49
  193.9 14.9 %collective-permute-start.45 = (bf16[4,112,384]{2,1,0:T(8,128)(2,1)S(1)}, bf16[4,112,384]{2,1,0:T(8,128)(2,1)S(1)}, u32[]{:S(2)}, u32[]{:S(2)}) collective-permute-start(bf16[4,112,384]{2,1,0:T(8,128)(2,1)S(1)} %get-tuple-element.306), channel_id=1, source_target_pairs={{0,4},{4,0},{8,12},{12,8},{16,20},{20,16},{24,28},{28,24},{1,5},{5... | collective-permute-start | bytes 1032200 | tf_op jit(solution)/shard_map/ppermute | solution.py:49
  194.8 24.2 %collective-permute-start.48 = (bf16[2,96,1536]{2,1,0:T(8,128)(2,1)S(1)}, bf16[2,96,1536]{2,1,0:T(8,128)(2,1)S(1)}, u32[]{:S(2)}, u32[]{:S(2)}) collective-permute-start(bf16[2,96,1536]{2,1,0:T(8,128)(2,1)S(1)} %get-tuple-element.310), channel_id=1, source_target_pairs={{0,8},{4,12},{8,0},{12,4},{16,24},{20,28},{24,16},{28,20},{1,9},{5... | collective-permute-start | bytes 1769480 | tf_op jit(solution)/shard_map/ppermute | solution.py:49
  207.3 14.1 %collective-permute-start.49 = (bf16[4,96,512]{2,1,0:T(8,128)(2,1)S(1)}, bf16[4,96,512]{2,1,0:T(8,128)(2,1)S(1)}, u32[]{:S(2)}, u32[]{:S(2)}) collective-permute-start(bf16[4,96,512]{2,1,0:T(8,128)(2,1)S(1)} %get-tuple-element.322), channel_id=1, source_target_pairs={{0,4},{4,0},{8,12},{12,8},{16,20},{20,16},{24,28},{28,24},{1,5},{5... | collective-permute-start | bytes 1179656 | tf_op jit(solution)/shard_map/ppermute | solution.py:49
  208.8 20.9 %collective-permute-start.50 = (bf16[2,112,384]{2,1,0:T(8,128)(2,1)S(1)}, bf16[2,112,384]{2,1,0:T(8,128)(2,1)S(1)}, u32[]{:S(2)}, u32[]{:S(2)}) collective-permute-start(bf16[2,112,384]{2,1,0:T(8,128)(2,1)S(1)} %get-tuple-element.326), channel_id=1, source_target_pairs={{0,8},{4,12},{8,0},{12,4},{16,24},{20,28},{24,16},{28,20},{1,9},{5... | collective-permute-start | bytes 516104 | tf_op jit(solution)/shard_map/ppermute | solution.py:49
  210.3 24.4 %collective-permute-start.55 = (bf16[4,96,640]{2,1,0:T(8,128)(2,1)S(1)}, bf16[4,96,640]{2,1,0:T(8,128)(2,1)S(1)}, u32[]{:S(2)}, u32[]{:S(2)}) collective-permute-start(bf16[4,96,640]{2,1,0:T(8,128)(2,1)S(1)} %get-tuple-element.323), channel_id=1, source_target_pairs={{0,8},{4,12},{8,0},{12,4},{16,24},{20,28},{24,16},{28,20},{1,9},{5... | collective-permute-start | bytes 1474568 | tf_op jit(solution)/shard_map/ppermute | solution.py:49
  218.9 17.3 %collective-permute-start.47 = (bf16[256,768]{1,0:T(8,128)(2,1)S(1)}, bf16[256,768]{1,0:T(8,128)(2,1)S(1)}, u32[]{:S(2)}, u32[]{:S(2)}) collective-permute-start(bf16[256,768]{1,0:T(8,128)(2,1)S(1)} %get-tuple-element.335), channel_id=1, source_target_pairs={{0,1},{1,0},{2,3},{3,2},{4,5},{5,4},{6,7},{7,6},{8,9},{9,8},{10,11... | collective-permute-start | bytes 1179656 | tf_op jit(solution)/shard_map/ppermute | solution.py:49
  219.1 36.0 %collective-permute-start.70 = (bf16[1,96,1536]{2,1,0:T(8,128)(2,1)S(1)}, bf16[1,96,1536]{2,1,0:T(8,128)(2,1)S(1)}, u32[]{:S(2)}, u32[]{:S(2)}) collective-permute-start(bf16[1,96,1536]{2,1,0:T(8,128)(2,1)S(1)} %get-tuple-element.340), channel_id=1, source_target_pairs={{0,16},{4,20},{8,24},{12,28},{16,0},{20,4},{24,8},{28,12},{1,17},{... | collective-permute-start | bytes 884744 | tf_op jit(solution)/shard_map/ppermute | solution.py:49
  221.5 15.8 %collective-permute-start.58 = (bf16[2,96,512]{2,1,0:T(8,128)(2,1)S(1)}, bf16[2,96,512]{2,1,0:T(8,128)(2,1)S(1)}, u32[]{:S(2)}, u32[]{:S(2)}) collective-permute-start(bf16[2,96,512]{2,1,0:T(8,128)(2,1)S(1)} %get-tuple-element.351), channel_id=1, source_target_pairs={{0,8},{4,12},{8,0},{12,4},{16,24},{20,28},{24,16},{28,20},{1,9},{5... | collective-permute-start | bytes 589832 | tf_op jit(solution)/shard_map/ppermute | solution.py:49
  233.8 12.1 %collective-permute-start.57 = (bf16[4,96,512]{2,1,0:T(8,128)(2,1)S(1)}, bf16[4,96,512]{2,1,0:T(8,128)(2,1)S(1)}, u32[]{:S(2)}, u32[]{:S(2)}) collective-permute-start(bf16[4,96,512]{2,1,0:T(8,128)(2,1)S(1)} %get-tuple-element.368), channel_id=1, source_target_pairs={{0,4},{4,0},{8,12},{12,8},{16,20},{20,16},{24,28},{28,24},{1,5},{5... | collective-permute-start | bytes 1179656 | tf_op jit(solution)/shard_map/ppermute | solution.py:49
  234.7 16.9 %collective-permute-start.54 = (bf16[4,96,640]{2,1,0:T(8,128)(2,1)S(1)}, bf16[4,96,640]{2,1,0:T(8,128)(2,1)S(1)}, u32[]{:S(2)}, u32[]{:S(2)}) collective-permute-start(bf16[4,96,640]{2,1,0:T(8,128)(2,1)S(1)} %get-tuple-element.369), channel_id=1, source_target_pairs={{0,8},{4,12},{8,0},{12,4},{16,24},{20,28},{24,16},{28,20},{1,9},{5... | collective-permute-start | bytes 1474568 | tf_op jit(solution)/shard_map/ppermute | solution.py:49
  237.2 12.9 %collective-permute-start.56 = (bf16[2,96,640]{2,1,0:T(8,128)(2,1)S(1)}, bf16[2,96,640]{2,1,0:T(8,128)(2,1)S(1)}, u32[]{:S(2)}, u32[]{:S(2)}) collective-permute-start(bf16[2,96,640]{2,1,0:T(8,128)(2,1)S(1)} %get-tuple-element.374), channel_id=1, source_target_pairs={{0,4},{4,0},{8,12},{12,8},{16,20},{20,16},{24,28},{28,24},{1,5},{5... | collective-permute-start | bytes 737288 | tf_op jit(solution)/shard_map/ppermute | solution.py:49
  245.9 8.5 %collective-permute-start.66 = (bf16[1,112,384]{2,1,0:T(8,128)(2,1)S(1)}, bf16[1,112,384]{2,1,0:T(8,128)(2,1)S(1)}, u32[]{:S(2)}, u32[]{:S(2)}) collective-permute-start(bf16[1,112,384]{2,1,0:T(8,128)(2,1)S(1)} %get-tuple-element.355), channel_id=1, source_target_pairs={{0,16},{4,20},{8,24},{12,28},{16,0},{20,4},{24,8},{28,12},{1,17},{... | collective-permute-start | bytes 258056 | tf_op jit(solution)/shard_map/ppermute | solution.py:49
  247.5 9.7 %collective-permute-start.64 = (bf16[1,96,512]{2,1,0:T(8,128)(2,1)S(1)}, bf16[1,96,512]{2,1,0:T(8,128)(2,1)}, u32[]{:S(2)}, u32[]{:S(2)}) collective-permute-start(bf16[1,96,512]{2,1,0:T(8,128)(2,1)S(1)} %get-tuple-element.379), channel_id=1, source_target_pairs={{0,16},{4,20},{8,24},{12,28},{16,0},{20,4},{24,8},{28,12},{1,17},{... | collective-permute-start | bytes 294920 | tf_op jit(solution)/shard_map/ppermute | solution.py:49
  250.1 16.9 %collective-permute-start.60 = (bf16[2,96,512]{2,1,0:T(8,128)(2,1)S(1)}, bf16[2,96,512]{2,1,0:T(8,128)(2,1)S(1)}, u32[]{:S(2)}, u32[]{:S(2)}) collective-permute-start(bf16[2,96,512]{2,1,0:T(8,128)(2,1)S(1)} %get-tuple-element.382), channel_id=1, source_target_pairs={{0,8},{4,12},{8,0},{12,4},{16,24},{20,28},{24,16},{28,20},{1,9},{5... | collective-permute-start | bytes 589832 | tf_op jit(solution)/shard_map/ppermute | solution.py:49
  251.6 12.4 %collective-permute-start.63 = (bf16[1,96,640]{2,1,0:T(8,128)(2,1)S(1)}, bf16[1,96,640]{2,1,0:T(8,128)(2,1)}, u32[]{:S(2)}, u32[]{:S(2)}) collective-permute-start(bf16[1,96,640]{2,1,0:T(8,128)(2,1)S(1)} %get-tuple-element.385), channel_id=1, source_target_pairs={{0,16},{4,20},{8,24},{12,28},{16,0},{20,4},{24,8},{28,12},{1,17},{... | collective-permute-start | bytes 368648 | tf_op jit(solution)/shard_map/ppermute | solution.py:49
  254.4 12.8 %collective-permute-start.53 = (bf16[128,768]{1,0:T(8,128)(2,1)}, bf16[128,768]{1,0:T(8,128)(2,1)}, u32[]{:S(2)}, u32[]{:S(2)}) collective-permute-start(bf16[128,768]{1,0:T(8,128)(2,1)} %slice.294), channel_id=1, source_target_pairs={{0,2},{1,3},{2,0},{3,1},{4,6},{5,7},{6,4},{7,5},{8,10},{9,11},{10,... | collective-permute-start | bytes 589832 | tf_op jit(solution)/shard_map/ppermute | solution.py:49
  257.2 15.6 %collective-permute-start.59 = (bf16[2,96,640]{2,1,0:T(8,128)(2,1)S(1)}, bf16[2,96,640]{2,1,0:T(8,128)(2,1)S(1)}, u32[]{:S(2)}, u32[]{:S(2)}) collective-permute-start(bf16[2,96,640]{2,1,0:T(8,128)(2,1)S(1)} %get-tuple-element.389), channel_id=1, source_target_pairs={{0,4},{4,0},{8,12},{12,8},{16,20},{20,16},{24,28},{28,24},{1,5},{5... | collective-permute-start | bytes 737288 | tf_op jit(solution)/shard_map/ppermute | solution.py:49
  (75 other events, 627.2 us)

commit v2 on v1

--- a/solution.py
+++ b/solution.py
@@ -143,7 +143,7 @@
         in_specs=[VM] * 2,
         out_shape=(struct(half, f32), struct(half, bf16)),
         compiler_params=PARAMS,
-        cost_estimate=cost(0.48),
+        cost_estimate=cost(0.432),
         name="fold",
     )(*pin(first, second))
 
@@ -662,7 +662,7 @@
         in_specs=[VM] * (6 + len(saved)),
         out_shape=outs + (struct((own, features), f32), struct((own, features), bf16)),
         compiler_params=PARAMS,
-        cost_estimate=cost(1.8),
+        cost_estimate=cost(1.17),
         name=name,
     )(*pin(*parts, *weights, *saved))
 
@@ -747,7 +747,7 @@
 
 
 def norm_call(kernel, name, outs, *args):
-    return pl.pallas_call(kernel, in_specs=[VM] * len(args), out_shape=outs, compiler_params=PARAMS, cost_estimate=cost(0.6), name=name)(*pin(*args))
+    return pl.pallas_call(kernel, in_specs=[VM] * len(args), out_shape=outs, compiler_params=PARAMS, cost_estimate=cost(0.75), name=name)(*pin(*args))
 
 
 def local(

time: 287 us -> 286 us (level)
  no operation moved by 1% of the time
where the time goes in v2:
time: 286 us; the launch traced here: 282 us
  waiting for transfers between devices  93.3 us (33%)
  Pallas kernels  89.5 us (31%)
  starting transfers between devices  63.9 us (22%)
  local copies, waits for them, and re-layouts  22.2 us (8%)
  other arithmetic  10.8 us (4%)
    ppermute x71, waiting for transfers between devices, swap(): lax.ppermute(value, axis, [(place, place ^ mask) for place in range(count)])  93.3 us
    ppermute x71, starting transfers between devices, swap(): lax.ppermute(value, axis, [(place, place ^ mask) for place in range(count)])  63.9 us
    pallas_call x4, Pallas kernels, attend(): pl.pallas_call(functools.partial(attend_kernel, batch, heads, final is no...  32.4 us
    pallas_call x4, Pallas kernels, attend_back(): pl.pallas_call(functools.partial(attend_back_kernel, heads, half), in_spe...  31.2 us
    unnamed x109, local copies, waits for them, and re-layouts  9.26 us
    pallas_call x2, Pallas kernels, attn_weights(): pl.pallas_call(functools.partial(attn_weights_kernel, batches, split), in...  8.15 us
    pallas_call x4, Pallas kernels, ff_call(): pl.pallas_call(kernel, in_specs=[VM] * (6 + len(saved)), out_shape=outs +...  6.53 us
  transfers between devices with their start and end apart: 71, of which 31 were waited for; matrix products, arithmetic and copies ran while one was open for 7% of the time, Pallas kernels for 30%

profile of v2, /device:TPU:0, one launch (start us, length us, event | category | flops | bytes accessed | tf_op | source)
XLA Modules:
  0.0 282.3 jit_solution(14401480774091775261)
XLA Ops:
  1.9 4.1 %collective-permute-start.6 = (bf16[1,96,640]{2,1,0:T(8,128)(2,1)S(1)}, bf16[1,96,640]{2,1,0:T(8,128)(2,1)S(1)}, u32[]{:S(2)}, u32[]{:S(2)}) collective-permute-start(bf16[1,96,640]{2,1,0:T(8,128)(2,1)S(1)} %fusion.11.first_ref), channel_id=1, source_target_pairs={{0,16},{4,20},{8,24},{12,28},{16,0},{20,4},{24,8},{28,12},{1,17},{... | collective-permute-start | bytes 368648 | tf_op jit(solution)/shard_map/ppermute | solution.py:49
  8.3 1.9 collective-permute-start.3
  14.7 1.9 collective-permute-start.2
  18.0 1.7 collective-permute-done.2
  26.8 2.7 collective-permute-start.8
  34.9 3.2 %collective-permute-done.8.second_ref = bf16[1,96,1152]{2,1,0:T(8,128)(2,1)S(1)} collective-permute-done((bf16[1,96,1152]{2,1,0:T(8,128)(2,1)S(1)}, bf16[1,96,1152]{2,1,0:T(8,128)(2,1)S(1)}, u32[]{:S(2)}, u32[]{:S(2)}) %collective-permute-start.8) | collective-permute-done | bytes 221216 | tf_op jit(solution)/shard_map/ppermute | solution.py:49
  38.2 1.7 collective-permute-done.14.refs_1_
  44.3 3.1 %collective-permute-done.18.second_ref = bf16[1,112,384]{2,1,0:T(8,128)(2,1)S(1)} collective-permute-done((bf16[1,112,384]{2,1,0:T(8,128)(2,1)S(1)}, bf16[1,112,384]{2,1,0:T(8,128)(2,1)S(1)}, u32[]{:S(2)}, u32[]{:S(2)}) %collective-permute-start.18) | collective-permute-done | bytes 86048 | tf_op jit(solution)/shard_map/ppermute | solution.py:49
  47.9 7.6 %collective-permute-done.13.refs_7_ = bf16[4,96,512]{2,1,0:T(8,128)(2,1)} collective-permute-done((bf16[4,96,512]{2,1,0:T(8,128)(2,1)}, bf16[4,96,512]{2,1,0:T(8,128)(2,1)}, u32[]{:S(2)}, u32[]{:S(2)}) %collective-permute-start.13) | collective-permute-done | bytes 393248 | tf_op jit(solution)/shard_map/ppermute | solution.py:49
  55.4 2.6 collective-permute-start.19
  59.4 8.2 %attend.4 = (bf16[3,512,128]{2,1,0:T(8,128)(2,1)}, bf16[3,512,128]{2,1,0:T(8,128)(2,1)}, bf16[3,512,64]{2,1,0:T(8,128)(2,1)}, bf16[3,512,512]{2,1,0:T(8,128)(2,1...) custom-call(s32[1]{0:T(128)} %bitcast.page_ref, bf16[2,2,128,768]{3,2,1,0:T(8,128)(2,1)S(1)} %pad_maximum_fusion.refs_0_, ...), custom_call_target="tpu_custom_call" | custom-call | flops 4409999872 | bytes 1890000 | tf_op jit(solution)/shard_map/attend/pallas_call | solution.py:375
  67.6 2.2 collective-permute-done.11.second_ref
  70.0 1.7 collective-permute-start.21
  71.7 6.8 %collective-permute-done.17.second_ref = bf16[1,96,1536]{2,1,0:T(8,128)(2,1)S(1)} collective-permute-done((bf16[1,96,1536]{2,1,0:T(8,128)(2,1)S(1)}, bf16[1,96,1536]{2,1,0:T(8,128)(2,1)S(1)}, u32[]{:S(2)}, u32[]{:S(2)}) %collective-permute-start.17) | collective-permute-done | bytes 294944 | tf_op jit(solution)/shard_map/ppermute | solution.py:49
  78.6 2.0 collective-permute-start.22
  80.6 7.8 %attend.5 = (bf16[3,512,128]{2,1,0:T(8,128)(2,1)}, bf16[3,512,128]{2,1,0:T(8,128)(2,1)}, bf16[3,512,64]{2,1,0:T(8,128)(2,1)}, bf16[3,512,512]{2,1,0:T(8,128)(2,1...) custom-call(s32[1]{0:T(128)} %bitcast.page_ref, bf16[2,2,128,768]{3,2,1,0:T(8,128)(2,1)S(1)} %pad_maximum_fusion.refs_0_, ...), custom_call_target="tpu_custom_call" | custom-call | flops 4409999872 | bytes 1890000 | tf_op jit(solution)/shard_map/attend/pallas_call | solution.py:375
  88.5 6.4 %collective-permute-done.20.second_ref = bf16[2,96,1536]{2,1,0:T(8,128)(2,1)S(1)} collective-permute-done((bf16[2,96,1536]{2,1,0:T(8,128)(2,1)S(1)}, bf16[2,96,1536]{2,1,0:T(8,128)(2,1)S(1)}, u32[]{:S(2)}, u32[]{:S(2)}) %collective-permute-start.20) | collective-permute-done | bytes 589856 | tf_op jit(solution)/shard_map/ppermute | solution.py:49
  96.4 3.5 %collective-permute-done.22.refs_7_ = bf16[4,112,384]{2,1,0:T(8,128)(2,1)S(1)} collective-permute-done((bf16[4,112,384]{2,1,0:T(8,128)(2,1)S(1)}, bf16[4,112,384]{2,1,0:T(8,128)(2,1)S(1)}, u32[]{:S(2)}, u32[]{:S(2)}) %collective-permute-start.22) | collective-permute-done | bytes 344096 | tf_op jit(solution)/shard_map/ppermute | solution.py:49
  99.9 8.4 %attend.6 = (bf16[3,512,128]{2,1,0:T(8,128)(2,1)}, bf16[3,512,128]{2,1,0:T(8,128)(2,1)}, bf16[3,512,64]{2,1,0:T(8,128)(2,1)}, bf16[3,512,512]{2,1,0:T(8,128)(2,1...) custom-call(s32[1]{0:T(128)} %bitcast.page_ref, ...), custom_call_target="tpu_custom_call" | custom-call | flops 4409999872 | bytes 1890000 | tf_op jit(solution)/shard_map/attend/pallas_call | solution.py:375
  108.3 8.0 %attend.7 = (bf16[3,512,128]{2,1,0:T(8,128)(2,1)}, bf16[3,512,128]{2,1,0:T(8,128)(2,1)}, bf16[3,512,64]{2,1,0:T(8,128)(2,1)}, bf16[3,512,512]{2,1,0:T(8,128)(2,1...) custom-call(s32[1]{0:T(128)} %bitcast.page_ref, ...), custom_call_target="tpu_custom_call" | custom-call | flops 4409999872 | bytes 1890000 | tf_op jit(solution)/shard_map/attend/pallas_call | solution.py:375
  119.7 2.4 collective-permute-done.23
  123.0 3.5 %collective-permute-done.31.far_ref = bf16[128,768]{1,0:T(8,128)(2,1)S(1)} collective-permute-done((bf16[128,768]{1,0:T(8,128)(2,1)S(1)}, bf16[128,768]{1,0:T(8,128)(2,1)S(1)}, u32[]{:S(2)}, u32[]{:S(2)}) %collective-permute-start.31) | collective-permute-done | bytes 196640 | tf_op jit(solution)/shard_map/ppermute | solution.py:49
  127.6 3.1 %collective-permute-done.24.far_ref = bf16[128,768]{1,0:T(8,128)(2,1)S(1)} collective-permute-done((bf16[128,768]{1,0:T(8,128)(2,1)S(1)}, bf16[128,768]{1,0:T(8,128)(2,1)S(1)}, u32[]{:S(2)}, u32[]{:S(2)}) %collective-permute-start.24) | collective-permute-done | bytes 196640 | tf_op jit(solution)/shard_map/ppermute | solution.py:49
  131.8 3.1 %collective-permute-done.32.side_ref.refs_3_ = bf16[128,768]{1,0:T(8,128)(2,1)S(1)} collective-permute-done((bf16[128,768]{1,0:T(8,128)(2,1)S(1)}, bf16[128,768]{1,0:T(8,128)(2,1)S(1)}, u32[]{:S(2)}, u32[]{:S(2)}) %collective-permute-start.32) | collective-permute-done | bytes 196640 | tf_op jit(solution)/shard_map/ppermute | solution.py:49
  134.9 1.7 forward.3
  138.8 1.7 forward.2
  141.3 1.7 collective-permute-done.33.far_ref
  144.7 3.7 %collective-permute-done.29.far_ref = bf16[128,768]{1,0:T(8,128)(2,1)S(1)} collective-permute-done((bf16[128,768]{1,0:T(8,128)(2,1)S(1)}, bf16[128,768]{1,0:T(8,128)(2,1)S(1)}, u32[]{:S(2)}, u32[]{:S(2)}) %collective-permute-start.29) | collective-permute-done | bytes 196640 | tf_op jit(solution)/shard_map/ppermute | solution.py:49
  149.6 3.0 %collective-permute-done.35.side_ref.refs_7_ = bf16[128,768]{1,0:T(8,128)(2,1)S(1)} collective-permute-done((bf16[128,768]{1,0:T(8,128)(2,1)S(1)}, bf16[128,768]{1,0:T(8,128)(2,1)S(1)}, u32[]{:S(2)}, u32[]{:S(2)}) %collective-permute-start.35) | collective-permute-done | bytes 196640 | tf_op jit(solution)/shard_map/ppermute | solution.py:49
  156.8 2.6 ff_weights.1
  160.3 3.7 %collective-permute-done.36.second_ref = bf16[8,96,1536]{2,1,0:T(8,128)(2,1)S(1)} collective-permute-done((bf16[8,96,1536]{2,1,0:T(8,128)(2,1)S(1)}, bf16[8,96,1536]{2,1,0:T(8,128)(2,1)S(1)}, u32[]{:S(2)}, u32[]{:S(2)}) %collective-permute-start.36) | collective-permute-done | bytes 2359328 | tf_op jit(solution)/shard_map/ppermute | solution.py:49
  170.6 4.0 %collective-permute-done.38.far_ref = bf16[128,768]{1,0:T(8,128)(2,1)S(1)} collective-permute-done((bf16[128,768]{1,0:T(8,128)(2,1)S(1)}, bf16[128,768]{1,0:T(8,128)(2,1)S(1)}, u32[]{:S(2)}, u32[]{:S(2)}) %collective-permute-start.38) | collective-permute-done | bytes 196640 | tf_op jit(solution)/shard_map/ppermute | solution.py:49
  178.4 1.8 pad_maximum_fusion.3
  180.2 2.9 %collective-permute-done.42.refs_5_.refs_1_ = bf16[128,768]{1,0:T(8,128)(2,1)} collective-permute-done((bf16[128,768]{1,0:T(8,128)(2,1)}, bf16[128,768]{1,0:T(8,128)(2,1)}, u32[]{:S(2)}, u32[]{:S(2)}) %collective-permute-start.42) | collective-permute-done | bytes 196640 | tf_op jit(solution)/shard_map/ppermute | solution.py:49
  183.3 7.9 %attend_back.4 = (bf16[512,960]{1,0:T(8,128)(2,1)S(1)}, f32[8,96,192]{2,1,0:T(8,128)S(1)}, f32[512,768]{1,0:T(8,128)S(1)}) custom-call(s32[1]{0:T(128)} %bitcast.page_ref, bf16[128,768]{1,0:T(8,128)(2,1)} %get-tuple-element.284.refs_0_, bf16[128,768]{1,0:T(8,128)(2,1)} %collective-permute-done.39.refs_1_, bf16[128,768]{1,0:T(8,128)(2,1)} %collective-permute-done.40.refs_2_, ...), custom_call_target="tpu_custom_call" | custom-call | flops 4200000000 | bytes 1800000 | tf_op jit(solution)/shard_map/attend_back/pallas_call | solution.py:489
  191.2 2.6 out_weights.1
  195.4 7.8 %attend_back.5 = (bf16[512,960]{1,0:T(8,128)(2,1)S(1)}, f32[8,96,192]{2,1,0:T(8,128)S(1)}, f32[512,768]{1,0:T(8,128)S(1)}) custom-call(s32[1]{0:T(128)} %bitcast.page_ref, bf16[128,768]{1,0:T(8,128)(2,1)} %get-tuple-element.289.refs_4_.refs_0_, bf16[128,768]{1,0:T(8,128)(2,1)} %collective-permute-done.42.refs_5_.refs_1_, ...), custom_call_target="tpu_custom_call" | custom-call | flops 4200000000 | bytes 1800000 | tf_op jit(solution)/shard_map/attend_back/pallas_call | solution.py:489
  203.2 4.1 %attn_weights.2 = (f32[4,96,640]{2,1,0:T(8,128)S(1)}, bf16[4,96,640]{2,1,0:T(8,128)(2,1)S(1)}, f32[4,96,512]{2,1,0:T(8,128)S(1)}, bf16[4,96,512]{2,1,0:T(8,128)(2,1)S(1)}) custom-call(s32[1]{0:T(128)} %bitcast.page_ref, bf16[2,2,128,768]{3,2,1,0:T(8,128)(2,1)S(1)} %copy-done.3, bf16[2,2,128,768]{3,2,1,0:T(8,128)(2,1)S(1)} %copy-done.11, ...), custom_call_target="tpu_custom_call" | custom-call | flops 2184000000 | bytes 936000 | tf_op jit(solution)/shard_map/attn_weights/pallas_call | solution.py:557
  210.9 8.0 %attend_back.6 = (bf16[512,960]{1,0:T(8,128)(2,1)S(1)}, f32[8,96,192]{2,1,0:T(8,128)S(1)}, f32[256,768]{1,0:T(8,128)S(1)}, bf16[256,768]{1,0:T(8,128)(2,1)S(1)}) custom-call(s32[1]{0:T(128)} %bitcast.page_ref, bf16[128,768]{1,0:T(8,128)(2,1)} %get-tuple-element.284.refs_0_, bf16[128,768]{1,0:T(8,128)(2,1)} %collective-permute-done.39.refs_1_, ...), custom_call_target="tpu_custom_call" | custom-call | flops 4200000000 | bytes 1800000 | tf_op jit(solution)/shard_map/attend_back/pallas_call | solution.py:489
  219.1 2.3 collective-permute-start.70
  222.1 7.6 %attend_back.7 = (bf16[512,960]{1,0:T(8,128)(2,1)S(1)}, f32[8,96,192]{2,1,0:T(8,128)S(1)}, f32[256,768]{1,0:T(8,128)S(1)}, bf16[256,768]{1,0:T(8,128)(2,1)S(1)}) custom-call(s32[1]{0:T(128)} %bitcast.page_ref, bf16[128,768]{1,0:T(8,128)(2,1)} %get-tuple-element.289.refs_4_.refs_0_, bf16[128,768]{1,0:T(8,128)(2,1)} %collective-permute-done.42.refs_5_.refs_1_, ...), custom_call_target="tpu_custom_call" | custom-call | flops 4200000000 | bytes 1800000 | tf_op jit(solution)/shard_map/attend_back/pallas_call | solution.py:489
  229.8 4.1 %attn_weights.3 = (f32[4,96,640]{2,1,0:T(8,128)S(1)}, bf16[4,96,640]{2,1,0:T(8,128)(2,1)S(1)}, f32[4,96,512]{2,1,0:T(8,128)S(1)}, bf16[4,96,512]{2,1,0:T(8,128)(2,1)S(1)}) custom-call(s32[1]{0:T(128)} %bitcast.page_ref, bf16[2,2,128,768]{3,2,1,0:T(8,128)(2,1)S(1)} %copy-done.3, bf16[2,2,128,768]{3,2,1,0:T(8,128)(2,1)S(1)} %copy-done.11, ...), custom_call_target="tpu_custom_call" | custom-call | flops 2184000000 | bytes 936000 | tf_op jit(solution)/shard_map/attn_weights/pallas_call | solution.py:557
  238.5 4.1 %collective-permute-done.51 = bf16[128,768]{1,0:T(8,128)(2,1)S(1)} collective-permute-done((bf16[128,768]{1,0:T(8,128)(2,1)S(1)}, bf16[128,768]{1,0:T(8,128)(2,1)S(1)}, u32[]{:S(2)}, u32[]{:S(2)}) %collective-permute-start.51) | collective-permute-done | bytes 196640 | tf_op jit(solution)/shard_map/ppermute | solution.py:49
  242.8 3.1 %collective-permute-done.57.second_ref = bf16[4,96,512]{2,1,0:T(8,128)(2,1)S(1)} collective-permute-done((bf16[4,96,512]{2,1,0:T(8,128)(2,1)S(1)}, bf16[4,96,512]{2,1,0:T(8,128)(2,1)S(1)}, u32[]{:S(2)}, u32[]{:S(2)}) %collective-permute-start.57) | collective-permute-done | bytes 393248 | tf_op jit(solution)/shard_map/ppermute | solution.py:49
  245.9 1.6 collective-permute-start.66
  252.5 1.8 collective-permute-done.66
  269.1 3.6 %collective-permute-done.62 = bf16[1,96,512]{2,1,0:T(8,128)(2,1)S(1)} collective-permute-done((bf16[1,96,512]{2,1,0:T(8,128)(2,1)S(1)}, bf16[1,96,512]{2,1,0:T(8,128)(2,1)S(1)}, u32[]{:S(2)}, u32[]{:S(2)}) %collective-permute-start.62) | collective-permute-done | bytes 98336 | tf_op jit(solution)/shard_map/ppermute | solution.py:49
  273.0 6.0 %collective-permute-done.61 = bf16[1,96,640]{2,1,0:T(8,128)(2,1)S(1)} collective-permute-done((bf16[1,96,640]{2,1,0:T(8,128)(2,1)S(1)}, bf16[1,96,640]{2,1,0:T(8,128)(2,1)S(1)}, u32[]{:S(2)}, u32[]{:S(2)}) %collective-permute-start.61) | collective-permute-done | bytes 122912 | tf_op jit(solution)/shard_map/ppermute | solution.py:49
  (348 shorter events, 90.7 us)
Async XLA Ops:
  1.9 12.7 %collective-permute-start.6 = (bf16[1,96,640]{2,1,0:T(8,128)(2,1)S(1)}, bf16[1,96,640]{2,1,0:T(8,128)(2,1)S(1)}, u32[]{:S(2)}, u32[]{:S(2)}) collective-permute-start(bf16[1,96,640]{2,1,0:T(8,128)(2,1)S(1)} %fusion.11.first_ref), channel_id=1, source_target_pairs={{0,16},{4,20},{8,24},{12,28},{16,0},{20,4},{24,8},{28,12},{1,17},{... | collective-permute-start | bytes 368648 | tf_op jit(solution)/shard_map/ppermute | solution.py:49
  8.2 8.7 %collective-permute-start.7 = (bf16[1,96,512]{2,1,0:T(8,128)(2,1)S(1)}, bf16[1,96,512]{2,1,0:T(8,128)(2,1)S(1)}, u32[]{:S(2)}, u32[]{:S(2)}) collective-permute-start(bf16[1,96,512]{2,1,0:T(8,128)(2,1)S(1)} %fusion.14.first_ref), channel_id=1, source_target_pairs={{0,16},{4,20},{8,24},{12,28},{16,0},{20,4},{24,8},{28,12},{1,17},{... | collective-permute-start | bytes 294920 | tf_op jit(solution)/shard_map/ppermute | solution.py:49
  8.3 8.3 %collective-permute-start.3 = (bf16[2,2,24]{2,1,0:T(2,128)(2,1)S(1)}, bf16[2,2,24]{2,1,0:T(2,128)(2,1)S(1)}, u32[]{:S(2)}, u32[]{:S(2)}) collective-permute-start(bf16[2,2,24]{2,1,0:T(2,128)(2,1)S(1)} %pad_maximum_fusion.10), channel_id=1, source_target_pairs={{0,2},{1,3},{2,0},{3,1},{4,6},{5,7},{6,4},{7,5},{8,10},{9,11},{10,... | collective-permute-start | bytes 584 | tf_op jit(solution)/shard_map/ppermute | solution.py:49
  10.2 15.3 %collective-permute-start = (bf16[5,96,192]{2,1,0:T(8,128)(2,1)S(1)}, bf16[5,96,192]{2,1,0:T(8,128)(2,1)}, u32[]{:S(2)}, u32[]{:S(2)}) collective-permute-start(bf16[5,96,192]{2,1,0:T(8,128)(2,1)S(1)} %dynamic-slice_bitcast_fusion), channel_id=1, source_target_pairs={{0,2},{1,3},{2,0},{3,1},{4,6},{5,7},{6,4},{7,5},{8,10},{9,11},{10,... | collective-permute-start | bytes 552968 | tf_op jit(solution)/shard_map/ppermute | solution.py:49
  16.6 8.8 %collective-permute-start.1 = (bf16[3,3,16,128]{3,2,1,0:T(8,128)(2,1)}, bf16[3,3,16,128]{3,2,1,0:T(8,128)(2,1)S(1)}, u32[]{:S(2)}, u32[]{:S(2)}) collective-permute-start(bf16[3,3,16,128]{3,2,1,0:T(8,128)(2,1)} %dynamic-slice_bitcast_fusion.6), channel_id=1, source_target_pairs={{0,2},{1,3},{2,0},{3,1},{4,6},{5,7},{6,4},{7,5},{8,10},{9,11},{10,... | collective-permute-start | bytes 110600 | tf_op jit(solution)/shard_map/ppermute | solution.py:49
  20.6 19.4 %collective-permute-start.14 = (bf16[2,2,128,768]{3,2,1,0:T(8,128)(2,1)}, bf16[2,2,128,768]{3,2,1,0:T(8,128)(2,1)S(1)}, u32[]{:S(2)}, u32[]{:S(2)}) collective-permute-start(bf16[2,2,128,768]{3,2,1,0:T(8,128)(2,1)} %pad_maximum_fusion.1), channel_id=1, source_target_pairs={{0,2},{1,3},{2,0},{3,1},{4,6},{5,7},{6,4},{7,5},{8,10},{9,11},{10,... | collective-permute-start | bytes 2359304 | tf_op jit(solution)/shard_map/ppermute | solution.py:49
  22.3 8.5 %collective-permute-start.10 = (bf16[2,96,640]{2,1,0:T(8,128)(2,1)S(1)}, bf16[2,96,640]{2,1,0:T(8,128)(2,1)S(1)}, u32[]{:S(2)}, u32[]{:S(2)}) collective-permute-start(bf16[2,96,640]{2,1,0:T(8,128)(2,1)S(1)} %join.10.first_ref), channel_id=1, source_target_pairs={{0,4},{4,0},{8,12},{12,8},{16,20},{20,16},{24,28},{28,24},{1,5},{5... | collective-permute-start | bytes 737288 | tf_op jit(solution)/shard_map/ppermute | solution.py:49
  23.8 8.7 %collective-permute-start.9 = (bf16[2,96,512]{2,1,0:T(8,128)(2,1)S(1)}, bf16[2,96,512]{2,1,0:T(8,128)(2,1)S(1)}, u32[]{:S(2)}, u32[]{:S(2)}) collective-permute-start(bf16[2,96,512]{2,1,0:T(8,128)(2,1)S(1)} %join.11.first_ref), channel_id=1, source_target_pairs={{0,8},{4,12},{8,0},{12,4},{16,24},{20,28},{24,16},{28,20},{1,9},{5... | collective-permute-start | bytes 589832 | tf_op jit(solution)/shard_map/ppermute | solution.py:49
  26.8 11.4 %collective-permute-start.8 = (bf16[1,96,1152]{2,1,0:T(8,128)(2,1)S(1)}, bf16[1,96,1152]{2,1,0:T(8,128)(2,1)S(1)}, u32[]{:S(2)}, u32[]{:S(2)}) collective-permute-start(bf16[1,96,1152]{2,1,0:T(8,128)(2,1)S(1)} %bitcast.154), channel_id=1, source_target_pairs={{0,16},{4,20},{8,24},{12,28},{16,0},{20,4},{24,8},{28,12},{1,17},{... | collective-permute-start | bytes 663560 | tf_op jit(solution)/shard_map/ppermute | solution.py:49
  30.7 27.7 %collective-permute-start.15 = (bf16[2,2,128,768]{3,2,1,0:T(8,128)(2,1)S(1)}, bf16[2,2,128,768]{3,2,1,0:T(8,128)(2,1)}, u32[]{:S(2)}, u32[]{:S(2)}) collective-permute-start(bf16[2,2,128,768]{3,2,1,0:T(8,128)(2,1)S(1)} %pad_maximum_fusion.refs_0_), channel_id=1, source_target_pairs={{0,1},{1,0},{2,3},{3,2},{4,5},{5,4},{6,7},{7,6},{8,9},{9,8},{10,11... | collective-permute-start | bytes 2359304 | tf_op jit(solution)/shard_map/ppermute | solution.py:49
  39.9 18.4 %collective-permute-start.16 = (bf16[2,2,128,768]{3,2,1,0:T(8,128)(2,1)S(1)}, bf16[2,2,128,768]{3,2,1,0:T(8,128)(2,1)}, u32[]{:S(2)}, u32[]{:S(2)}) collective-permute-start(bf16[2,2,128,768]{3,2,1,0:T(8,128)(2,1)S(1)} %collective-permute-done.14.refs_1_), channel_id=1, source_target_pairs={{0,1},{1,0},{2,3},{3,2},{4,5},{5,4},{6,7},{7,6},{8,9},{9,8},{10,11... | collective-permute-start | bytes 2359304 | tf_op jit(solution)/shard_map/ppermute | solution.py:49
  40.0 18.0 %collective-permute-start.12 = (bf16[4,96,640]{2,1,0:T(8,128)(2,1)S(1)}, bf16[4,96,640]{2,1,0:T(8,128)(2,1)}, u32[]{:S(2)}, u32[]{:S(2)}) collective-permute-start(bf16[4,96,640]{2,1,0:T(8,128)(2,1)S(1)} %join.12.refs_4_), channel_id=1, source_target_pairs={{0,8},{4,12},{8,0},{12,4},{16,24},{20,28},{24,16},{28,20},{1,9},{5... | collective-permute-start | bytes 1474568 | tf_op jit(solution)/shard_map/ppermute | solution.py:49
  43.7 11.7 %collective-permute-start.13 = (bf16[4,96,512]{2,1,0:T(8,128)(2,1)}, bf16[4,96,512]{2,1,0:T(8,128)(2,1)}, u32[]{:S(2)}, u32[]{:S(2)}) collective-permute-start(bf16[4,96,512]{2,1,0:T(8,128)(2,1)} %copy-done.12), channel_id=1, source_target_pairs={{0,4},{4,0},{8,12},{12,8},{16,20},{20,16},{24,28},{28,24},{1,5},{5... | collective-permute-start | bytes 1179656 | tf_op jit(solution)/shard_map/ppermute | solution.py:49
  47.4 22.5 %collective-permute-start.11 = (bf16[2,96,1152]{2,1,0:T(8,128)(2,1)S(1)}, bf16[2,96,1152]{2,1,0:T(8,128)(2,1)S(1)}, u32[]{:S(2)}, u32[]{:S(2)}) collective-permute-start(bf16[2,96,1152]{2,1,0:T(8,128)(2,1)S(1)} %join.14.first_ref), channel_id=1, source_target_pairs={{0,8},{4,12},{8,0},{12,4},{16,24},{20,28},{24,16},{28,20},{1,9},{5... | collective-permute-start | bytes 1327112 | tf_op jit(solution)/shard_map/ppermute | solution.py:49
  55.4 16.2 %collective-permute-start.19 = (bf16[2,112,384]{2,1,0:T(8,128)(2,1)S(1)}, bf16[2,112,384]{2,1,0:T(8,128)(2,1)S(1)}, u32[]{:S(2)}, u32[]{:S(2)}) collective-permute-start(bf16[2,112,384]{2,1,0:T(8,128)(2,1)S(1)} %join.16.first_ref), channel_id=1, source_target_pairs={{0,16},{4,20},{8,24},{12,28},{16,0},{20,4},{24,8},{28,12},{1,17},{... | collective-permute-start | bytes 516104 | tf_op jit(solution)/shard_map/ppermute | solution.py:49
  58.0 20.5 %collective-permute-start.17 = (bf16[1,96,1536]{2,1,0:T(8,128)(2,1)S(1)}, bf16[1,96,1536]{2,1,0:T(8,128)(2,1)S(1)}, u32[]{:S(2)}, u32[]{:S(2)}) collective-permute-start(bf16[1,96,1536]{2,1,0:T(8,128)(2,1)S(1)} %maximum_bitcast_fusion.1.first_ref), channel_id=1, source_target_pairs={{0,16},{4,20},{8,24},{12,28},{16,0},{20,4},{24,8},{28,12},{1,17},{... | collective-permute-start | bytes 884744 | tf_op jit(solution)/shard_map/ppermute | solution.py:49
  70.0 29.9 %collective-permute-start.21 = (bf16[4,96,1152]{2,1,0:T(8,128)(2,1)S(1)}, bf16[4,96,1152]{2,1,0:T(8,128)(2,1)S(1)}, u32[]{:S(2)}, u32[]{:S(2)}) collective-permute-start(bf16[4,96,1152]{2,1,0:T(8,128)(2,1)S(1)} %join.15.refs_4_), channel_id=1, source_target_pairs={{0,4},{4,0},{8,12},{12,8},{16,20},{20,16},{24,28},{28,24},{1,5},{5... | collective-permute-start | bytes 2654216 | tf_op jit(solution)/shard_map/ppermute | solution.py:49
  78.5 16.3 %collective-permute-start.20 = (bf16[2,96,1536]{2,1,0:T(8,128)(2,1)S(1)}, bf16[2,96,1536]{2,1,0:T(8,128)(2,1)S(1)}, u32[]{:S(2)}, u32[]{:S(2)}) collective-permute-start(bf16[2,96,1536]{2,1,0:T(8,128)(2,1)S(1)} %join.18.first_ref), channel_id=1, source_target_pairs={{0,8},{4,12},{8,0},{12,4},{16,24},{20,28},{24,16},{28,20},{1,9},{5... | collective-permute-start | bytes 1769480 | tf_op jit(solution)/shard_map/ppermute | solution.py:49
  78.6 21.3 %collective-permute-start.22 = (bf16[4,112,384]{2,1,0:T(8,128)(2,1)S(1)}, bf16[4,112,384]{2,1,0:T(8,128)(2,1)S(1)}, u32[]{:S(2)}, u32[]{:S(2)}) collective-permute-start(bf16[4,112,384]{2,1,0:T(8,128)(2,1)S(1)} %join.17.refs_6_), channel_id=1, source_target_pairs={{0,8},{4,12},{8,0},{12,4},{16,24},{20,28},{24,16},{28,20},{1,9},{5... | collective-permute-start | bytes 1032200 | tf_op jit(solution)/shard_map/ppermute | solution.py:49
  94.9 23.3 %collective-permute-start.26 = (bf16[4,96,1536]{2,1,0:T(8,128)(2,1)S(1)}, bf16[4,96,1536]{2,1,0:T(8,128)(2,1)S(1)}, u32[]{:S(2)}, u32[]{:S(2)}) collective-permute-start(bf16[4,96,1536]{2,1,0:T(8,128)(2,1)S(1)} %join.19.refs_0_), channel_id=1, source_target_pairs={{0,4},{4,0},{8,12},{12,8},{16,20},{20,16},{24,28},{28,24},{1,5},{5... | collective-permute-start | bytes 3538952 | tf_op jit(solution)/shard_map/ppermute | solution.py:49
  116.4 18.5 %collective-permute-start.27 = (bf16[4,96,1536]{2,1,0:T(8,128)(2,1)S(1)}, bf16[4,96,1536]{2,1,0:T(8,128)(2,1)S(1)}, u32[]{:S(2)}, u32[]{:S(2)}) collective-permute-start(bf16[4,96,1536]{2,1,0:T(8,128)(2,1)S(1)} %join.19.refs_0_), channel_id=1, source_target_pairs={{0,1},{1,0},{2,3},{3,2},{4,5},{5,4},{6,7},{7,6},{8,9},{9,8},{10,11... | collective-permute-start | bytes 3538952 | tf_op jit(solution)/shard_map/ppermute | solution.py:49
  118.3 16.7 %collective-permute-start.28 = (bf16[4,96,1536]{2,1,0:T(8,128)(2,1)S(1)}, bf16[4,96,1536]{2,1,0:T(8,128)(2,1)S(1)}, u32[]{:S(2)}, u32[]{:S(2)}) collective-permute-start(bf16[4,96,1536]{2,1,0:T(8,128)(2,1)S(1)} %collective-permute-done.26.refs_1_), channel_id=1, source_target_pairs={{0,1},{1,0},{2,3},{3,2},{4,5},{5,4},{6,7},{7,6},{8,9},{9,8},{10,11... | collective-permute-start | bytes 3538952 | tf_op jit(solution)/shard_map/ppermute | solution.py:49
  122.1 8.6 %collective-permute-start.24 = (bf16[128,768]{1,0:T(8,128)(2,1)S(1)}, bf16[128,768]{1,0:T(8,128)(2,1)S(1)}, u32[]{:S(2)}, u32[]{:S(2)}) collective-permute-start(bf16[128,768]{1,0:T(8,128)(2,1)S(1)} %get-tuple-element.440), channel_id=1, source_target_pairs={{0,2},{1,3},{2,0},{3,1},{4,6},{5,7},{6,4},{7,5},{8,10},{9,11},{10,... | collective-permute-start | bytes 589832 | tf_op jit(solution)/shard_map/ppermute | solution.py:49
  126.8 8.1 %collective-permute-start.32 = (bf16[128,768]{1,0:T(8,128)(2,1)S(1)}, bf16[128,768]{1,0:T(8,128)(2,1)S(1)}, u32[]{:S(2)}, u32[]{:S(2)}) collective-permute-start(bf16[128,768]{1,0:T(8,128)(2,1)S(1)} %get-tuple-element.264.own_ref.refs_2_), channel_id=1, source_target_pairs={{0,2},{1,3},{2,0},{3,1},{4,6},{5,7},{6,4},{7,5},{8,10},{9,11},{10,... | collective-permute-start | bytes 589832 | tf_op jit(solution)/shard_map/ppermute | solution.py:49
  140.5 7.9 %collective-permute-start.29 = (bf16[128,768]{1,0:T(8,128)(2,1)S(1)}, bf16[128,768]{1,0:T(8,128)(2,1)S(1)}, u32[]{:S(2)}, u32[]{:S(2)}) collective-permute-start(bf16[128,768]{1,0:T(8,128)(2,1)S(1)} %get-tuple-element.259), channel_id=1, source_target_pairs={{0,2},{1,3},{2,0},{3,1},{4,6},{5,7},{6,4},{7,5},{8,10},{9,11},{10,... | collective-permute-start | bytes 589832 | tf_op jit(solution)/shard_map/ppermute | solution.py:49
  144.0 8.6 %collective-permute-start.35 = (bf16[128,768]{1,0:T(8,128)(2,1)S(1)}, bf16[128,768]{1,0:T(8,128)(2,1)S(1)}, u32[]{:S(2)}, u32[]{:S(2)}) collective-permute-start(bf16[128,768]{1,0:T(8,128)(2,1)S(1)} %get-tuple-element.270.own_ref.refs_6_), channel_id=1, source_target_pairs={{0,2},{1,3},{2,0},{3,1},{4,6},{5,7},{6,4},{7,5},{8,10},{9,11},{10,... | collective-permute-start | bytes 589832 | tf_op jit(solution)/shard_map/ppermute | solution.py:49
  159.5 8.1 %collective-permute-start.37 = (bf16[128,768]{1,0:T(8,128)(2,1)S(1)}, bf16[128,768]{1,0:T(8,128)(2,1)S(1)}, u32[]{:S(2)}, u32[]{:S(2)}) collective-permute-start(bf16[128,768]{1,0:T(8,128)(2,1)S(1)} %get-tuple-element.281), channel_id=1, source_target_pairs={{0,2},{1,3},{2,0},{3,1},{4,6},{5,7},{6,4},{7,5},{8,10},{9,11},{10,... | collective-permute-start | bytes 589832 | tf_op jit(solution)/shard_map/ppermute | solution.py:49
  165.5 29.1 %collective-permute-start.46 = (bf16[4,96,1536]{2,1,0:T(8,128)(2,1)}, bf16[4,96,1536]{2,1,0:T(8,128)(2,1)S(1)}, u32[]{:S(2)}, u32[]{:S(2)}) collective-permute-start(bf16[4,96,1536]{2,1,0:T(8,128)(2,1)} %get-tuple-element.279), channel_id=1, source_target_pairs={{0,4},{4,0},{8,12},{12,8},{16,20},{20,16},{24,28},{28,24},{1,5},{5... | collective-permute-start | bytes 3538952 | tf_op jit(solution)/shard_map/ppermute | solution.py:49
  169.3 8.6 %collective-permute-start.39 = (bf16[128,768]{1,0:T(8,128)(2,1)}, bf16[128,768]{1,0:T(8,128)(2,1)}, u32[]{:S(2)}, u32[]{:S(2)}) collective-permute-start(bf16[128,768]{1,0:T(8,128)(2,1)} %get-tuple-element.284.refs_0_), channel_id=1, source_target_pairs={{0,2},{1,3},{2,0},{3,1},{4,6},{5,7},{6,4},{7,5},{8,10},{9,11},{10,... | collective-permute-start | bytes 589832 | tf_op jit(solution)/shard_map/ppermute | solution.py:49
  180.2 10.9 %collective-permute-start.43 = (bf16[128,768]{1,0:T(8,128)(2,1)}, bf16[128,768]{1,0:T(8,128)(2,1)S(1)}, u32[]{:S(2)}, u32[]{:S(2)}) collective-permute-start(bf16[128,768]{1,0:T(8,128)(2,1)} %get-tuple-element.289.refs_4_.refs_0_), channel_id=1, source_target_pairs={{0,1},{1,0},{2,3},{3,2},{4,5},{5,4},{6,7},{7,6},{8,9},{9,8},{10,11... | collective-permute-start | bytes 589832 | tf_op jit(solution)/shard_map/ppermute | solution.py:49
  183.2 8.0 %collective-permute-start.44 = (bf16[128,768]{1,0:T(8,128)(2,1)}, bf16[128,768]{1,0:T(8,128)(2,1)S(1)}, u32[]{:S(2)}, u32[]{:S(2)}) collective-permute-start(bf16[128,768]{1,0:T(8,128)(2,1)} %collective-permute-done.42.refs_5_.refs_1_), channel_id=1, source_target_pairs={{0,1},{1,0},{2,3},{3,2},{4,5},{5,4},{6,7},{7,6},{8,9},{9,8},{10,11... | collective-permute-start | bytes 589832 | tf_op jit(solution)/shard_map/ppermute | solution.py:49
  193.9 14.9 %collective-permute-start.45 = (bf16[4,112,384]{2,1,0:T(8,128)(2,1)S(1)}, bf16[4,112,384]{2,1,0:T(8,128)(2,1)S(1)}, u32[]{:S(2)}, u32[]{:S(2)}) collective-permute-start(bf16[4,112,384]{2,1,0:T(8,128)(2,1)S(1)} %get-tuple-element.306), channel_id=1, source_target_pairs={{0,4},{4,0},{8,12},{12,8},{16,20},{20,16},{24,28},{28,24},{1,5},{5... | collective-permute-start | bytes 1032200 | tf_op jit(solution)/shard_map/ppermute | solution.py:49
  194.8 24.2 %collective-permute-start.48 = (bf16[2,96,1536]{2,1,0:T(8,128)(2,1)S(1)}, bf16[2,96,1536]{2,1,0:T(8,128)(2,1)S(1)}, u32[]{:S(2)}, u32[]{:S(2)}) collective-permute-start(bf16[2,96,1536]{2,1,0:T(8,128)(2,1)S(1)} %get-tuple-element.310), channel_id=1, source_target_pairs={{0,8},{4,12},{8,0},{12,4},{16,24},{20,28},{24,16},{28,20},{1,9},{5... | collective-permute-start | bytes 1769480 | tf_op jit(solution)/shard_map/ppermute | solution.py:49
  207.3 14.1 %collective-permute-start.49 = (bf16[4,96,512]{2,1,0:T(8,128)(2,1)S(1)}, bf16[4,96,512]{2,1,0:T(8,128)(2,1)S(1)}, u32[]{:S(2)}, u32[]{:S(2)}) collective-permute-start(bf16[4,96,512]{2,1,0:T(8,128)(2,1)S(1)} %get-tuple-element.322), channel_id=1, source_target_pairs={{0,4},{4,0},{8,12},{12,8},{16,20},{20,16},{24,28},{28,24},{1,5},{5... | collective-permute-start | bytes 1179656 | tf_op jit(solution)/shard_map/ppermute | solution.py:49
  208.8 20.9 %collective-permute-start.50 = (bf16[2,112,384]{2,1,0:T(8,128)(2,1)S(1)}, bf16[2,112,384]{2,1,0:T(8,128)(2,1)S(1)}, u32[]{:S(2)}, u32[]{:S(2)}) collective-permute-start(bf16[2,112,384]{2,1,0:T(8,128)(2,1)S(1)} %get-tuple-element.326), channel_id=1, source_target_pairs={{0,8},{4,12},{8,0},{12,4},{16,24},{20,28},{24,16},{28,20},{1,9},{5... | collective-permute-start | bytes 516104 | tf_op jit(solution)/shard_map/ppermute | solution.py:49
  210.3 24.4 %collective-permute-start.55 = (bf16[4,96,640]{2,1,0:T(8,128)(2,1)S(1)}, bf16[4,96,640]{2,1,0:T(8,128)(2,1)S(1)}, u32[]{:S(2)}, u32[]{:S(2)}) collective-permute-start(bf16[4,96,640]{2,1,0:T(8,128)(2,1)S(1)} %get-tuple-element.323), channel_id=1, source_target_pairs={{0,8},{4,12},{8,0},{12,4},{16,24},{20,28},{24,16},{28,20},{1,9},{5... | collective-permute-start | bytes 1474568 | tf_op jit(solution)/shard_map/ppermute | solution.py:49
  218.9 17.4 %collective-permute-start.47 = (bf16[256,768]{1,0:T(8,128)(2,1)S(1)}, bf16[256,768]{1,0:T(8,128)(2,1)S(1)}, u32[]{:S(2)}, u32[]{:S(2)}) collective-permute-start(bf16[256,768]{1,0:T(8,128)(2,1)S(1)} %get-tuple-element.335), channel_id=1, source_target_pairs={{0,1},{1,0},{2,3},{3,2},{4,5},{5,4},{6,7},{7,6},{8,9},{9,8},{10,11... | collective-permute-start | bytes 1179656 | tf_op jit(solution)/shard_map/ppermute | solution.py:49
  219.1 36.1 %collective-permute-start.70 = (bf16[1,96,1536]{2,1,0:T(8,128)(2,1)S(1)}, bf16[1,96,1536]{2,1,0:T(8,128)(2,1)S(1)}, u32[]{:S(2)}, u32[]{:S(2)}) collective-permute-start(bf16[1,96,1536]{2,1,0:T(8,128)(2,1)S(1)} %get-tuple-element.340), channel_id=1, source_target_pairs={{0,16},{4,20},{8,24},{12,28},{16,0},{20,4},{24,8},{28,12},{1,17},{... | collective-permute-start | bytes 884744 | tf_op jit(solution)/shard_map/ppermute | solution.py:49
  221.5 15.8 %collective-permute-start.58 = (bf16[2,96,512]{2,1,0:T(8,128)(2,1)S(1)}, bf16[2,96,512]{2,1,0:T(8,128)(2,1)S(1)}, u32[]{:S(2)}, u32[]{:S(2)}) collective-permute-start(bf16[2,96,512]{2,1,0:T(8,128)(2,1)S(1)} %get-tuple-element.351), channel_id=1, source_target_pairs={{0,8},{4,12},{8,0},{12,4},{16,24},{20,28},{24,16},{28,20},{1,9},{5... | collective-permute-start | bytes 589832 | tf_op jit(solution)/shard_map/ppermute | solution.py:49
  233.8 12.1 %collective-permute-start.57 = (bf16[4,96,512]{2,1,0:T(8,128)(2,1)S(1)}, bf16[4,96,512]{2,1,0:T(8,128)(2,1)S(1)}, u32[]{:S(2)}, u32[]{:S(2)}) collective-permute-start(bf16[4,96,512]{2,1,0:T(8,128)(2,1)S(1)} %get-tuple-element.368), channel_id=1, source_target_pairs={{0,4},{4,0},{8,12},{12,8},{16,20},{20,16},{24,28},{28,24},{1,5},{5... | collective-permute-start | bytes 1179656 | tf_op jit(solution)/shard_map/ppermute | solution.py:49
  234.7 16.9 %collective-permute-start.54 = (bf16[4,96,640]{2,1,0:T(8,128)(2,1)S(1)}, bf16[4,96,640]{2,1,0:T(8,128)(2,1)S(1)}, u32[]{:S(2)}, u32[]{:S(2)}) collective-permute-start(bf16[4,96,640]{2,1,0:T(8,128)(2,1)S(1)} %get-tuple-element.369), channel_id=1, source_target_pairs={{0,8},{4,12},{8,0},{12,4},{16,24},{20,28},{24,16},{28,20},{1,9},{5... | collective-permute-start | bytes 1474568 | tf_op jit(solution)/shard_map/ppermute | solution.py:49
  237.2 12.9 %collective-permute-start.56 = (bf16[2,96,640]{2,1,0:T(8,128)(2,1)S(1)}, bf16[2,96,640]{2,1,0:T(8,128)(2,1)S(1)}, u32[]{:S(2)}, u32[]{:S(2)}) collective-permute-start(bf16[2,96,640]{2,1,0:T(8,128)(2,1)S(1)} %get-tuple-element.374), channel_id=1, source_target_pairs={{0,4},{4,0},{8,12},{12,8},{16,20},{20,16},{24,28},{28,24},{1,5},{5... | collective-permute-start | bytes 737288 | tf_op jit(solution)/shard_map/ppermute | solution.py:49
  245.9 8.5 %collective-permute-start.66 = (bf16[1,112,384]{2,1,0:T(8,128)(2,1)S(1)}, bf16[1,112,384]{2,1,0:T(8,128)(2,1)S(1)}, u32[]{:S(2)}, u32[]{:S(2)}) collective-permute-start(bf16[1,112,384]{2,1,0:T(8,128)(2,1)S(1)} %get-tuple-element.355), channel_id=1, source_target_pairs={{0,16},{4,20},{8,24},{12,28},{16,0},{20,4},{24,8},{28,12},{1,17},{... | collective-permute-start | bytes 258056 | tf_op jit(solution)/shard_map/ppermute | solution.py:49
  247.5 9.7 %collective-permute-start.64 = (bf16[1,96,512]{2,1,0:T(8,128)(2,1)S(1)}, bf16[1,96,512]{2,1,0:T(8,128)(2,1)}, u32[]{:S(2)}, u32[]{:S(2)}) collective-permute-start(bf16[1,96,512]{2,1,0:T(8,128)(2,1)S(1)} %get-tuple-element.379), channel_id=1, source_target_pairs={{0,16},{4,20},{8,24},{12,28},{16,0},{20,4},{24,8},{28,12},{1,17},{... | collective-permute-start | bytes 294920 | tf_op jit(solution)/shard_map/ppermute | solution.py:49
  250.1 16.9 %collective-permute-start.60 = (bf16[2,96,512]{2,1,0:T(8,128)(2,1)S(1)}, bf16[2,96,512]{2,1,0:T(8,128)(2,1)S(1)}, u32[]{:S(2)}, u32[]{:S(2)}) collective-permute-start(bf16[2,96,512]{2,1,0:T(8,128)(2,1)S(1)} %get-tuple-element.382), channel_id=1, source_target_pairs={{0,8},{4,12},{8,0},{12,4},{16,24},{20,28},{24,16},{28,20},{1,9},{5... | collective-permute-start | bytes 589832 | tf_op jit(solution)/shard_map/ppermute | solution.py:49
  251.6 12.4 %collective-permute-start.63 = (bf16[1,96,640]{2,1,0:T(8,128)(2,1)S(1)}, bf16[1,96,640]{2,1,0:T(8,128)(2,1)}, u32[]{:S(2)}, u32[]{:S(2)}) collective-permute-start(bf16[1,96,640]{2,1,0:T(8,128)(2,1)S(1)} %get-tuple-element.385), channel_id=1, source_target_pairs={{0,16},{4,20},{8,24},{12,28},{16,0},{20,4},{24,8},{28,12},{1,17},{... | collective-permute-start | bytes 368648 | tf_op jit(solution)/shard_map/ppermute | solution.py:49
  254.4 12.7 %collective-permute-start.53 = (bf16[128,768]{1,0:T(8,128)(2,1)}, bf16[128,768]{1,0:T(8,128)(2,1)}, u32[]{:S(2)}, u32[]{:S(2)}) collective-permute-start(bf16[128,768]{1,0:T(8,128)(2,1)} %slice.294), channel_id=1, source_target_pairs={{0,2},{1,3},{2,0},{3,1},{4,6},{5,7},{6,4},{7,5},{8,10},{9,11},{10,... | collective-permute-start | bytes 589832 | tf_op jit(solution)/shard_map/ppermute | solution.py:49
  257.2 15.6 %collective-permute-start.59 = (bf16[2,96,640]{2,1,0:T(8,128)(2,1)S(1)}, bf16[2,96,640]{2,1,0:T(8,128)(2,1)S(1)}, u32[]{:S(2)}, u32[]{:S(2)}) collective-permute-start(bf16[2,96,640]{2,1,0:T(8,128)(2,1)S(1)} %get-tuple-element.389), channel_id=1, source_target_pairs={{0,4},{4,0},{8,12},{12,8},{16,20},{20,16},{24,28},{28,24},{1,5},{5... | collective-permute-start | bytes 737288 | tf_op jit(solution)/shard_map/ppermute | solution.py:49
  (75 other events, 627.2 us)
